TPU v7x, 256 devices: a whole 4x4x8 slice. The times are simulated.
256 devices in a mesh: dim: 8 (over y, core), rows: 32 (over x, z).
Axes of the slice: x: 4, y: 4, z: 8, core: 2. Of those that a mesh axis runs over, the one named last changes fastest.
Arguments:
- user_rows: bfloat16 [2048, 2048], P('rows', 'dim'), may hold values from -0.125 to 0.125
- item_table: bfloat16 [32768, 2048], P('rows', 'dim')
- observed_items: int32 [2048, 32], P('rows'), may hold values from 0 to 32767, as said below
- counts: int32 [2048], P('rows'), may hold values from 1 to 32
- item_row: int32 [32768], replicated, may hold values from 0 to 32767, as said below
Outputs:
- new_users: float32 [2048, 2048], P('rows', 'dim')
Inputs may be any that keep to these rules, and one draw needn't show every extreme that they name: item_row is a permutation; rows k * 1024 to (k + 1) * 1024 - 1 of item_table form item block k. In the rows of observed_items of each 64 consecutive users (padding slots included), exactly 64 slots name items whose table row lies in item block k, for every k.
All inputs are finite; a program needn't handle non-finite values.
Results may differ from a plain program's by a relative error of at most 0.0003.
Values may be sent and summed in bfloat16 or wider, within the bound.
No kernel may reach another device: no remote copies, remote signals or barrier semaphores. Data moves between devices by JAX's collectives and lax.ppermute only.
A program may use at most 64 MiB of HBM per device.

v0:
```python
import jax
import jax.numpy as jnp
from jax import lax
from jax.sharding import PartitionSpec as P


def on_device(user_rows, item_table, observed_items, counts, item_row):
    highest = lax.Precision.HIGHEST
    width = user_rows.shape[1]
    users_dev = user_rows.shape[0]
    list_len = observed_items.shape[1]
    weight_unobs = 32.0 / item_row.shape[0]
    gram_part = lax.dot_general(
        item_table,
        lax.all_gather(item_table, "dim", axis=1, tiled=True),
        (((0,), (0,)), ((), ())),
        preferred_element_type=jnp.float32,
    )
    gram_rows = lax.psum(gram_part, "rows")
    gram_times = lax.dot_general(
        lax.all_gather(user_rows, "dim", axis=1, tiled=True).astype(jnp.float32),
        gram_rows,
        (((1,), (1,)), ((), ())),
        precision=highest,
    )
    table_rows = item_row[observed_items]
    shard_rows = lax.all_gather(item_table, "rows", axis=0, tiled=True)
    inside = (table_rows >= 0) & (table_rows < shard_rows.shape[0])
    picked = shard_rows[jnp.clip(table_rows, 0, shard_rows.shape[0] - 1)]
    fetched = jnp.where(
        inside[..., None], picked, jnp.zeros((users_dev, list_len, width), jnp.bfloat16)
    )
    partial_value = jnp.einsum("ub,ujb->uj", user_rows, fetched, preferred_element_type=jnp.float32)
    predicted = lax.psum(partial_value, "dim")
    live = (lax.broadcasted_iota(jnp.int32, (users_dev, list_len), 1) < counts[:, None]).astype(
        jnp.float32
    )
    residual = live * (predicted - 1.0)
    first_column = lax.axis_index("dim") * width
    diag_block = lax.dynamic_slice_in_dim(gram_rows, first_column, width, 1)
    diag_shift = weight_unobs * diag_block + jnp.eye(width, dtype=jnp.float32)
    own_float = user_rows.astype(jnp.float32)
    shift_factor = jnp.linalg.cholesky(diag_shift)
    shift_inverse = jax.scipy.linalg.cho_solve(
        (shift_factor, True), jnp.eye(width, dtype=jnp.float32)
    )
    masked = fetched.astype(jnp.float32) * live[..., None]
    gradient = (
        jnp.einsum("uj,ujb->ub", residual, masked, precision=highest)
        + weight_unobs * gram_times
        + own_float
    )
    scaled_grad = jnp.dot(gradient, shift_inverse, precision=highest)
    scaled_rows = jnp.einsum("ujb,bc->ujc", masked, shift_inverse, precision=highest)
    inner = jnp.einsum("ujb,ukb->ujk", scaled_rows, masked, precision=highest) + jnp.eye(
        list_len, dtype=jnp.float32
    )
    projected = jnp.einsum("ujb,ub->uj", masked, scaled_grad, precision=highest)
    inner_factor = jnp.linalg.cholesky(inner)
    middle = jax.scipy.linalg.solve_triangular(inner_factor, projected[..., None], lower=True)
    weights = jax.scipy.linalg.solve_triangular(inner_factor, middle, lower=True, trans="T")[..., 0]
    update = scaled_grad - jnp.einsum("uj,ujb->ub", weights, scaled_rows, precision=highest)
    return own_float - update


def solution(mesh):
    in_specs = (P("rows", "dim"), P("rows", "dim"), P("rows", None), P("rows"), P())
    out_specs = P("rows", "dim")
    return jax.shard_map(
        on_device, mesh=mesh, in_specs=in_specs, out_specs=out_specs, check_vma=False
    )
```

profile of v0, /device:TPU:2, one launch (start us, length us, event | category | flops | bytes accessed | tf_op | source)
XLA Modules:
  0.0 625.2 jit_solution(383704435187583185)
XLA Ops:
  6.5 0.7 all-gather.5.cloned.1.call-update
  7.3 42.9 %all-gather.5.cloned.1.call-done = bf16[1024,2048]{1,0:T(8,128)(2,1)} async-done(((bf16[1024,256]{1,0:T(8,128)(2,1)}), bf16[1024,2048]{1,0:T(8,128)(2,1)}) %all-gather.5.cloned.1.call-update) | async-done | bytes 4194320 | tf_op jit(solution)/shard_map/all_gather | solution.py:15
  50.2 5.4 fusion.47
  55.7 0.7 all-gather.3.cloned.1.call-update
  56.6 11.8 %gather_fusion = s32[2048]{0:T(1024)S(1)} fusion(s32[32768]{0:T(1024)S(1)} %copy-done, s32[2048]{0:T(1024)S(1)} %broadcast_clamp_fusion.1), kind=kCustom, calls=%fused_computation | custom fusion | bytes 24576 | tf_op jit(solution)/shard_map/gather | solution.py:26
  68.7 0.6 fusion.37
  69.4 14.1 %all_gather.11 = bf16[64,2048]{1,0:T(8,128)(2,1)} all-gather(bf16[64,256]{1,0:T(8,128)(2,1)S(1)} %copy-done.6), channel_id=1, replica_groups=mesh['dim'=8,'rows'=32] {'dim'}, dimensions={1}, use_global_device_ids=true | all-gather | bytes 294912 | tf_op jit(solution)/shard_map/all_gather | solution.py:21
  83.6 126.0 %all-reduce.3.cloned.1.call-done = f32[256,2048]{0,1:T(8,128)} async-done(((f32[256,2048]{0,1:T(8,128)}), f32[256,2048]{0,1:T(8,128)}) %all-reduce.3.cloned.1.call-update) | async-done | bytes 2097168 | tf_op jit(solution)/shard_map/psum | solution.py:19
  209.6 1.0 multiply_add_fusion
  210.7 1.0 fusion.21
  211.7 11.7 %cholesky.65 = f32[128,128]{1,0:T(8,128)S(1)} custom-call(f32[128,128]{1,0:T(8,128)S(1)} %cholesky.159), custom_call_target="Cholesky" | custom-call | tf_op jit(solution)/shard_map/jit(cholesky)/cholesky | solution.py:43
  223.5 9.8 %custom-call.29 = f32[1,128,128]{1,2,0:T(8,128)S(1)} custom-call(f32[1,128,128]{2,1,0:T(8,128)S(1)} %get-tuple-element.26), custom_call_target="InvertDiagBlocksLowerTriangular" | custom-call | tf_op jit(solution)/shard_map/jit(cholesky)/cholesky | solution.py:43
  233.6 0.3 convolution_subtract_fusion.2
  233.8 11.7 %cholesky.135 = f32[128,128]{1,0:T(8,128)S(1)} custom-call(f32[128,128]{1,0:T(8,128)S(1)} %convolution_subtract_fusion.2), custom_call_target="Cholesky" | custom-call | tf_op jit(solution)/shard_map/jit(cholesky)/cholesky | solution.py:43
  245.6 0.7 compare_reduce_fusion.1
  247.7 4.3 while.1
  247.9 0.6 fusion.70
  248.5 1.4 bitcast_dynamic-update-slice_fusion.2
  250.0 0.6 fusion.70
  250.6 1.4 bitcast_dynamic-update-slice_fusion.2
  252.0 19.7 %custom-call.30 = f32[2,128,128]{1,2,0:T(8,128)S(1)} custom-call(f32[2,128,128]{2,1,0:T(8,128)S(1)} %get-tuple-element.12), custom_call_target="InvertDiagBlocksLowerTriangular" | custom-call | tf_op jit(solution)/shard_map/jit(_cho_solve)/triangular_solve | solution.py:44
  271.7 0.3 fusion.23
  272.0 0.4 convolution_subtract_fusion.1
  272.4 0.3 fusion.33
  272.7 0.3 fusion.32
  272.9 0.3 convolution_subtract_fusion
  273.3 0.3 fusion.31
  273.5 76.7 %all-gather.3.cloned.1.call-done = bf16[32768,256]{1,0:T(8,128)(2,1)} async-done(((bf16[1024,256]{1,0:T(8,128)(2,1)}), bf16[32768,256]{1,0:T(8,128)(2,1)}) %all-gather.3.cloned.1.call-update) | async-done | bytes 16777232 | tf_op jit(solution)/shard_map/all_gather | solution.py:27
  350.2 14.6 %gather_fusion.1 = bf16[2048,256]{1,0:T(8,128)(2,1)S(1)} fusion(bf16[32768,256]{1,0:T(8,128)(2,1)} %all-gather.3.cloned.1.call-done, s32[2048]{0:T(1024)S(1)} %broadcast_clamp_fusion), kind=kCustom, calls=%fused_computation.1 | custom fusion | bytes 2105344 | tf_op jit(solution)/shard_map/gather | solution.py:29
  364.8 0.4 fusion.14
  365.2 25.0 %psum.14 = f32[64,32]{1,0:T(8,128)S(1)} all-reduce(f32[64,32]{1,0:T(8,128)S(1)} %bitcast.110), channel_id=1, replica_groups=mesh['dim'=8,'rows'=32] {'dim'}, use_global_device_ids=true, to_apply=%region_0.0 | all-reduce | flops 2048 | bytes 16384 | tf_op jit(solution)/shard_map/psum | solution.py:34
  390.3 1.7 fusion.3
  392.0 2.8 fusion.2
  394.9 0.9 fusion.6
  395.8 0.3 fusion.22
  396.1 0.6 copy-done.9
  396.7 2.4 fusion.7
  399.1 3.3 fusion.1
  402.4 2.6 copy.21
  405.1 2.4 fusion.9
  407.5 188.9 %custom-call.31 = f32[64,32,32]{2,1,0:T(8,128)} custom-call(f32[64,32,32]{2,1,0:T(8,128)} %fusion.9), custom_call_target="Cholesky" | custom-call | tf_op jit(solution)/shard_map/jit(cholesky)/cholesky | solution.py:59
  596.4 1.8 copy.22
  598.6 13.5 %custom-call.32 = f32[64,1,32,32]{0,2,3,1:T(8,128)} custom-call(f32[64,1,32,32]{0,3,2,1:T(8,128)S(1)} %select_bitcast_fusion), custom_call_target="InvertDiagBlocksLowerTriangular" | custom-call | tf_op jit(solution)/shard_map/jit(_solve_triangular)/vmap()/triangular_solve | solution.py:61
  612.1 2.0 copy.35
  614.1 1.0 convolution_bitcast_fusion.1
  615.1 1.7 convolution_bitcast_fusion
  616.8 1.1 fusion.48
  618.0 0.6 convert_subtract_fusion
  (65 shorter events, 1.8 us)
Async XLA Ops:
  6.5 50.1 %copy-start = (s32[32768]{0:T(1024)S(1)}, s32[32768]{0:T(1024)}, u32[]{:S(2)}) copy-start(s32[32768]{0:T(1024)} %param.9) | copy-start | bytes 393220
  6.5 43.7 %all-gather.5.cloned.1.call-start = ((), (), s32[]{:S(2)}) async-start(), calls=%async_computation.1 | async-start | bytes 4718592 | tf_op jit(solution)/shard_map/all_gather | solution.py:15
  7.3 202.3 %all-reduce.3.cloned.1.call-start = ((), (), s32[]{:S(2)}) async-start(), calls=%async_computation.2 | async-start | bytes 4194304 | tf_op jit(solution)/shard_map/psum | solution.py:19
  55.6 0.8 copy-start.13
  55.7 294.5 %all-gather.3.cloned.1.call-start = ((), (), s32[]{:S(2)}) async-start(), calls=%async_computation | async-start | bytes 17301504 | tf_op jit(solution)/shard_map/all_gather | solution.py:27
  56.6 12.8 %copy-start.6 = (bf16[64,256]{1,0:T(8,128)(2,1)S(1)}, bf16[64,256]{1,0:T(8,128)(2,1)}, u32[]{:S(2)}) copy-start(bf16[64,256]{1,0:T(8,128)(2,1)} %param.5) | copy-start | bytes 98308
  56.6 26.9 %copy-start.14 = (s32[64]{0:T(128)S(1)}, s32[64]{0:T(128)}, u32[]{:S(2)}) copy-start(s32[64]{0:T(128)} %param.8) | copy-start | bytes 772
  83.6 306.7 %copy-start.4 = (f32[64,32]{1,0:T(8,128)}, f32[64,32]{1,0:T(8,128)S(1)}, u32[]{:S(2)}) copy-start(f32[64,32]{1,0:T(8,128)S(1)} %fusion.36) | copy-start | bytes 24580
  392.0 2.9 copy-start.2
  392.0 2.9 copy-start.3
  392.0 2.9 copy-start.7
  394.9 1.8 copy-start.5
  396.0 0.6 copy-start.9
  402.4 2.6 copy-start.1
  402.4 2.6 copy-start.11
  402.4 2.6 copy-start.12
  614.0 3.9 copy-start.8
  614.1 3.9 copy-start.10
Sparse Core Ops, SparseCore 0:
  9.2 41.0 all-gather.4
  55.8 153.7 all-reduce.2
  212.2 137.9 all-gather.2
where the time goes:
time: 626 us; the launch traced here: 625 us
  other arithmetic  262 us (42%)
  waiting for transfers between devices  247 us (39%)
  blocking collectives  39.1 us (6%)
  local copies, waits for them, and re-layouts  38.1 us (6%)
  matrix products  23.4 us (4%)
  between operations  14.8 us (2%)
    another operation x4, other arithmetic, on_device(): inner_factor = jnp.linalg.cholesky(inner)  189 us
    psum x1, waiting for transfers between devices, on_device(): gram_rows = lax.psum(gram_part, 'rows')  126 us
    all_gather x1, waiting for transfers between devices, on_device(): shard_rows = lax.all_gather(item_table, 'rows', axis=0, tiled=True)  76.7 us
    all_gather x1, waiting for transfers between devices, on_device(): lax.all_gather(item_table, 'dim', axis=1, tiled=True)  42.9 us
    another operation x6, other arithmetic, on_device(): shift_factor = jnp.linalg.cholesky(diag_shift)  34 us
    psum x1, blocking collectives, on_device(): predicted = lax.psum(partial_value, 'dim')  25 us
    another operation x3, other arithmetic, on_device(): jax.scipy.linalg.cho_solve((shift_factor, True), jnp.eye(width, dtype=jnp...  19.7 us
    gather x1, local copies, waits for them, and re-layouts, on_device(): picked = shard_rows[jnp.clip(table_rows, 0, shard_rows.shape[0] - 1)]  14.6 us
  transfers between devices with their start and end apart: 3, of which 3 were waited for; matrix products, arithmetic and copies ran while one was open for 12% of the time, Pallas kernels for 0%

commit v1 on v0

v1 whole, which is shorter than its diff:
```python
import jax
import jax.numpy as jnp
from jax import lax
from jax.experimental import pallas as pl
from jax.experimental.pallas import tpu as pltpu
from jax.sharding import Mesh, PartitionSpec as P

F32 = jnp.float32
BF16 = jnp.bfloat16
I32 = jnp.int32
ROWS = ("x", "z")
DIM = ("y", "core")
BLOCK = 256
LIST = 32
USERS_DEV = 64
SLOTS = USERS_DEV * LIST
ITEM_DEV = 1024
N_ROWS = 32
N_DIM = 8
PER = SLOTS // N_ROWS
CHUNK = 256
CHUNKS = SLOTS // CHUNK
WEIGHT = 32.0 / 32768.0
VMEM = pl.BlockSpec(memory_space=pltpu.VMEM)
SMEM = pl.BlockSpec(memory_space=pltpu.SMEM)


def iota(shape, dim):
    return lax.broadcasted_iota(I32, shape, dim)


def dot(a, b, ca=1, cb=0):
    return lax.dot_general(a, b, (((ca,), (cb,)), ((), ())), preferred_element_type=F32)


def split(a):
    top = a.astype(BF16)
    rest = a - top.astype(F32)
    mid = rest.astype(BF16)
    low = (rest - mid.astype(F32)).astype(BF16)
    return top, mid, low


def dot_split(a, b):
    a0, a1, a2 = a
    b0, b1, b2 = b
    small = dot(a2, b0) + dot(a0, b2) + dot(a1, b1)
    return (small + (dot(a1, b0) + dot(a0, b1))) + dot(a0, b0)


def one_hot(column, width):
    hit = iota((column.shape[0], width), 1) == column
    return jnp.where(hit, 1.0, 0.0).astype(BF16)


def call(kernel, out_shape, n_in, flops, nbytes, scratch=(), in_specs=None):
    multi = isinstance(out_shape, (tuple, list))
    return pl.pallas_call(
        kernel,
        out_shape=out_shape,
        in_specs=in_specs or [VMEM] * n_in,
        out_specs=[VMEM] * len(out_shape) if multi else VMEM,
        scratch_shapes=list(scratch),
        compiler_params=pltpu.CompilerParams(vmem_limit_bytes=48 << 20),
        cost_estimate=pl.CostEstimate(flops=flops, bytes_accessed=nbytes, transcendentals=0),
    )


def index_kernel(ids_ref, table_ref, pos_ref, req_ref):
    table = table_ref[...]
    table_hi = (table >> 8).astype(F32).astype(BF16)
    table_lo = (table & 255).astype(F32).astype(BF16)
    lane = iota((CHUNK, 128), 1)
    before = jnp.where(
        iota((CHUNK, CHUNK), 0) > iota((CHUNK, CHUNK), 1), 1.0, 0.0
    ).astype(BF16)
    totals = jnp.zeros((1, 128), F32)
    asked = jnp.zeros((128, SLOTS), F32)
    for c in range(CHUNKS):
        ids = ids_ref[c * CHUNK : (c + 1) * CHUNK, :]
        picked = one_hot(ids >> 7, 256)
        values = dot(picked, table_hi) * 256.0 + dot(picked, table_lo)
        row = jnp.sum(jnp.where(lane == (ids & 127), values, 0.0), axis=1, keepdims=True)
        row = row.astype(I32)
        member = jnp.where(lane == (row >> 10), 1.0, 0.0)
        rank = dot(before, member.astype(BF16)) + totals
        place = rank + (lane * PER).astype(F32)
        pos = jnp.sum(member * place, axis=1, keepdims=True).astype(I32)
        totals = totals + jnp.sum(member, axis=0, keepdims=True)
        pos_ref[c * CHUNK : (c + 1) * CHUNK, :] = pos
        within = row & 1023
        parts = jnp.where(lane == 0, within >> 5, jnp.where(lane == 1, within & 31, 0))
        asked = asked + dot(parts.astype(F32).astype(BF16), one_hot(pos, SLOTS), 0, 0)
    req_ref[...] = (asked[0:1, :] * 32.0 + asked[1:2, :]).astype(I32)


def pick_kernel(req_ref, table_ref, rows_ref):
    table = table_ref[...]
    for c in range(CHUNKS):
        part = slice(c * CHUNK, (c + 1) * CHUNK)
        rows_ref[part, :] = dot(one_hot(req_ref[part, :], ITEM_DEV), table).astype(BF16)


def place_kernel(pos_ref, came_ref, users_ref, fetched_ref, pred_ref):
    came = came_ref[...]
    users = users_ref[...]
    lane = iota((LIST, USERS_DEV), 1)
    pred = jnp.zeros((LIST, USERS_DEV), F32)
    for c in range(CHUNKS):
        part = slice(c * CHUNK, (c + 1) * CHUNK)
        rows = dot(one_hot(pos_ref[part, :], SLOTS), came).astype(BF16)
        fetched_ref[part, :] = rows
        cross = dot(rows, users, 1, 1)
        for i in range(CHUNK // LIST):
            user = c * (CHUNK // LIST) + i
            pred = pred + jnp.where(lane == user, cross[i * LIST : (i + 1) * LIST, :], 0.0)
    pred_ref[...] = pred


def product_kernel(block_ref, users_ref, *refs):
    tables, out_ref = refs[:N_DIM], refs[N_DIM]
    scores = jnp.zeros((BLOCK, ITEM_DEV), F32)
    for i in range(N_DIM):
        scores = scores + dot(users_ref[block_ref[i]], tables[i][...], 1, 1)
    s0, s1, s2 = split(scores)
    for i in range(N_DIM):
        table = tables[i][...]
        times = (dot(s2, table) + dot(s1, table)) + dot(s0, table)
        first = pl.multiple_of(block_ref[i] * BLOCK, BLOCK)
        out_ref[:, pl.ds(first, BLOCK)] = times


def inverse_kernel(diag_ref, out_ref, work):
    eye = jnp.where(iota((BLOCK, BLOCK), 0) == iota((BLOCK, BLOCK), 1), 1.0, 0.0)
    work[...] = WEIGHT * diag_ref[...] + eye
    row_lane = iota((1, BLOCK), 1)
    half_lane = iota((128, 128), 1)
    for half in range(2):

        def step(k, carry):
            here = half * 128 + k
            row = work[pl.ds(here, 1), :]
            pivot = jnp.sum(jnp.where(row_lane == here, row, 0.0), axis=1, keepdims=True)
            inv = 1.0 / pivot
            scaled = row * inv
            for i in range(2):
                column = jnp.transpose(
                    jnp.broadcast_to(row[:, i * 128 : (i + 1) * 128], (128, 128))
                )
                for j in range(2):
                    at = (slice(i * 128, (i + 1) * 128), slice(j * 128, (j + 1) * 128))
                    new = work[at] - column * scaled[:, j * 128 : (j + 1) * 128]
                    if j == half:
                        new = jnp.where(half_lane == k, column * inv, new)
                    work[at] = new
            work[pl.ds(here, 1), :] = jnp.where(row_lane == here, -inv, scaled)
            return carry

        lax.fori_loop(0, 128, step, 0)
    out_ref[...] = -work[...]


def inner_kernel(fetched_ref, inverse_ref, counts_ref, out_ref, folded, work):
    i0, i1, i2 = split(inverse_ref[...])
    same = iota((CHUNK, CHUNK), 0) // LIST == iota((CHUNK, CHUNK), 1) // LIST
    for c in range(CHUNKS):
        part = slice(c * CHUNK, (c + 1) * CHUNK)
        rows = fetched_ref[part, :]
        scaled = (dot(rows, i2) + dot(rows, i1)) + dot(rows, i0)
        s0, s1, s2 = split(scaled)
        cross = (dot(s2, rows, 1, 1) + dot(s1, rows, 1, 1)) + dot(s0, rows, 1, 1)
        cross = jnp.where(same, cross, 0.0)
        both = cross[:, :128] + cross[:, 128:]
        both = both + pltpu.roll(both, 64, 1)
        folded[part, :] = both + pltpu.roll(both, 32, 1)
    slot = iota((LIST, USERS_DEV), 0)
    live = jnp.where(slot < counts_ref[...], 1.0, 0.0)
    for a in range(LIST):
        mine = jnp.transpose(folded[pl.ds(a, USERS_DEV, stride=LIST), :])[:LIST, :]
        work[a] = mine * (live * live[a : a + 1, :]) + jnp.where(slot == a, 1.0, 0.0)

    def step(k, carry):
        row = work[k]
        pivot = work[k, pl.ds(k, 1), :]
        inv = 1.0 / pivot
        scaled = row * inv
        here = slot == k
        for a in range(LIST):
            factor = row[a : a + 1, :]
            work[a] = jnp.where(here, factor * inv, work[a] - factor * scaled)
        work[k] = jnp.where(here, -inv, scaled)
        return carry

    lax.fori_loop(0, LIST, step, 0)
    out_ref[...] = -work[...]


def spread(values):
    flat = jnp.transpose(values)
    wide = jnp.concatenate([flat] * 4, axis=1)
    wide = jnp.concatenate([wide] * (SLOTS // 128), axis=1)
    own = iota((USERS_DEV, SLOTS), 1) // LIST == iota((USERS_DEV, SLOTS), 0)
    return jnp.where(own, wide, 0.0)


def weigh(values, fetched):
    s0, s1, s2 = split(spread(values))
    return (dot(s2, fetched) + dot(s1, fetched)) + dot(s0, fetched)


def final_kernel(
    fetched_ref, inverse_ref, inner_ref, counts_ref, pred_ref, users_ref, times_ref, out_ref
):
    fetched = fetched_ref[...]
    inverse = split(inverse_ref[...])
    own = users_ref[...].astype(F32)
    slot = iota((LIST, USERS_DEV), 0)
    lane = iota((LIST, USERS_DEV), 1)
    live = jnp.where(slot < counts_ref[...], 1.0, 0.0)
    pred = pred_ref[0]
    for i in range(1, N_DIM):
        pred = pred + pred_ref[i]
    residual = live * (pred - 1.0)
    gradient = weigh(residual, fetched) + WEIGHT * times_ref[...] + own
    scaled = dot_split(split(gradient), inverse)
    y0, y1, y2 = split(scaled)
    cross = (dot(fetched, y2, 1, 1) + dot(fetched, y1, 1, 1)) + dot(fetched, y0, 1, 1)
    projected = jnp.zeros((LIST, USERS_DEV), F32)
    for user in range(USERS_DEV):
        projected = projected + jnp.where(
            lane == user, cross[user * LIST : (user + 1) * LIST, :], 0.0
        )
    projected = projected * live
    weights = jnp.zeros((LIST, USERS_DEV), F32)
    for a in range(LIST):
        weights = weights + inner_ref[a] * projected[a : a + 1, :]
    weights = weights * live
    back = dot_split(split(weigh(weights, fetched)), inverse)
    out_ref[...] = own - (scaled - back)


def shape(dims, dtype):
    return jax.ShapeDtypeStruct(dims, dtype)


def gather_dims(table):
    up = [(i, (i + 1) % 4) for i in range(4)]
    down = [(i, (i + 3) % 4) for i in range(4)]
    swap = [(0, 1), (1, 0)]
    half = ITEM_DEV // 2
    next_y = lax.ppermute(table, "y", down)
    last_y = lax.ppermute(table, "y", up)
    far_top = lax.ppermute(next_y[:half], "y", down)
    far_low = lax.ppermute(last_y[half:], "y", up)
    far = jnp.concatenate([far_top, far_low], axis=0)
    tables = [table, next_y, far, last_y]
    others = [lax.ppermute(t, "core", swap) for t in tables]
    y = lax.axis_index("y")
    core = lax.axis_index("core")
    blocks = [((y + i) % 4) * 2 + core for i in range(4)]
    blocks += [((y + i) % 4) * 2 + (1 - core) for i in range(4)]
    return tables + others, jnp.stack(blocks).astype(I32)


def on_device(user_rows, item_table, observed_items, counts, item_row):
    exchange = lambda x, axes: lax.all_to_all(x, axes, 0, 0, tiled=True)
    group = USERS_DEV // N_DIM
    users = exchange(user_rows.reshape(N_DIM, group, BLOCK), DIM)
    tables, blocks = gather_dims(item_table)
    diag = dot(item_table, item_table, 0, 0)
    diag = exchange(diag.reshape(N_ROWS, BLOCK // N_ROWS, BLOCK), ROWS)
    pos, req = call(
        index_kernel, (shape((SLOTS, 1), I32), shape((1, SLOTS), I32)), 2, 3 << 30, 4 << 20
    )(observed_items.reshape(SLOTS, 1), item_row.reshape(256, 128))
    req = exchange(req.reshape(N_ROWS, PER), ROWS)
    users = exchange(jnp.broadcast_to(users[None], (8, N_DIM, group, BLOCK)), "z")
    diag = jnp.sum(diag, axis=0)
    diag = exchange(jnp.broadcast_to(diag[None], (N_ROWS, BLOCK // N_ROWS, BLOCK)), ROWS)
    users = exchange(jnp.broadcast_to(users[None], (4, 8, N_DIM, group, BLOCK)), "x")
    users = users.transpose(2, 0, 1, 3, 4).reshape(N_DIM, BLOCK, BLOCK)
    rows = call(pick_kernel, shape((SLOTS, BLOCK), BF16), 2, 1 << 30, 4 << 20)(
        req.reshape(SLOTS, 1), item_table
    )
    came = exchange(rows.reshape(N_ROWS, PER, BLOCK), ROWS).reshape(SLOTS, BLOCK)
    times = call(
        product_kernel,
        shape((BLOCK, N_DIM * BLOCK), F32),
        2 + N_DIM,
        4 << 30,
        8 << 20,
        in_specs=[SMEM] + [VMEM] * (1 + N_DIM),
    )(blocks, users, *tables)
    times = exchange(times.reshape(4, 8, group, N_DIM * BLOCK), "x")
    inverse = call(
        inverse_kernel,
        shape((BLOCK, BLOCK), F32),
        1,
        8 << 30,
        16 << 20,
        scratch=[pltpu.VMEM((BLOCK, BLOCK), F32)],
    )(diag.reshape(BLOCK, BLOCK))
    counts = counts.reshape(1, USERS_DEV)
    fetched, pred = call(
        place_kernel,
        (shape((SLOTS, BLOCK), BF16), shape((LIST, USERS_DEV), F32)),
        3,
        3 << 30,
        8 << 20,
    )(pos, came, user_rows)
    pred = exchange(jnp.broadcast_to(pred[None], (N_DIM, LIST, USERS_DEV)), DIM)
    times = exchange(jnp.sum(times, axis=0), "z")
    inner = call(
        inner_kernel,
        shape((LIST, LIST, USERS_DEV), F32),
        3,
        3 << 30,
        16 << 20,
        scratch=[
            pltpu.VMEM((SLOTS, 128), F32),
            pltpu.VMEM((LIST, LIST, USERS_DEV), F32),
        ],
    )(fetched, inverse, counts)
    times = jnp.sum(times, axis=0).reshape(group, N_DIM, BLOCK).transpose(1, 0, 2)
    times = exchange(times, DIM).reshape(USERS_DEV, BLOCK)
    return call(final_kernel, shape((USERS_DEV, BLOCK), F32), 7, 1 << 30, 4 << 20)(
        fetched, inverse, inner, counts, pred, user_rows, times
    )


def solution(mesh):
    fine = Mesh(mesh.devices.reshape(4, 2, 4, 8), ("y", "core", "x", "z"))
    in_specs = (P(ROWS, DIM), P(ROWS, DIM), P(ROWS, None), P(ROWS), P())
    return jax.shard_map(
        on_device, mesh=fine, in_specs=in_specs, out_specs=P(ROWS, DIM), check_vma=False
    )
```

time: 626 us -> 238 us (0.38)
  other arithmetic: 262 us -> 6.35 us
  waiting for transfers between devices: 247 us -> 65.2 us
  Pallas kernels: 0 us -> 64.8 us
  starting transfers between devices: 0.08 us -> 52.8 us
  local copies, waits for them, and re-layouts: 38.1 us -> 14.6 us
  matrix products: 23.4 us -> 1.04 us
  between operations: 14.8 us -> 0.29 us
  blocking collectives: 39.1 us -> 29.8 us
    another operation x16 -> x0, other arithmetic: 257 us -> none  [the longest x4 189 us: on_device(): inner_factor = jnp.linalg.cholesky(inner)]
    psum x1 -> x0, waiting for transfers between devices: 126 us -> none  [on_device(): gram_rows = lax.psum(gram_part, 'rows')]
    all_gather x2 -> x0, waiting for transfers between devices: 120 us -> none  [the longest x1 76.7 us: on_device(): shard_rows = lax.all_gather(item_table, 'rows', axis=0, tiled=True)]
    all_to_all x0 -> x9, waiting for transfers between devices: none -> 65.2 us  [on_device(): exchange = lambda x, axes: lax.all_to_all(x, axes, 0, 0, tiled=True)]
    pallas_call x0 -> x7, Pallas kernels: none -> 64.8 us  [the longest x1 33.8 us: on_device(): call(inverse_kernel, shape((BLOCK, BLOCK), F32), 1, 8 << 30, 16 << 20, sc...]
    all_to_all x0 -> x9, starting transfers between devices: none -> 47.3 us  [on_device(): exchange = lambda x, axes: lax.all_to_all(x, axes, 0, 0, tiled=True)]
    all_to_all x0 -> x2, blocking collectives: none -> 29.8 us  [on_device(): exchange = lambda x, axes: lax.all_to_all(x, axes, 0, 0, tiled=True)]
    gather x2 -> x0, local copies, waits for them, and re-layouts: 26.3 us -> none  [the longest x1 14.6 us: on_device(): picked = shard_rows[jnp.clip(table_rows, 0, shard_rows.shape[0] - 1)]]
  transfers between devices with their start and end apart: 3 -> 17, of which waited for: 3 -> 7; matrix products, arithmetic and copies ran while one was open for 12% -> 6% of each run, Pallas kernels for 0% -> 23%
where the time goes in v1:
time: 238 us; the launch traced here: 235 us
  waiting for transfers between devices  65.2 us (27%)
  Pallas kernels  64.8 us (27%)
  starting transfers between devices  52.8 us (22%)
  blocking collectives  29.8 us (13%)
  local copies, waits for them, and re-layouts  14.6 us (6%)
  other arithmetic  6.35 us (3%)
    all_to_all x9, waiting for transfers between devices, on_device(): exchange = lambda x, axes: lax.all_to_all(x, axes, 0, 0, tiled=True)  65.2 us
    all_to_all x9, starting transfers between devices, on_device(): exchange = lambda x, axes: lax.all_to_all(x, axes, 0, 0, tiled=True)  47.3 us
    pallas_call x1, Pallas kernels, on_device(): call(inverse_kernel, shape((BLOCK, BLOCK), F32), 1, 8 << 30, 16 << 20, sc...  33.8 us
    all_to_all x2, blocking collectives, on_device(): exchange = lambda x, axes: lax.all_to_all(x, axes, 0, 0, tiled=True)  29.8 us
    pallas_call x1, Pallas kernels, on_device(): call(product_kernel, shape((BLOCK, N_DIM * BLOCK), F32), 2 + N_DIM, 4 <<...  7.16 us
    unnamed x18, local copies, waits for them, and re-layouts  5.72 us
    pallas_call x1, Pallas kernels, on_device(): call(index_kernel, (shape((SLOTS, 1), I32), shape((1, SLOTS), I32)), 2, 3...  5.59 us
    pallas_call x1, Pallas kernels, on_device(): call(place_kernel, (shape((SLOTS, BLOCK), BF16), shape((LIST, USERS_DEV),...  5.35 us
  transfers between devices with their start and end apart: 17, of which 7 were waited for; matrix products, arithmetic and copies ran while one was open for 6% of the time, Pallas kernels for 23%

profile of v1, /device:TPU:2, one launch (start us, length us, event | category | flops | bytes accessed | tf_op | source)
XLA Modules:
  0.0 234.9 jit_solution(11370961407761241918)
XLA Ops:
  0.0 0.8 copy.16
  0.8 1.1 reshape.61.ids_ref
  1.9 0.9 copy-done.2
  2.8 5.6 %shard_map.55 = (s32[2048,1]{1,0:T(8,128)S(1)}, s32[1,2048]{1,0:T(1,128)S(1)}) custom-call(s32[2048,1]{1,0:T(8,128)S(1)} %reshape.61.ids_ref, s32[256,128]{1,0:T(8,128)S(1)} %bitcast.31), custom_call_target="tpu_custom_call" | custom-call | flops 3221225472 | bytes 4194304 | tf_op jit(solution)/shard_map/pallas_call | solution.py:272
  8.4 1.0 copy-done.4
  10.6 20.1 %all_to_all.59 = s32[32,1,64]{2,1,0:T(1,128)S(1)} all-to-all(s32[32,1,64]{2,1,0:T(1,128)S(1)} %bitcast.35), channel_id=1, replica_groups=mesh['y'=4,'core'=2,'x'=4,'z'=8] {'x','z'}, dimensions={0} | all-to-all | bytes 16384 | tf_op jit(solution)/shard_map/all_to_all | solution.py:266
  30.7 9.7 %all_to_all.60 = bf16[8,8,256]{2,1,0:T(8,128)(2,1)S(1)} all-to-all(bf16[8,8,256]{2,1,0:T(8,128)(2,1)S(1)} %bitcast.30), channel_id=1, replica_groups=mesh['y'=4,'core'=2,'x'=4,'z'=8] {'y','core'}, dimensions={0} | all-to-all | bytes 65536 | tf_op jit(solution)/shard_map/all_to_all | solution.py:266
  40.4 0.7 broadcast_in_dim.10
  41.1 3.4 %all-to-all-start.6 = ((bf16[8,8,8,256]{3,2,1,0:T(8,128)(2,1)}), bf16[8,8,8,256]{3,2,1,0:T(8,128)(2,1)S(1)}, u32[]{:S(2)}, u32[]{:S(2)}) async-start(bf16[8,8,8,256]{3,2,1,0:T(8,128)(2,1)} %broadcast_in_dim.10), calls=%async_computation.6 | async-start | bytes 524288 | tf_op jit(solution)/shard_map/all_to_all | solution.py:266
  44.5 1.2 collective-permute-start
  45.8 0.9 collective-permute-start.2
  46.6 1.0 convolution_bitcast_fusion
  47.7 8.9 %all-to-all-done.6 = bf16[8,8,8,256]{3,2,1,0:T(8,128)(2,1)S(1)} async-done(((bf16[8,8,8,256]{3,2,1,0:T(8,128)(2,1)}), bf16[8,8,8,256]{3,2,1,0:T(8,128)(2,1)S(1)}, u32[]{:S(2)}, u32[]{:S(2)}) %all-to-all-start.6) | async-done | bytes 262176 | tf_op jit(solution)/shard_map/all_to_all | solution.py:266
  56.5 5.0 %all-to-all-start.2 = ((f32[32,8,256]{2,1,0:T(8,128)}), f32[32,8,256]{2,1,0:T(8,128)S(1)}, u32[]{:S(2)}, u32[]{:S(2)}) async-start(f32[32,8,256]{2,1,0:T(8,128)} %convolution_bitcast_fusion), calls=%async_computation.2 | async-start | bytes 524288 | tf_op jit(solution)/shard_map/all_to_all | solution.py:266
  61.6 1.2 collective-permute-start.1
  62.8 0.7 slice.9
  63.5 0.9 collective-permute-start.3
  64.4 7.3 %all-to-all-done.2 = f32[32,8,256]{2,1,0:T(8,128)S(1)} async-done(((f32[32,8,256]{2,1,0:T(8,128)}), f32[32,8,256]{2,1,0:T(8,128)S(1)}, u32[]{:S(2)}, u32[]{:S(2)}) %all-to-all-start.2) | async-done | bytes 262176 | tf_op jit(solution)/shard_map/all_to_all | solution.py:266
  71.7 1.1 broadcast_in_dim.11
  72.9 5.6 %all-to-all-start.7 = ((bf16[4,8,8,8,256]{4,3,1,2,0:T(8,128)(2,1)}), bf16[4,8,8,8,256]{4,3,1,2,0:T(8,128)(2,1)}, u32[]{:S(2)}, u32[]{:S(2)}) async-start(bf16[4,8,8,8,256]{4,3,1,2,0:T(8,128)(2,1)} %broadcast_in_dim.11), calls=%async_computation.7 | async-start | bytes 2097152 | tf_op jit(solution)/shard_map/all_to_all | solution.py:266
  79.0 1.0 constant_dynamic-update-slice_fusion.1
  80.0 1.0 constant_dynamic-update-slice_fusion.refs_2_
  80.9 0.8 collective-permute-start.6
  81.7 1.0 reduce_sum.27
  82.7 6.8 %all-to-all-done.7 = bf16[4,8,8,8,256]{4,3,1,2,0:T(8,128)(2,1)} async-done(((bf16[4,8,8,8,256]{4,3,1,2,0:T(8,128)(2,1)}), bf16[4,8,8,8,256]{4,3,1,2,0:T(8,128)(2,1)}, u32[]{:S(2)}, u32[]{:S(2)}) %all-to-all-start.7) | async-done | bytes 1048608 | tf_op jit(solution)/shard_map/all_to_all | solution.py:266
  89.5 0.7 broadcast_in_dim.8
  90.2 6.3 %all-to-all-start.3 = ((f32[32,8,256]{2,1,0:T(8,128)}), f32[32,8,256]{2,1,0:T(8,128)S(1)}, u32[]{:S(2)}, u32[]{:S(2)}) async-start(f32[32,8,256]{2,1,0:T(8,128)} %broadcast_in_dim.8), calls=%async_computation.3 | async-start | bytes 524288 | tf_op jit(solution)/shard_map/all_to_all | solution.py:266
  96.7 1.3 copy.21
  98.1 7.2 %shard_map.60 = f32[256,2048]{1,0:T(8,128)} custom-call(s32[8]{0:T(128)S(1)} %stack.35.block_ref, bf16[8,256,256]{2,1,0:T(8,128)(2,1)S(1)} %bitcast.26, bf16[1024,256]{1,0:T(8,128)(2,1)S(1)} %copy-done, bf16[1024,256]{1,0:T(8,128)(2,1)S(1)} %collective-permute-done.refs_1_, bf16[1024,256]{1,0:T(8,128)(2,1)S(1)} %constant_dynamic-update-slice_fusion.refs_2_, ...), custom_call_target="tpu_custom_call" | custom-call | flops 4294967296 | bytes 8388608 | tf_op jit(solution)/shard_map/pallas_call | solution.py:285
  105.2 1.0 all-to-all-done.3
  106.2 5.8 %all-to-all-start.8 = ((f32[4,8,8,2048]{3,2,1,0:T(8,128)}), f32[4,8,8,2048]{3,2,1,0:T(8,128)}, u32[]{:S(2)}, u32[]{:S(2)}) async-start(f32[4,8,8,2048]{3,2,1,0:T(8,128)} %bitcast.34), calls=%async_computation.8 | async-start | bytes 4194304 | tf_op jit(solution)/shard_map/all_to_all | solution.py:266
  112.8 1.0 reshape.62.req_ref
  113.8 2.3 shard_map.56
  116.1 16.5 %all-to-all-done.8 = f32[4,8,8,2048]{3,2,1,0:T(8,128)} async-done(((f32[4,8,8,2048]{3,2,1,0:T(8,128)}), f32[4,8,8,2048]{3,2,1,0:T(8,128)}, u32[]{:S(2)}, u32[]{:S(2)}) %all-to-all-start.8) | async-done | bytes 2097184 | tf_op jit(solution)/shard_map/all_to_all | solution.py:266
  132.6 7.9 %all-to-all-start.1 = ((bf16[32,64,256]{2,1,0:T(8,128)(2,1)}), bf16[32,64,256]{2,1,0:T(8,128)(2,1)S(1)}, u32[]{:S(2)}, u32[]{:S(2)}) async-start(bf16[32,64,256]{2,1,0:T(8,128)(2,1)} %bitcast.2), calls=%async_computation.1 | async-start | bytes 2097152 | tf_op jit(solution)/shard_map/all_to_all | solution.py:266
  140.5 2.5 %reduce_sum.28 = f32[8,8,2048]{2,1,0:T(8,128)} reduce(f32[4,8,8,2048]{3,2,1,0:T(8,128)} %all-to-all-done.8, f32[]{:T(128)} %constant.42.clone.1), dimensions={0}, to_apply=%region_1.2 | reduce | flops 393216 | bytes 2621444 | tf_op jit(solution)/shard_map/reduce_sum | solution.py:311
  143.1 18.8 %all-to-all-done.1 = bf16[32,64,256]{2,1,0:T(8,128)(2,1)S(1)} async-done(((bf16[32,64,256]{2,1,0:T(8,128)(2,1)}), bf16[32,64,256]{2,1,0:T(8,128)(2,1)S(1)}, u32[]{:S(2)}, u32[]{:S(2)}) %all-to-all-start.1) | async-done | bytes 1048608 | tf_op jit(solution)/shard_map/all_to_all | solution.py:266
  161.9 5.2 %all-to-all-start.9 = ((f32[8,8,2048]{2,1,0:T(8,128)}), f32[8,8,2048]{2,1,0:T(8,128)S(1)}, u32[]{:S(2)}, u32[]{:S(2)}) async-start(f32[8,8,2048]{2,1,0:T(8,128)} %reduce_sum.28), calls=%async_computation.9 | async-start | bytes 1048576 | tf_op jit(solution)/shard_map/all_to_all | solution.py:266
  167.1 1.2 copy-done.5
  168.3 5.4 %shard_map.57 = (bf16[2048,256]{1,0:T(8,128)(2,1)S(1)}, f32[32,64]{1,0:T(8,128)S(1)}) custom-call(s32[2048,1]{1,0:T(8,128)S(1)} %copy-done.5, bf16[2048,256]{1,0:T(8,128)(2,1)S(1)} %bitcast.27, bf16[64,256]{1,0:T(8,128)(2,1)S(1)} %copy-done.1), custom_call_target="tpu_custom_call" | custom-call | flops 3221225472 | bytes 8388608 | tf_op jit(solution)/shard_map/pallas_call | solution.py:303
  173.7 0.8 reshape.79
  174.4 5.9 %all-to-all-done.9 = f32[8,8,2048]{2,1,0:T(8,128)S(1)} async-done(((f32[8,8,2048]{2,1,0:T(8,128)}), f32[8,8,2048]{2,1,0:T(8,128)S(1)}, u32[]{:S(2)}, u32[]{:S(2)}) %all-to-all-start.9) | async-done | bytes 524320 | tf_op jit(solution)/shard_map/all_to_all | solution.py:266
  180.3 3.4 %all-to-all-start.4 = ((f32[8,1,2048]{2,1,0:T(1,128)}), f32[8,1,2048]{2,1,0:T(1,128)S(1)}, u32[]{:S(2)}, u32[]{:S(2)}) async-start(f32[8,1,2048]{2,1,0:T(1,128)} %reshape.79), calls=%async_computation.4 | async-start | bytes 131072 | tf_op jit(solution)/shard_map/all_to_all | solution.py:266
  183.7 33.8 %shard_map.58.inverse_ref = f32[256,256]{1,0:T(8,128)S(1)} custom-call(f32[256,256]{1,0:T(8,128)S(1)} %bitcast.28), custom_call_target="tpu_custom_call" | custom-call | flops 8589934592 | bytes 16777216 | tf_op jit(solution)/shard_map/pallas_call | solution.py:294
  218.2 4.7 %all-to-all-start.10 = ((f32[8,8,256]{2,1,0:T(8,128)}), f32[8,8,256]{2,1,0:T(8,128)S(1)}, u32[]{:S(2)}, u32[]{:S(2)}) async-start(f32[8,8,256]{2,1,0:T(8,128)} %bitcast.20), calls=%async_computation.10 | async-start | bytes 131072 | tf_op jit(solution)/shard_map/all_to_all | solution.py:266
  223.0 5.3 %shard_map.59.inner_ref = f32[32,32,64]{2,1,0:T(8,128)S(1)} custom-call(bf16[2048,256]{1,0:T(8,128)(2,1)S(1)} %get-tuple-element.11.fetched_ref, f32[256,256]{1,0:T(8,128)S(1)} %shard_map.58.inverse_ref, s32[1,64]{1,0:T(1,128)S(1)} %bitcast.32), custom_call_target="tpu_custom_call" | custom-call | flops 3221225472 | bytes 16777216 | tf_op jit(solution)/shard_map/pallas_call | solution.py:312
  228.7 0.8 reduce.8
  229.6 5.3 %shard_map.61 = f32[64,256]{1,0:T(8,128)} custom-call(bf16[2048,256]{1,0:T(8,128)(2,1)S(1)} %get-tuple-element.11.fetched_ref, f32[256,256]{1,0:T(8,128)S(1)} %shard_map.58.inverse_ref, f32[32,32,64]{2,1,0:T(8,128)S(1)} %shard_map.59.inner_ref, s32[1,64]{1,0:T(1,128)S(1)} %bitcast.33, f32[8,32,64]{2,1,0:T(8,128)S(1)} %reshape.80.pred_ref, ...), custom_call_target="tpu_custom_call" | custom-call | flops 1073741824 | bytes 4194304 | tf_op jit(solution)/shard_map/pallas_call | solution.py:325
  (35 shorter events, 3.9 us)
Async XLA Ops:
  1.9 0.9 copy-start.2
  2.8 27.9 %copy-start.1 = (bf16[64,256]{1,0:T(8,128)(2,1)S(1)}, bf16[64,256]{1,0:T(8,128)(2,1)}, u32[]{:S(2)}) copy-start(bf16[64,256]{1,0:T(8,128)(2,1)} %users_ref.3) | copy-start | bytes 98308
  2.8 41.7 %copy-start = (bf16[1024,256]{1,0:T(8,128)(2,1)S(1)}, bf16[1024,256]{1,0:T(8,128)(2,1)}, u32[]{:S(2)}) copy-start(bf16[1024,256]{1,0:T(8,128)(2,1)} %refs_0_.1) | copy-start | bytes 1572868
  8.4 1.0 copy-start.4
  41.1 15.4 %all-to-all-start.6 = ((bf16[8,8,8,256]{3,2,1,0:T(8,128)(2,1)}), bf16[8,8,8,256]{3,2,1,0:T(8,128)(2,1)S(1)}, u32[]{:S(2)}, u32[]{:S(2)}) async-start(bf16[8,8,8,256]{3,2,1,0:T(8,128)(2,1)} %broadcast_in_dim.10), calls=%async_computation.6 | async-start | bytes 524288 | tf_op jit(solution)/shard_map/all_to_all | solution.py:266
  44.5 17.0 %collective-permute-start = (bf16[1024,256]{1,0:T(8,128)(2,1)S(1)}, bf16[1024,256]{1,0:T(8,128)(2,1)S(1)}, u32[]{:S(2)}, u32[]{:S(2)}) collective-permute-start(bf16[1024,256]{1,0:T(8,128)(2,1)S(1)} %copy-done), channel_id=1, source_target_pairs={{0,192},{64,0},{128,64},{192,128},{1,193},{65,1},{129,65},{193,129... | collective-permute-start | bytes 1572872 | tf_op jit(solution)/shard_map/ppermute | solution.py:251
  45.8 17.0 %collective-permute-start.2 = (bf16[1024,256]{1,0:T(8,128)(2,1)S(1)}, bf16[1024,256]{1,0:T(8,128)(2,1)S(1)}, u32[]{:S(2)}, u32[]{:S(2)}) collective-permute-start(bf16[1024,256]{1,0:T(8,128)(2,1)S(1)} %copy-done), channel_id=1, source_target_pairs={{0,64},{64,128},{128,192},{192,0},{1,65},{65,129},{129,193},{193,1... | collective-permute-start | bytes 1572872 | tf_op jit(solution)/shard_map/ppermute | solution.py:252
  56.5 15.2 %all-to-all-start.2 = ((f32[32,8,256]{2,1,0:T(8,128)}), f32[32,8,256]{2,1,0:T(8,128)S(1)}, u32[]{:S(2)}, u32[]{:S(2)}) async-start(f32[32,8,256]{2,1,0:T(8,128)} %convolution_bitcast_fusion), calls=%async_computation.2 | async-start | bytes 524288 | tf_op jit(solution)/shard_map/all_to_all | solution.py:266
  61.6 17.4 %collective-permute-start.1 = (bf16[512,256]{1,0:T(8,128)(2,1)S(1)}, bf16[512,256]{1,0:T(8,128)(2,1)}, u32[]{:S(2)}, u32[]{:S(2)}) collective-permute-start(bf16[512,256]{1,0:T(8,128)(2,1)S(1)} %slice.8), channel_id=1, source_target_pairs={{0,192},{64,0},{128,64},{192,128},{1,193},{65,1},{129,65},{193,129... | collective-permute-start | bytes 786440 | tf_op jit(solution)/shard_map/ppermute | solution.py:253
  63.5 16.4 %collective-permute-start.3 = (bf16[512,256]{1,0:T(8,128)(2,1)}, bf16[512,256]{1,0:T(8,128)(2,1)}, u32[]{:S(2)}, u32[]{:S(2)}) collective-permute-start(bf16[512,256]{1,0:T(8,128)(2,1)} %slice.9), channel_id=1, source_target_pairs={{0,64},{64,128},{128,192},{192,0},{1,65},{65,129},{129,193},{193,1... | collective-permute-start | bytes 786440 | tf_op jit(solution)/shard_map/ppermute | solution.py:254
  71.7 1.1 copy-start.6
  72.9 16.6 %all-to-all-start.7 = ((bf16[4,8,8,8,256]{4,3,1,2,0:T(8,128)(2,1)}), bf16[4,8,8,8,256]{4,3,1,2,0:T(8,128)(2,1)}, u32[]{:S(2)}, u32[]{:S(2)}) async-start(bf16[4,8,8,8,256]{4,3,1,2,0:T(8,128)(2,1)} %broadcast_in_dim.11), calls=%async_computation.7 | async-start | bytes 2097152 | tf_op jit(solution)/shard_map/all_to_all | solution.py:266
  78.5 19.6 %collective-permute-start.4 = (bf16[1024,256]{1,0:T(8,128)(2,1)S(1)}, bf16[1024,256]{1,0:T(8,128)(2,1)S(1)}, u32[]{:S(2)}, u32[]{:S(2)}) collective-permute-start(bf16[1024,256]{1,0:T(8,128)(2,1)S(1)} %copy-done), channel_id=1, source_target_pairs={{0,32},{32,0},{1,33},{33,1},{2,34},{34,2},{3,35},{35,3},{4,36},{36... | collective-permute-start | bytes 1572872 | tf_op jit(solution)/shard_map/ppermute | solution.py:257
  78.5 19.6 %collective-permute-start.5 = (bf16[1024,256]{1,0:T(8,128)(2,1)S(1)}, bf16[1024,256]{1,0:T(8,128)(2,1)S(1)}, u32[]{:S(2)}, u32[]{:S(2)}) collective-permute-start(bf16[1024,256]{1,0:T(8,128)(2,1)S(1)} %collective-permute-done.refs_1_), channel_id=1, source_target_pairs={{0,32},{32,0},{1,33},{33,1},{2,34},{34,2},{3,35},{35,3},{4,36},{36... | collective-permute-start | bytes 1572872 | tf_op jit(solution)/shard_map/ppermute | solution.py:257
  79.0 19.1 %collective-permute-start.7 = (bf16[1024,256]{1,0:T(8,128)(2,1)S(1)}, bf16[1024,256]{1,0:T(8,128)(2,1)}, u32[]{:S(2)}, u32[]{:S(2)}) collective-permute-start(bf16[1024,256]{1,0:T(8,128)(2,1)S(1)} %collective-permute-done.2.refs_3_), channel_id=1, source_target_pairs={{0,32},{32,0},{1,33},{33,1},{2,34},{34,2},{3,35},{35,3},{4,36},{36... | collective-permute-start | bytes 1572872 | tf_op jit(solution)/shard_map/ppermute | solution.py:257
  80.9 17.1 %collective-permute-start.6 = (bf16[1024,256]{1,0:T(8,128)(2,1)S(1)}, bf16[1024,256]{1,0:T(8,128)(2,1)}, u32[]{:S(2)}, u32[]{:S(2)}) collective-permute-start(bf16[1024,256]{1,0:T(8,128)(2,1)S(1)} %constant_dynamic-update-slice_fusion.refs_2_), channel_id=1, source_target_pairs={{0,32},{32,0},{1,33},{33,1},{2,34},{34,2},{3,35},{35,3},{4,36},{36... | collective-permute-start | bytes 1572872 | tf_op jit(solution)/shard_map/ppermute | solution.py:257
  90.2 16.0 %all-to-all-start.3 = ((f32[32,8,256]{2,1,0:T(8,128)}), f32[32,8,256]{2,1,0:T(8,128)S(1)}, u32[]{:S(2)}, u32[]{:S(2)}) async-start(f32[32,8,256]{2,1,0:T(8,128)} %broadcast_in_dim.8), calls=%async_computation.3 | async-start | bytes 524288 | tf_op jit(solution)/shard_map/all_to_all | solution.py:266
  106.2 26.3 %all-to-all-start.8 = ((f32[4,8,8,2048]{3,2,1,0:T(8,128)}), f32[4,8,8,2048]{3,2,1,0:T(8,128)}, u32[]{:S(2)}, u32[]{:S(2)}) async-start(f32[4,8,8,2048]{3,2,1,0:T(8,128)} %bitcast.34), calls=%async_computation.8 | async-start | bytes 4194304 | tf_op jit(solution)/shard_map/all_to_all | solution.py:266
  132.6 29.3 %all-to-all-start.1 = ((bf16[32,64,256]{2,1,0:T(8,128)(2,1)}), bf16[32,64,256]{2,1,0:T(8,128)(2,1)S(1)}, u32[]{:S(2)}, u32[]{:S(2)}) async-start(bf16[32,64,256]{2,1,0:T(8,128)(2,1)} %bitcast.2), calls=%async_computation.1 | async-start | bytes 2097152 | tf_op jit(solution)/shard_map/all_to_all | solution.py:266
  161.9 18.5 %all-to-all-start.9 = ((f32[8,8,2048]{2,1,0:T(8,128)}), f32[8,8,2048]{2,1,0:T(8,128)S(1)}, u32[]{:S(2)}, u32[]{:S(2)}) async-start(f32[8,8,2048]{2,1,0:T(8,128)} %reduce_sum.28), calls=%async_computation.9 | async-start | bytes 1048576 | tf_op jit(solution)/shard_map/all_to_all | solution.py:266
  167.1 1.2 copy-start.5
  180.3 37.9 %all-to-all-start.4 = ((f32[8,1,2048]{2,1,0:T(1,128)}), f32[8,1,2048]{2,1,0:T(1,128)S(1)}, u32[]{:S(2)}, u32[]{:S(2)}) async-start(f32[8,1,2048]{2,1,0:T(1,128)} %reshape.79), calls=%async_computation.4 | async-start | bytes 131072 | tf_op jit(solution)/shard_map/all_to_all | solution.py:266
  183.7 39.2 %copy-start.3 = (s32[64]{0:T(128)S(1)}, s32[64]{0:T(128)}, u32[]{:S(2)}) copy-start(s32[64]{0:T(128)} %param.8) | copy-start | bytes 772
  218.2 11.4 %all-to-all-start.10 = ((f32[8,8,256]{2,1,0:T(8,128)}), f32[8,8,256]{2,1,0:T(8,128)S(1)}, u32[]{:S(2)}, u32[]{:S(2)}) async-start(f32[8,8,256]{2,1,0:T(8,128)} %bitcast.20), calls=%async_computation.10 | async-start | bytes 131072 | tf_op jit(solution)/shard_map/all_to_all | solution.py:266

commit v2 on v1

v2 whole, which is shorter than its diff:
```python
import jax
import jax.numpy as jnp
from jax import lax
from jax.experimental import pallas as pl
from jax.experimental.pallas import tpu as pltpu
from jax.sharding import Mesh, PartitionSpec as P

F32 = jnp.float32
BF16 = jnp.bfloat16
I32 = jnp.int32
ROWS = ("x", "z")
DIM = ("y", "core")
BLOCK = 256
LIST = 32
USERS_DEV = 64
SLOTS = USERS_DEV * LIST
ITEM_DEV = 1024
N_ROWS = 32
N_DIM = 8
PER = SLOTS // N_ROWS
CHUNK = 256
CHUNKS = SLOTS // CHUNK
WEIGHT = 32.0 / 32768.0
VMEM = pl.BlockSpec(memory_space=pltpu.VMEM)
SMEM = pl.BlockSpec(memory_space=pltpu.SMEM)


def iota(shape, dim):
    return lax.broadcasted_iota(I32, shape, dim)


def dot(a, b, ca=1, cb=0):
    return lax.dot_general(a, b, (((ca,), (cb,)), ((), ())), preferred_element_type=F32)


def split(a):
    top = a.astype(BF16)
    rest = a - top.astype(F32)
    mid = rest.astype(BF16)
    low = (rest - mid.astype(F32)).astype(BF16)
    return top, mid, low


def dot_split(a, b, ca=1, cb=0):
    a0, a1, a2 = a
    b0, b1, b2 = b
    small = dot(a2, b0, ca, cb) + dot(a0, b2, ca, cb) + dot(a1, b1, ca, cb)
    return (small + (dot(a1, b0, ca, cb) + dot(a0, b1, ca, cb))) + dot(a0, b0, ca, cb)


def one_hot(column, width):
    hit = iota((column.shape[0], width), 1) == column
    return jnp.where(hit, 1.0, 0.0).astype(BF16)


def call(kernel, out_shape, n_in, flops, nbytes, scratch=(), in_specs=None):
    multi = isinstance(out_shape, (tuple, list))
    return pl.pallas_call(
        kernel,
        out_shape=out_shape,
        in_specs=in_specs or [VMEM] * n_in,
        out_specs=[VMEM] * len(out_shape) if multi else VMEM,
        scratch_shapes=list(scratch),
        compiler_params=pltpu.CompilerParams(vmem_limit_bytes=20 << 20),
        cost_estimate=pl.CostEstimate(flops=flops, bytes_accessed=nbytes, transcendentals=0),
    )


def chunk_column(array, c):
    width = array.shape[0]
    step = CHUNK // width
    return jnp.concatenate(
        [array[:, c * step + i : c * step + i + 1] for i in range(step)], axis=0
    )


def index_kernel(ids_ref, table_ref, diag_ref, pos_ref, sent_ref):
    table = table_ref[...]
    table_hi = (table >> 8).astype(F32).astype(BF16)
    table_lo = (table & 255).astype(F32).astype(BF16)
    lane = iota((CHUNK, 128), 1)
    before = jnp.where(
        iota((CHUNK, CHUNK), 0) > iota((CHUNK, CHUNK), 1), 1.0, 0.0
    ).astype(BF16)
    totals = jnp.zeros((1, 128), F32)
    asked = jnp.zeros((128, 128), F32)
    places = jnp.zeros((CHUNK, 128), I32)
    ids_all = ids_ref[...]
    for c in range(CHUNKS):
        ids = chunk_column(ids_all, c)
        picked = one_hot(ids >> 7, 256)
        values = dot(picked, table_hi) * 256.0 + dot(picked, table_lo)
        row = jnp.sum(jnp.where(lane == (ids & 127), values, 0.0), axis=1, keepdims=True)
        row = row.astype(I32)
        member = jnp.where(lane == (row >> 10), 1.0, 0.0)
        ranks = dot(before, member.astype(BF16)) + totals
        rank = jnp.sum(member * ranks, axis=1, keepdims=True).astype(I32)
        totals = totals + jnp.sum(member, axis=0, keepdims=True)
        places = jnp.where(lane == c, (row >> 10) * PER + rank, places)
        ranked = one_hot(rank, 128)
        high = member * ((row >> 5) & 31).astype(F32)
        low = member * (row & 31).astype(F32)
        asked = asked + dot(high.astype(BF16), ranked, 0, 0) * 32.0
        asked = asked + dot(low.astype(BF16), ranked, 0, 0)
    pos_ref[...] = places
    sent_ref[...] = jnp.zeros(sent_ref.shape, F32)
    sent_ref[:, :8, :] = diag_ref[...]
    for k in range(N_ROWS):
        sent_ref[k, 8:9, :128] = asked[k : k + 1, :]


def pick_kernel(came_ref, table_ref, rows_ref, diag_ref):
    table = table_ref[...]
    diag = came_ref[0, :8, :]
    for r in range(1, N_ROWS):
        diag = diag + came_ref[r, :8, :]
    diag_ref[...] = jnp.broadcast_to(diag[None], diag_ref.shape)
    asked = jnp.concatenate([came_ref[r, 8:9, :128] for r in range(N_ROWS)], axis=0)
    asked = jnp.transpose(asked).astype(I32)
    asked = asked[:PER, :]
    for c in range(CHUNKS):
        column = chunk_column(asked, c)
        rows = dot(one_hot(column, ITEM_DEV), table).astype(BF16)
        rows_ref[c * CHUNK : (c + 1) * CHUNK, :] = rows


def place_kernel(pos_ref, came_ref, users_ref, fetched_ref, pred_ref):
    came = came_ref[...]
    users = users_ref[...]
    lane = iota((LIST, USERS_DEV), 1)
    pred = jnp.zeros((LIST, USERS_DEV), F32)
    for c in range(CHUNKS):
        part = slice(c * CHUNK, (c + 1) * CHUNK)
        rows = dot(one_hot(pos_ref[:, c : c + 1], SLOTS), came).astype(BF16)
        fetched_ref[part, :] = rows
        cross = dot(rows, users, 1, 1)
        for i in range(CHUNK // LIST):
            user = c * (CHUNK // LIST) + i
            pred = pred + jnp.where(lane == user, cross[i * LIST : (i + 1) * LIST, :], 0.0)
    pred_ref[...] = pred


def product_kernel(block_ref, *refs):
    users_refs, tables = refs[:4], refs[4 : 4 + N_DIM]
    out_refs, held, sems = refs[4 + N_DIM : -2], refs[-2], refs[-1]
    quarter = BLOCK // 4
    copies = [pltpu.make_async_copy(tables[i], held.at[i], sems.at[i]) for i in range(N_DIM)]
    for copy in copies:
        copy.start()
    scores = jnp.zeros((BLOCK, ITEM_DEV), F32)
    for i in range(N_DIM):
        block = block_ref[i]
        users = [u[:, block].astype(F32).reshape(quarter, BLOCK) for u in users_refs]
        users = jnp.concatenate(users, axis=0).astype(BF16)
        copies[i].wait()
        scores = scores + dot(users, held[i], 1, 1)
    s0, s1, s2 = split(scores)
    for i in range(N_DIM):
        table = held[i]
        times = (dot(s2, table) + dot(s1, table)) + dot(s0, table)
        for n, out_ref in enumerate(out_refs):
            part = times[n * quarter : (n + 1) * quarter]
            out_ref[:, block_ref[i]] = part.reshape(8, quarter // 8, BLOCK)


def sweep(work):
    size = 128
    lane = iota((8, size), 1)
    wide = iota((size, size), 1)

    def at_lane(row, k):
        return jnp.take_along_axis(row, jnp.full((8, size), k, I32), axis=1)

    def load(k):
        return jnp.broadcast_to(work[pl.ds(k, 1), :], (8, size))

    def column(row):
        return jnp.transpose(jnp.broadcast_to(row[:1], (size, size)))

    def step(n, rows):
        row0, raw1 = rows
        k = 2 * n
        after = jnp.minimum(k + 2, size - 2)
        old2 = load(after)
        old3 = load(after + 1)
        inv0 = 1.0 / at_lane(row0, k)
        c01 = at_lane(row0, k + 1)
        a2, a3 = at_lane(row0, after), at_lane(row0, after + 1)
        b2, b3 = at_lane(raw1, after), at_lane(raw1, after + 1)
        low = c01 * inv0
        inv1 = 1.0 / (at_lane(raw1, k + 1) - c01 * low)
        w0 = row0 * inv0
        row1 = jnp.where(lane == k, low, raw1 - c01 * w0)
        w1 = row1 * inv1
        b2 = b2 - low * a2
        b3 = b3 - low * a3

        def advance(old, a, b):
            once = jnp.where(lane == k, a * inv0, old - a * w0)
            return jnp.where(lane == k + 1, b * inv1, once - b * w1)

        next0 = advance(old2, a2, b2)
        next1 = advance(old3, a3, b3)
        col0, col1 = column(row0), column(row1)
        new = jnp.where(wide == k, col0 * inv0[:1], work[...] - col0 * w0[:1])
        work[...] = jnp.where(wide == k + 1, col1 * inv1[:1], new - col1 * w1[:1])
        done0 = jnp.where(lane == k, -inv0, w0)
        done0 = jnp.where(lane == k + 1, low * inv1, done0 - low * w1)
        work[pl.ds(k, 1), :] = done0[:1]
        work[pl.ds(k + 1, 1), :] = jnp.where(lane == k + 1, -inv1, w1)[:1]
        return next0, next1

    lax.fori_loop(0, size // 2, step, (load(0), load(1)))
    return -work[...]


def inverse_kernel(diag_ref, out_ref, work):
    half = BLOCK // 2
    eye = jnp.where(iota((half, half), 0) == iota((half, half), 1), 1.0, 0.0)
    upper = WEIGHT * diag_ref[:half, half:]
    work[...] = WEIGHT * diag_ref[:half, :half] + eye
    lead = sweep(work)
    lead_split = split(lead)
    upper_split = split(upper)
    mixed = dot_split(lead_split, upper_split)
    mixed_split = split(mixed)
    work[...] = WEIGHT * diag_ref[half:, half:] + eye - dot_split(upper_split, mixed_split, 0, 0)
    rest = sweep(work)
    cross = dot_split(mixed_split, split(rest))
    out_ref[:half, :half] = lead + dot_split(split(cross), mixed_split, 1, 1)
    out_ref[:half, half:] = -cross
    out_ref[half:, :half] = -jnp.transpose(cross)
    out_ref[half:, half:] = rest


def inner_kernel(fetched_ref, inverse_ref, counts_ref, out_ref, folded, work):
    i0, i1, i2 = split(inverse_ref[...])
    same = iota((CHUNK, CHUNK), 0) // LIST == iota((CHUNK, CHUNK), 1) // LIST

    def chunk(c, carry):
        part = pl.ds(pl.multiple_of(c * CHUNK, CHUNK), CHUNK)
        rows = fetched_ref[part, :]
        scaled = (dot(rows, i2) + dot(rows, i1)) + dot(rows, i0)
        s0, s1, s2 = split(scaled)
        cross = (dot(s2, rows, 1, 1) + dot(s1, rows, 1, 1)) + dot(s0, rows, 1, 1)
        cross = jnp.where(same, cross, 0.0)
        both = cross[:, :128] + cross[:, 128:]
        both = both + pltpu.roll(both, 64, 1)
        folded[part, :] = both + pltpu.roll(both, 32, 1)
        return carry

    lax.fori_loop(0, CHUNKS, chunk, 0, unroll=2)
    slot = iota((LIST, USERS_DEV), 0)
    live = jnp.where(slot < counts_ref[...], 1.0, 0.0)
    for a in range(LIST):
        mine = jnp.transpose(folded[pl.ds(a, USERS_DEV, stride=LIST), :])[:LIST, :]
        work[a] = mine * (live * live[a : a + 1, :]) + jnp.where(slot == a, 1.0, 0.0)

    def step(k, carry):
        row = work[k]
        pivot = work[k, pl.ds(k, 1), :]
        inv = 1.0 / pivot
        scaled = row * inv
        here = slot == k
        for a in range(LIST):
            factor = row[a : a + 1, :]
            work[a] = jnp.where(here, factor * inv, work[a] - factor * scaled)
        work[k] = jnp.where(here, -inv, scaled)
        return carry

    lax.fori_loop(0, LIST, step, 0)
    out_ref[...] = -work[...]


def spread(values):
    flat = jnp.transpose(values)
    wide = jnp.concatenate([flat] * 4, axis=1)
    wide = jnp.concatenate([wide] * (SLOTS // 128), axis=1)
    own = iota((USERS_DEV, SLOTS), 1) // LIST == iota((USERS_DEV, SLOTS), 0)
    return jnp.where(own, wide, 0.0)


def weigh(values, fetched):
    s0, s1, s2 = split(spread(values))
    return (dot(s2, fetched) + dot(s1, fetched)) + dot(s0, fetched)


def final_kernel(
    fetched_ref, inverse_ref, inner_ref, counts_ref, users_ref, times_ref, *refs
):
    pred_refs, out_ref = refs[:-1], refs[-1]
    fetched = fetched_ref[...]
    inverse = split(inverse_ref[...])
    own = users_ref[...].astype(F32)
    slot = iota((LIST, USERS_DEV), 0)
    lane = iota((LIST, USERS_DEV), 1)
    live = jnp.where(slot < counts_ref[...], 1.0, 0.0)
    pred = pred_refs[0][...]
    for ref in pred_refs[1:]:
        pred = pred + ref[...]
    residual = live * (pred - 1.0)
    times = times_ref[0]
    for i in range(1, 8):
        times = times + times_ref[i]
    gradient = weigh(residual, fetched) + WEIGHT * times + own
    scaled = dot_split(split(gradient), inverse)
    y0, y1, y2 = split(scaled)
    cross = (dot(fetched, y2, 1, 1) + dot(fetched, y1, 1, 1)) + dot(fetched, y0, 1, 1)
    projected = jnp.zeros((LIST, USERS_DEV), F32)
    for user in range(USERS_DEV):
        projected = projected + jnp.where(
            lane == user, cross[user * LIST : (user + 1) * LIST, :], 0.0
        )
    projected = projected * live
    weights = jnp.zeros((LIST, USERS_DEV), F32)
    for a in range(LIST):
        weights = weights + inner_ref[a] * projected[a : a + 1, :]
    weights = weights * live
    back = dot_split(split(weigh(weights, fetched)), inverse)
    out_ref[...] = own - (scaled - back)


def shape(dims, dtype):
    return jax.ShapeDtypeStruct(dims, dtype)


def shift(x, axis, by):
    size = {"x": 4, "y": 4, "core": 2}[axis]
    return lax.ppermute(x, axis, [(i, (i + by) % size) for i in range(size)])


def gather_dims(table):
    tables = [table] + [shift(table, "y", 4 - i) for i in (1, 3, 2)]
    tables = tables + [shift(t, "core", 1) for t in tables]
    y = lax.axis_index("y")
    core = lax.axis_index("core")
    blocks = [((y + i) % 4) * 2 + (core + j) % 2 for j in (0, 1) for i in (0, 1, 3, 2)]
    return tables, jnp.stack(blocks).astype(I32)


def exchange(x, axes):
    return lax.all_to_all(x, axes, 0, 0, tiled=True)


def body(user_rows, item_table, observed_items, counts, item_row):
    group = USERS_DEV // N_DIM
    slice_rows = BLOCK // N_ROWS
    users = user_rows.reshape(1, N_DIM, group, BLOCK)
    users = jnp.broadcast_to(users, (8, N_DIM, group, BLOCK))
    users = exchange(users.reshape(8 * N_DIM, group, BLOCK), ("z",) + DIM)
    tables, blocks = gather_dims(item_table)
    diag = dot(item_table, item_table, 0, 0).reshape(N_ROWS, slice_rows, BLOCK)
    pos, sent = call(
        index_kernel, (shape((CHUNK, 128), I32), shape((N_ROWS, 16, BLOCK), F32)), 3, 1 << 30, 4 << 20
    )(observed_items.T, item_row.reshape(256, 128), diag)
    came = exchange(sent, ROWS)
    users = users.reshape(8, N_DIM, group, BLOCK)
    users = [users] + [shift(users, "x", 4 - i) for i in range(1, 4)]
    rows, diag = call(
        pick_kernel,
        (shape((SLOTS, BLOCK), BF16), shape((N_ROWS, slice_rows, BLOCK), F32)),
        2,
        1 << 30,
        4 << 20,
    )(came, item_table)
    came = exchange(rows.reshape(N_ROWS, PER, BLOCK), ROWS).reshape(SLOTS, BLOCK)
    diag = exchange(diag, ROWS)
    times = call(
        product_kernel,
        [shape((8, N_DIM, group, BLOCK), F32)] * 4,
        5 + len(tables),
        4 << 30,
        8 << 20,
        scratch=[
            pltpu.VMEM((N_DIM, ITEM_DEV, BLOCK), BF16),
            pltpu.SemaphoreType.DMA((N_DIM,)),
        ],
        in_specs=[SMEM] + [VMEM] * 4 + [pl.BlockSpec(memory_space=pl.ANY)] * N_DIM,
    )(blocks, *users, *tables)
    times = [times[0]] + [shift(times[i], "x", i) for i in range(1, 4)]
    inverse = call(
        inverse_kernel,
        shape((BLOCK, BLOCK), F32),
        1,
        4 << 30,
        8 << 20,
        scratch=[pltpu.VMEM((BLOCK // 2, BLOCK // 2), F32)],
    )(diag.reshape(BLOCK, BLOCK))
    counts = counts.reshape(1, USERS_DEV)
    fetched, pred = call(
        place_kernel,
        (shape((SLOTS, BLOCK), BF16), shape((LIST, USERS_DEV), F32)),
        3,
        3 << 30,
        8 << 20,
    )(pos, came, user_rows)
    pred = pred + shift(pred, "core", 1)
    pred = [pred] + [shift(pred, "y", i) for i in range(1, 4)]
    times = (times[0] + times[1]) + (times[2] + times[3])
    times = exchange(times.reshape(8 * N_DIM, group, BLOCK), ("z",) + DIM)
    inner = call(
        inner_kernel,
        shape((LIST, LIST, USERS_DEV), F32),
        3,
        3 << 30,
        16 << 20,
        scratch=[
            pltpu.VMEM((SLOTS, 128), F32),
            pltpu.VMEM((LIST, LIST, USERS_DEV), F32),
        ],
    )(fetched, inverse, counts)
    times = times.reshape(8, USERS_DEV, BLOCK)
    return call(final_kernel, shape((USERS_DEV, BLOCK), F32), 10, 1 << 30, 4 << 20)(
        fetched, inverse, inner, counts, user_rows, times, *pred
    )


def solution(mesh):
    fine = Mesh(mesh.devices.reshape(4, 2, 4, 8), ("y", "core", "x", "z"))
    in_specs = (P(ROWS, DIM), P(ROWS, DIM), P(ROWS, None), P(ROWS), P())
    return jax.shard_map(
        body, mesh=fine, in_specs=in_specs, out_specs=P(ROWS, DIM), check_vma=False
    )
```

time: 238 us -> 206 us (0.87)
  local copies, waits for them, and re-layouts: 14.6 us -> 3.31 us
  Pallas kernels: 64.8 us -> 56.8 us
  other arithmetic: 6.35 us -> 0.93 us
  starting transfers between devices: 52.8 us -> 48.6 us
  blocking collectives: 29.8 us -> 27 us
    all_to_all x9 -> x4, waiting for transfers between devices: 65.2 us -> 18.2 us  [exchange(): return lax.all_to_all(x, axes, 0, 0, tiled=True)]
    ppermute x8 -> x17, waiting for transfers between devices: 0.02 us -> 46.8 us  [shift(): return lax.ppermute(x, axis, [(i, (i + by) % size) for i in range(size)])]
    all_to_all x9 -> x4, starting transfers between devices: 47.3 us -> 28.8 us  [exchange(): return lax.all_to_all(x, axes, 0, 0, tiled=True)]
    ppermute x8 -> x17, starting transfers between devices: 5.49 us -> 19.8 us  [shift(): return lax.ppermute(x, axis, [(i, (i + by) % size) for i in range(size)])]
    pallas_call x7, Pallas kernels: 64.8 us -> 56.8 us  [the longest x1 24.7 us: body(): call(inverse_kernel, shape((BLOCK, BLOCK), F32), 1, 4 << 30, 8 << 20, scr...]
    reduce_sum x3 -> x0, other arithmetic: 4.2 us -> none  [the longest x1 2.55 us: on_device(): times = exchange(jnp.sum(times, axis=0), 'z')]
    unnamed x18, local copies, waits for them, and re-layouts: 5.72 us -> 2.51 us
    all_to_all x2 -> x1, blocking collectives: 29.8 us -> 27 us  [exchange(): return lax.all_to_all(x, axes, 0, 0, tiled=True)]
  transfers between devices with their start and end apart: 17 -> 21, of which waited for: 7 -> 9; matrix products, arithmetic and copies ran while one was open for 6% -> 1% of each run, Pallas kernels for 23% -> 23%
where the time goes in v2:
time: 206 us; the launch traced here: 203 us
  waiting for transfers between devices  65 us (32%)
  Pallas kernels  56.8 us (28%)
  starting transfers between devices  48.6 us (24%)
  blocking collectives  27 us (13%)
  local copies, waits for them, and re-layouts  3.31 us (2%)
    ppermute x17, waiting for transfers between devices, shift(): return lax.ppermute(x, axis, [(i, (i + by) % size) for i in range(size)])  46.8 us
    all_to_all x4, starting transfers between devices, exchange(): return lax.all_to_all(x, axes, 0, 0, tiled=True)  28.8 us
    all_to_all x1, blocking collectives, exchange(): return lax.all_to_all(x, axes, 0, 0, tiled=True)  27 us
    pallas_call x1, Pallas kernels, body(): call(inverse_kernel, shape((BLOCK, BLOCK), F32), 1, 4 << 30, 8 << 20, scr...  24.7 us
    ppermute x17, starting transfers between devices, shift(): return lax.ppermute(x, axis, [(i, (i + by) % size) for i in range(size)])  19.8 us
    all_to_all x4, waiting for transfers between devices, exchange(): return lax.all_to_all(x, axes, 0, 0, tiled=True)  18.2 us
    pallas_call x1, Pallas kernels, body(): call(inner_kernel, shape((LIST, LIST, USERS_DEV), F32), 3, 3 << 30, 16 <<...  7.05 us
    pallas_call x1, Pallas kernels, body(): call(product_kernel, [shape((8, N_DIM, group, BLOCK), F32)] * 4, 5 + len(...  6.78 us
  transfers between devices with their start and end apart: 21, of which 9 were waited for; matrix products, arithmetic and copies ran while one was open for 1% of the time, Pallas kernels for 23%

profile of v2, /device:TPU:2, one launch (start us, length us, event | category | flops | bytes accessed | tf_op | source)
XLA Modules:
  0.0 203.5 jit_solution(2663390150773330450)
XLA Ops:
  0.0 1.6 convolution_bitcast_fusion.diag_ref
  1.6 5.1 %shard_map.55 = (s32[256,128]{1,0:T(8,128)S(1)}, f32[32,16,256]{2,1,0:T(8,128)S(1)}) custom-call(s32[32,64]{1,0:T(8,128)S(1)} %bitcast.32, s32[256,128]{1,0:T(8,128)S(1)} %bitcast.31, f32[32,8,256]{2,1,0:T(8,128)S(1)} %convolution_bitcast_fusion.diag_ref), custom_call_target="tpu_custom_call" | custom-call | flops 1073741824 | bytes 4194304 | tf_op jit(solution)/shard_map/pallas_call | solution.py:353
  6.7 0.0 copy-start.1
  6.8 27.0 %all_to_all.25.came_ref = f32[32,16,256]{2,1,0:T(8,128)S(1)} all-to-all(f32[32,16,256]{2,1,0:T(8,128)S(1)} %get-tuple-element.16), channel_id=1, replica_groups=mesh['y'=4,'core'=2,'x'=4,'z'=8] {'x','z'}, dimensions={0} | all-to-all | bytes 1048576 | tf_op jit(solution)/shard_map/all_to_all | solution.py:342
  33.8 0.7 broadcast_in_dim.8
  34.5 8.3 %all-to-all-start.3 = ((bf16[64,8,256]{2,1,0:T(8,128)(2,1)}), bf16[64,8,256]{2,1,0:T(8,128)(2,1)S(1)}, u32[]{:S(2)}, u32[]{:S(2)}) async-start(bf16[64,8,256]{2,1,0:T(8,128)(2,1)} %bitcast.16), calls=%async_computation.3 | async-start | bytes 524288 | tf_op jit(solution)/shard_map/all_to_all | solution.py:342
  42.8 2.5 %shard_map.56 = (bf16[2048,256]{1,0:T(8,128)(2,1)}, f32[32,8,256]{2,1,0:T(8,128)}) custom-call(f32[32,16,256]{2,1,0:T(8,128)S(1)} %all_to_all.25.came_ref, bf16[1024,256]{1,0:T(8,128)(2,1)S(1)} %copy-done), custom_call_target="tpu_custom_call" | custom-call | flops 1073741824 | bytes 4194304 | tf_op jit(solution)/shard_map/pallas_call | solution.py:359
  45.3 10.4 %all-to-all-done.3 = bf16[64,8,256]{2,1,0:T(8,128)(2,1)S(1)} async-done(((bf16[64,8,256]{2,1,0:T(8,128)(2,1)}), bf16[64,8,256]{2,1,0:T(8,128)(2,1)S(1)}, u32[]{:S(2)}, u32[]{:S(2)}) %all-to-all-start.3) | async-done | bytes 262176 | tf_op jit(solution)/shard_map/all_to_all | solution.py:342
  55.6 5.8 %all-to-all-start.2 = ((f32[32,8,256]{2,1,0:T(8,128)}), f32[32,8,256]{2,1,0:T(8,128)S(1)}, u32[]{:S(2)}, u32[]{:S(2)}) async-start(f32[32,8,256]{2,1,0:T(8,128)} %get-tuple-element.19), calls=%async_computation.2 | async-start | bytes 524288 | tf_op jit(solution)/shard_map/all_to_all | solution.py:342
  61.4 1.2 collective-permute-start.3
  62.6 0.9 collective-permute-start.4
  63.5 1.3 collective-permute-start.5
  64.8 7.8 %all-to-all-done.2 = f32[32,8,256]{2,1,0:T(8,128)S(1)} async-done(((f32[32,8,256]{2,1,0:T(8,128)}), f32[32,8,256]{2,1,0:T(8,128)S(1)}, u32[]{:S(2)}, u32[]{:S(2)}) %all-to-all-start.2) | async-done | bytes 262176 | tf_op jit(solution)/shard_map/all_to_all | solution.py:342
  72.6 5.6 %all-to-all-start.1 = ((bf16[32,64,256]{2,1,0:T(8,128)(2,1)}), bf16[32,64,256]{2,1,0:T(8,128)(2,1)S(1)}, u32[]{:S(2)}, u32[]{:S(2)}) async-start(bf16[32,64,256]{2,1,0:T(8,128)(2,1)} %bitcast.3), calls=%async_computation.1 | async-start | bytes 2097152 | tf_op jit(solution)/shard_map/all_to_all | solution.py:342
  78.2 0.1 collective-permute-start.6
  78.3 0.3 collective-permute-start
  78.7 0.0 collective-permute-done.3.refs_5_
  78.7 0.2 collective-permute-start.7
  78.8 8.7 %collective-permute-done.4.refs_6_ = bf16[1024,256]{1,0:T(8,128)(2,1)S(1)} collective-permute-done((bf16[1024,256]{1,0:T(8,128)(2,1)S(1)}, bf16[1024,256]{1,0:T(8,128)(2,1)S(1)}, u32[]{:S(2)}, u32[]{:S(2)}) %collective-permute-start.4) | collective-permute-done | bytes 524320 | tf_op jit(solution)/shard_map/ppermute | solution.py:329
  87.6 0.0 collective-permute-start.8
  87.6 0.0 collective-permute-done.5.refs_7_
  87.6 0.5 collective-permute-start.9
  88.1 0.0 collective-permute-done.6.refs_8_
  88.1 0.8 copy-done.2
  88.9 2.1 %collective-permute-start.1 = (bf16[8,8,8,256]{3,2,1,0:T(8,128)(2,1)S(1)}, bf16[8,8,8,256]{3,2,1,0:T(8,128)(2,1)}, u32[]{:S(2)}, u32[]{:S(2)}) collective-permute-start(bf16[8,8,8,256]{3,2,1,0:T(8,128)(2,1)S(1)} %bitcast.27), channel_id=1, source_target_pairs={{0,16},{8,24},{16,0},{24,8},{1,17},{9,25},{17,1},{25,9},{2,18},{10... | collective-permute-start | bytes 786440 | tf_op jit(solution)/shard_map/ppermute | solution.py:329
  91.0 0.2 collective-permute-done.refs_1_
  91.3 2.7 %collective-permute-start.2 = (bf16[8,8,8,256]{3,2,1,0:T(8,128)(2,1)S(1)}, bf16[8,8,8,256]{3,2,1,0:T(8,128)(2,1)}, u32[]{:S(2)}, u32[]{:S(2)}) collective-permute-start(bf16[8,8,8,256]{3,2,1,0:T(8,128)(2,1)S(1)} %bitcast.28), channel_id=1, source_target_pairs={{0,8},{8,16},{16,24},{24,0},{1,9},{9,17},{17,25},{25,1},{2,10},{10... | collective-permute-start | bytes 786440 | tf_op jit(solution)/shard_map/ppermute | solution.py:329
  94.0 0.1 stack.35.block_ref
  94.1 9.8 %collective-permute-done.1.refs_2_ = bf16[8,8,8,256]{3,2,1,0:T(8,128)(2,1)} collective-permute-done((bf16[8,8,8,256]{3,2,1,0:T(8,128)(2,1)S(1)}, bf16[8,8,8,256]{3,2,1,0:T(8,128)(2,1)}, u32[]{:S(2)}, u32[]{:S(2)}) %collective-permute-start.1) | collective-permute-done | bytes 262176 | tf_op jit(solution)/shard_map/ppermute | solution.py:329
  103.9 4.4 %collective-permute-done.2.refs_3_ = bf16[8,8,8,256]{3,2,1,0:T(8,128)(2,1)} collective-permute-done((bf16[8,8,8,256]{3,2,1,0:T(8,128)(2,1)S(1)}, bf16[8,8,8,256]{3,2,1,0:T(8,128)(2,1)}, u32[]{:S(2)}, u32[]{:S(2)}) %collective-permute-start.2) | collective-permute-done | bytes 262176 | tf_op jit(solution)/shard_map/ppermute | solution.py:329
  108.3 1.0 copy-done.3
  109.3 6.8 %shard_map.60 = (f32[8,8,8,256]{3,2,1,0:T(8,128)S(1)}, f32[8,8,8,256]{3,2,1,0:T(8,128)S(1)}, f32[8,8,8,256]{3,2,1,0:T(8,128)S(1)}, f32[8,8,8,256]{3,2,1,0:T(8,128)S(1)}) custom-call(s32[8]{0:T(128)S(1)} %stack.35.block_ref, bf16[8,8,8,256]{3,2,1,0:T(8,128)(2,1)S(1)} %bitcast.29, bf16[8,8,8,256]{3,2,1,0:T(8,128)(2,1)S(1)} %collective-permute-done.refs_1_, ...), custom_call_target="tpu_custom_call" | custom-call | flops 4294967296 | bytes 8388608 | tf_op jit(solution)/shard_map/pallas_call | solution.py:368
  116.1 1.5 collective-permute-start.10
  117.6 2.7 %collective-permute-start.11 = (f32[8,8,8,256]{3,2,1,0:T(8,128)S(1)}, f32[8,8,8,256]{3,2,1,0:T(8,128)S(1)}, u32[]{:S(2)}, u32[]{:S(2)}) collective-permute-start(f32[8,8,8,256]{3,2,1,0:T(8,128)S(1)} %get-tuple-element.22), channel_id=1, source_target_pairs={{0,16},{8,24},{16,0},{24,8},{1,17},{9,25},{17,1},{25,9},{2,18},{10... | collective-permute-start | bytes 1572872 | tf_op jit(solution)/shard_map/ppermute | solution.py:329
  120.3 10.7 %collective-permute-done.10 = f32[8,8,8,256]{3,2,1,0:T(8,128)S(1)} collective-permute-done((f32[8,8,8,256]{3,2,1,0:T(8,128)S(1)}, f32[8,8,8,256]{3,2,1,0:T(8,128)S(1)}, u32[]{:S(2)}, u32[]{:S(2)}) %collective-permute-start.10) | collective-permute-done | bytes 524320 | tf_op jit(solution)/shard_map/ppermute | solution.py:329
  131.0 3.0 %collective-permute-done.11 = f32[8,8,8,256]{3,2,1,0:T(8,128)S(1)} collective-permute-done((f32[8,8,8,256]{3,2,1,0:T(8,128)S(1)}, f32[8,8,8,256]{3,2,1,0:T(8,128)S(1)}, u32[]{:S(2)}, u32[]{:S(2)}) %collective-permute-start.11) | collective-permute-done | bytes 524320 | tf_op jit(solution)/shard_map/ppermute | solution.py:329
  134.0 10.0 %collective-permute-done.12 = f32[8,8,8,256]{3,2,1,0:T(8,128)S(1)} collective-permute-done((f32[8,8,8,256]{3,2,1,0:T(8,128)S(1)}, f32[8,8,8,256]{3,2,1,0:T(8,128)S(1)}, u32[]{:S(2)}, u32[]{:S(2)}) %collective-permute-start.12) | collective-permute-done | bytes 524320 | tf_op jit(solution)/shard_map/ppermute | solution.py:329
  143.9 0.9 add_add_fusion
  144.9 9.2 %all-to-all-start.4 = ((f32[64,8,256]{2,1,0:T(8,128)}), f32[64,8,256]{2,1,0:T(8,128)S(1)}, u32[]{:S(2)}, u32[]{:S(2)}) async-start(f32[64,8,256]{2,1,0:T(8,128)} %bitcast.18), calls=%async_computation.4 | async-start | bytes 1048576 | tf_op jit(solution)/shard_map/all_to_all | solution.py:342
  154.1 5.4 %shard_map.57 = (bf16[2048,256]{1,0:T(8,128)(2,1)S(1)}, f32[32,64]{1,0:T(8,128)S(1)}) custom-call(s32[256,128]{1,0:T(8,128)S(1)} %copy-done.8, bf16[2048,256]{1,0:T(8,128)(2,1)S(1)} %bitcast.23, bf16[64,256]{1,0:T(8,128)(2,1)S(1)} %copy-done.1), custom_call_target="tpu_custom_call" | custom-call | flops 3221225472 | bytes 8388608 | tf_op jit(solution)/shard_map/pallas_call | solution.py:390
  159.5 0.4 collective-permute-start.13
  159.8 24.7 %shard_map.58.inverse_ref = f32[256,256]{1,0:T(8,128)S(1)} custom-call(f32[256,256]{1,0:T(8,128)S(1)} %bitcast.25), custom_call_target="tpu_custom_call" | custom-call | flops 4294967296 | bytes 8388608 | tf_op jit(solution)/shard_map/pallas_call | solution.py:381
  184.6 1.7 collective-permute-start.14
  186.3 2.7 %collective-permute-start.15 = (f32[32,64]{1,0:T(8,128)S(1)}, f32[32,64]{1,0:T(8,128)S(1)}, u32[]{:S(2)}, u32[]{:S(2)}) collective-permute-start(f32[32,64]{1,0:T(8,128)S(1)} %add.104.refs_0_), channel_id=1, source_target_pairs={{0,128},{64,192},{128,0},{192,64},{1,129},{65,193},{129,1},{193,65... | collective-permute-start | bytes 24584 | tf_op jit(solution)/shard_map/ppermute | solution.py:329
  189.0 1.5 collective-permute-start.16
  190.4 0.7 copy-done.6
  191.1 7.0 %shard_map.59.inner_ref = f32[32,32,64]{2,1,0:T(8,128)S(1)} custom-call(bf16[2048,256]{1,0:T(8,128)(2,1)S(1)} %get-tuple-element.18.fetched_ref, f32[256,256]{1,0:T(8,128)S(1)} %shard_map.58.inverse_ref, s32[1,64]{1,0:T(1,128)S(1)} %bitcast.33), custom_call_target="tpu_custom_call" | custom-call | flops 3221225472 | bytes 16777216 | tf_op jit(solution)/shard_map/pallas_call | solution.py:401
  198.2 5.3 %shard_map.61 = f32[64,256]{1,0:T(8,128)} custom-call(bf16[2048,256]{1,0:T(8,128)(2,1)S(1)} %get-tuple-element.18.fetched_ref, f32[256,256]{1,0:T(8,128)S(1)} %shard_map.58.inverse_ref, f32[32,32,64]{2,1,0:T(8,128)S(1)} %shard_map.59.inner_ref, s32[1,64]{1,0:T(1,128)S(1)} %bitcast.34, bf16[64,256]{1,0:T(8,128)(2,1)S(1)} %copy-done.1, ...), custom_call_target="tpu_custom_call" | custom-call | flops 1073741824 | bytes 4194304 | tf_op jit(solution)/shard_map/pallas_call | solution.py:413
  (25 shorter events, 0.1 us)
Async XLA Ops:
  0.0 1.6 copy-start.5
  0.0 1.6 copy-start.4
  6.7 27.0 %copy-start.7 = (s32[256,128]{1,0:T(8,128)}, s32[256,128]{1,0:T(8,128)S(1)}, u32[]{:S(2)}) copy-start(s32[256,128]{1,0:T(8,128)S(1)} %get-tuple-element.15.pos_ref) | copy-start | bytes 393220
  6.7 27.0 %copy-start.1 = (bf16[64,256]{1,0:T(8,128)(2,1)S(1)}, bf16[64,256]{1,0:T(8,128)(2,1)}, u32[]{:S(2)}) copy-start(bf16[64,256]{1,0:T(8,128)(2,1)} %users_ref.3) | copy-start | bytes 98308
  33.8 9.0 %copy-start = (bf16[1024,256]{1,0:T(8,128)(2,1)S(1)}, bf16[1024,256]{1,0:T(8,128)(2,1)}, u32[]{:S(2)}) copy-start(bf16[1024,256]{1,0:T(8,128)(2,1)} %refs_4_.1) | copy-start | bytes 1572868
  34.5 21.2 %all-to-all-start.3 = ((bf16[64,8,256]{2,1,0:T(8,128)(2,1)}), bf16[64,8,256]{2,1,0:T(8,128)(2,1)S(1)}, u32[]{:S(2)}, u32[]{:S(2)}) async-start(bf16[64,8,256]{2,1,0:T(8,128)(2,1)} %bitcast.16), calls=%async_computation.3 | async-start | bytes 524288 | tf_op jit(solution)/shard_map/all_to_all | solution.py:342
  55.6 17.0 %all-to-all-start.2 = ((f32[32,8,256]{2,1,0:T(8,128)}), f32[32,8,256]{2,1,0:T(8,128)S(1)}, u32[]{:S(2)}, u32[]{:S(2)}) async-start(f32[32,8,256]{2,1,0:T(8,128)} %get-tuple-element.19), calls=%async_computation.2 | async-start | bytes 524288 | tf_op jit(solution)/shard_map/all_to_all | solution.py:342
  61.4 17.3 %collective-permute-start.3 = (bf16[1024,256]{1,0:T(8,128)(2,1)S(1)}, bf16[1024,256]{1,0:T(8,128)(2,1)S(1)}, u32[]{:S(2)}, u32[]{:S(2)}) collective-permute-start(bf16[1024,256]{1,0:T(8,128)(2,1)S(1)} %copy-done), channel_id=1, source_target_pairs={{0,192},{64,0},{128,64},{192,128},{1,193},{65,1},{129,65},{193,129... | collective-permute-start | bytes 1572872 | tf_op jit(solution)/shard_map/ppermute | solution.py:329
  62.6 25.0 %collective-permute-start.4 = (bf16[1024,256]{1,0:T(8,128)(2,1)S(1)}, bf16[1024,256]{1,0:T(8,128)(2,1)S(1)}, u32[]{:S(2)}, u32[]{:S(2)}) collective-permute-start(bf16[1024,256]{1,0:T(8,128)(2,1)S(1)} %copy-done), channel_id=1, source_target_pairs={{0,64},{64,128},{128,192},{192,0},{1,65},{65,129},{129,193},{193,1... | collective-permute-start | bytes 1572872 | tf_op jit(solution)/shard_map/ppermute | solution.py:329
  63.5 24.1 %collective-permute-start.5 = (bf16[1024,256]{1,0:T(8,128)(2,1)S(1)}, bf16[1024,256]{1,0:T(8,128)(2,1)}, u32[]{:S(2)}, u32[]{:S(2)}) collective-permute-start(bf16[1024,256]{1,0:T(8,128)(2,1)S(1)} %copy-done), channel_id=1, source_target_pairs={{0,128},{64,192},{128,0},{192,64},{1,129},{65,193},{129,1},{193,65... | collective-permute-start | bytes 1572872 | tf_op jit(solution)/shard_map/ppermute | solution.py:329
  72.6 72.2 %all-to-all-start.1 = ((bf16[32,64,256]{2,1,0:T(8,128)(2,1)}), bf16[32,64,256]{2,1,0:T(8,128)(2,1)S(1)}, u32[]{:S(2)}, u32[]{:S(2)}) async-start(bf16[32,64,256]{2,1,0:T(8,128)(2,1)} %bitcast.3), calls=%async_computation.1 | async-start | bytes 2097152 | tf_op jit(solution)/shard_map/all_to_all | solution.py:342
  78.2 9.9 %collective-permute-start.6 = (bf16[1024,256]{1,0:T(8,128)(2,1)S(1)}, bf16[1024,256]{1,0:T(8,128)(2,1)S(1)}, u32[]{:S(2)}, u32[]{:S(2)}) collective-permute-start(bf16[1024,256]{1,0:T(8,128)(2,1)S(1)} %copy-done), channel_id=1, source_target_pairs={{0,32},{32,0},{1,33},{33,1},{2,34},{34,2},{3,35},{35,3},{4,36},{36... | collective-permute-start | bytes 1572872 | tf_op jit(solution)/shard_map/ppermute | solution.py:329
  78.3 12.9 %collective-permute-start = (bf16[8,8,8,256]{3,2,1,0:T(8,128)(2,1)S(1)}, bf16[8,8,8,256]{3,2,1,0:T(8,128)(2,1)S(1)}, u32[]{:S(2)}, u32[]{:S(2)}) collective-permute-start(bf16[8,8,8,256]{3,2,1,0:T(8,128)(2,1)S(1)} %bitcast.26), channel_id=1, source_target_pairs={{0,24},{8,0},{16,8},{24,16},{1,25},{9,1},{17,9},{25,17},{2,26},{10... | collective-permute-start | bytes 786440 | tf_op jit(solution)/shard_map/ppermute | solution.py:329
  78.7 29.6 %collective-permute-start.7 = (bf16[1024,256]{1,0:T(8,128)(2,1)S(1)}, bf16[1024,256]{1,0:T(8,128)(2,1)}, u32[]{:S(2)}, u32[]{:S(2)}) collective-permute-start(bf16[1024,256]{1,0:T(8,128)(2,1)S(1)} %collective-permute-done.3.refs_5_), channel_id=1, source_target_pairs={{0,32},{32,0},{1,33},{33,1},{2,34},{34,2},{3,35},{35,3},{4,36},{36... | collective-permute-start | bytes 1572872 | tf_op jit(solution)/shard_map/ppermute | solution.py:329
  87.6 20.7 %collective-permute-start.8 = (bf16[1024,256]{1,0:T(8,128)(2,1)S(1)}, bf16[1024,256]{1,0:T(8,128)(2,1)}, u32[]{:S(2)}, u32[]{:S(2)}) collective-permute-start(bf16[1024,256]{1,0:T(8,128)(2,1)S(1)} %collective-permute-done.4.refs_6_), channel_id=1, source_target_pairs={{0,32},{32,0},{1,33},{33,1},{2,34},{34,2},{3,35},{35,3},{4,36},{36... | collective-permute-start | bytes 1572872 | tf_op jit(solution)/shard_map/ppermute | solution.py:329
  87.6 20.7 %collective-permute-start.9 = (bf16[1024,256]{1,0:T(8,128)(2,1)}, bf16[1024,256]{1,0:T(8,128)(2,1)}, u32[]{:S(2)}, u32[]{:S(2)}) collective-permute-start(bf16[1024,256]{1,0:T(8,128)(2,1)} %collective-permute-done.5.refs_7_), channel_id=1, source_target_pairs={{0,32},{32,0},{1,33},{33,1},{2,34},{34,2},{3,35},{35,3},{4,36},{36... | collective-permute-start | bytes 1572872 | tf_op jit(solution)/shard_map/ppermute | solution.py:329
  88.1 0.8 copy-start.2
  88.9 14.9 %collective-permute-start.1 = (bf16[8,8,8,256]{3,2,1,0:T(8,128)(2,1)S(1)}, bf16[8,8,8,256]{3,2,1,0:T(8,128)(2,1)}, u32[]{:S(2)}, u32[]{:S(2)}) collective-permute-start(bf16[8,8,8,256]{3,2,1,0:T(8,128)(2,1)S(1)} %bitcast.27), channel_id=1, source_target_pairs={{0,16},{8,24},{16,0},{24,8},{1,17},{9,25},{17,1},{25,9},{2,18},{10... | collective-permute-start | bytes 786440 | tf_op jit(solution)/shard_map/ppermute | solution.py:329
  91.3 17.0 %collective-permute-start.2 = (bf16[8,8,8,256]{3,2,1,0:T(8,128)(2,1)S(1)}, bf16[8,8,8,256]{3,2,1,0:T(8,128)(2,1)}, u32[]{:S(2)}, u32[]{:S(2)}) collective-permute-start(bf16[8,8,8,256]{3,2,1,0:T(8,128)(2,1)S(1)} %bitcast.28), channel_id=1, source_target_pairs={{0,8},{8,16},{16,24},{24,0},{1,9},{9,17},{17,25},{25,1},{2,10},{10... | collective-permute-start | bytes 786440 | tf_op jit(solution)/shard_map/ppermute | solution.py:329
  108.3 1.0 copy-start.3
  116.1 14.9 %collective-permute-start.10 = (f32[8,8,8,256]{3,2,1,0:T(8,128)S(1)}, f32[8,8,8,256]{3,2,1,0:T(8,128)S(1)}, u32[]{:S(2)}, u32[]{:S(2)}) collective-permute-start(f32[8,8,8,256]{3,2,1,0:T(8,128)S(1)} %get-tuple-element.21), channel_id=1, source_target_pairs={{0,8},{8,16},{16,24},{24,0},{1,9},{9,17},{17,25},{25,1},{2,10},{10... | collective-permute-start | bytes 1572872 | tf_op jit(solution)/shard_map/ppermute | solution.py:329
  117.6 16.3 %collective-permute-start.11 = (f32[8,8,8,256]{3,2,1,0:T(8,128)S(1)}, f32[8,8,8,256]{3,2,1,0:T(8,128)S(1)}, u32[]{:S(2)}, u32[]{:S(2)}) collective-permute-start(f32[8,8,8,256]{3,2,1,0:T(8,128)S(1)} %get-tuple-element.22), channel_id=1, source_target_pairs={{0,16},{8,24},{16,0},{24,8},{1,17},{9,25},{17,1},{25,9},{2,18},{10... | collective-permute-start | bytes 1572872 | tf_op jit(solution)/shard_map/ppermute | solution.py:329
  120.3 23.6 %collective-permute-start.12 = (f32[8,8,8,256]{3,2,1,0:T(8,128)S(1)}, f32[8,8,8,256]{3,2,1,0:T(8,128)S(1)}, u32[]{:S(2)}, u32[]{:S(2)}) collective-permute-start(f32[8,8,8,256]{3,2,1,0:T(8,128)S(1)} %get-tuple-element.23), channel_id=1, source_target_pairs={{0,24},{8,0},{16,8},{24,16},{1,25},{9,1},{17,9},{25,17},{2,26},{10... | collective-permute-start | bytes 1572872 | tf_op jit(solution)/shard_map/ppermute | solution.py:329
  144.9 9.2 %copy-start.8 = (s32[256,128]{1,0:T(8,128)S(1)}, s32[256,128]{1,0:T(8,128)}, u32[]{:S(2)}) copy-start(s32[256,128]{1,0:T(8,128)} %copy-done.7) | copy-start | bytes 393220
  144.9 53.3 %all-to-all-start.4 = ((f32[64,8,256]{2,1,0:T(8,128)}), f32[64,8,256]{2,1,0:T(8,128)S(1)}, u32[]{:S(2)}, u32[]{:S(2)}) async-start(f32[64,8,256]{2,1,0:T(8,128)} %bitcast.18), calls=%async_computation.4 | async-start | bytes 1048576 | tf_op jit(solution)/shard_map/all_to_all | solution.py:342
  159.5 25.1 %collective-permute-start.13 = (f32[32,64]{1,0:T(8,128)S(1)}, f32[32,64]{1,0:T(8,128)S(1)}, u32[]{:S(2)}, u32[]{:S(2)}) collective-permute-start(f32[32,64]{1,0:T(8,128)S(1)} %get-tuple-element.24), channel_id=1, source_target_pairs={{0,32},{32,0},{1,33},{33,1},{2,34},{34,2},{3,35},{35,3},{4,36},{36... | collective-permute-start | bytes 24584 | tf_op jit(solution)/shard_map/ppermute | solution.py:329
  184.6 13.6 %collective-permute-start.14 = (f32[32,64]{1,0:T(8,128)S(1)}, f32[32,64]{1,0:T(8,128)S(1)}, u32[]{:S(2)}, u32[]{:S(2)}) collective-permute-start(f32[32,64]{1,0:T(8,128)S(1)} %add.104.refs_0_), channel_id=1, source_target_pairs={{0,64},{64,128},{128,192},{192,0},{1,65},{65,129},{129,193},{193,1... | collective-permute-start | bytes 24584 | tf_op jit(solution)/shard_map/ppermute | solution.py:329
  186.3 11.9 %collective-permute-start.15 = (f32[32,64]{1,0:T(8,128)S(1)}, f32[32,64]{1,0:T(8,128)S(1)}, u32[]{:S(2)}, u32[]{:S(2)}) collective-permute-start(f32[32,64]{1,0:T(8,128)S(1)} %add.104.refs_0_), channel_id=1, source_target_pairs={{0,128},{64,192},{128,0},{192,64},{1,129},{65,193},{129,1},{193,65... | collective-permute-start | bytes 24584 | tf_op jit(solution)/shard_map/ppermute | solution.py:329
  189.0 9.2 %collective-permute-start.16 = (f32[32,64]{1,0:T(8,128)S(1)}, f32[32,64]{1,0:T(8,128)S(1)}, u32[]{:S(2)}, u32[]{:S(2)}) collective-permute-start(f32[32,64]{1,0:T(8,128)S(1)} %add.104.refs_0_), channel_id=1, source_target_pairs={{0,192},{64,0},{128,64},{192,128},{1,193},{65,1},{129,65},{193,129... | collective-permute-start | bytes 24584 | tf_op jit(solution)/shard_map/ppermute | solution.py:329
  190.4 0.7 copy-start.6

commit v3 on v2

--- a/solution.py
+++ b/solution.py
@@ -104,18 +104,18 @@
         asked = asked + dot(low.astype(BF16), ranked, 0, 0)
     pos_ref[...] = places
     sent_ref[...] = jnp.zeros(sent_ref.shape, F32)
-    sent_ref[:, :8, :] = diag_ref[...]
+    sent_ref[:, :, :BLOCK] = diag_ref[...]
     for k in range(N_ROWS):
-        sent_ref[k, 8:9, :128] = asked[k : k + 1, :]
+        sent_ref[k, 0:1, BLOCK:] = asked[k : k + 1, :]
 
 
 def pick_kernel(came_ref, table_ref, rows_ref, diag_ref):
     table = table_ref[...]
-    diag = came_ref[0, :8, :]
+    diag = came_ref[0, :, :BLOCK]
     for r in range(1, N_ROWS):
-        diag = diag + came_ref[r, :8, :]
+        diag = diag + came_ref[r, :, :BLOCK]
     diag_ref[...] = jnp.broadcast_to(diag[None], diag_ref.shape)
-    asked = jnp.concatenate([came_ref[r, 8:9, :128] for r in range(N_ROWS)], axis=0)
+    asked = jnp.concatenate([came_ref[r, 0:1, BLOCK:] for r in range(N_ROWS)], axis=0)
     asked = jnp.transpose(asked).astype(I32)
     asked = asked[:PER, :]
     for c in range(CHUNKS):
@@ -163,71 +163,43 @@
             out_ref[:, block_ref[i]] = part.reshape(8, quarter // 8, BLOCK)
 
 
-def sweep(work):
-    size = 128
-    lane = iota((8, size), 1)
-    wide = iota((size, size), 1)
-
-    def at_lane(row, k):
-        return jnp.take_along_axis(row, jnp.full((8, size), k, I32), axis=1)
-
-    def load(k):
-        return jnp.broadcast_to(work[pl.ds(k, 1), :], (8, size))
-
-    def column(row):
-        return jnp.transpose(jnp.broadcast_to(row[:1], (size, size)))
-
-    def step(n, rows):
-        row0, raw1 = rows
-        k = 2 * n
-        after = jnp.minimum(k + 2, size - 2)
-        old2 = load(after)
-        old3 = load(after + 1)
-        inv0 = 1.0 / at_lane(row0, k)
-        c01 = at_lane(row0, k + 1)
-        a2, a3 = at_lane(row0, after), at_lane(row0, after + 1)
-        b2, b3 = at_lane(raw1, after), at_lane(raw1, after + 1)
-        low = c01 * inv0
-        inv1 = 1.0 / (at_lane(raw1, k + 1) - c01 * low)
-        w0 = row0 * inv0
-        row1 = jnp.where(lane == k, low, raw1 - c01 * w0)
-        w1 = row1 * inv1
-        b2 = b2 - low * a2
-        b3 = b3 - low * a3
-
-        def advance(old, a, b):
-            once = jnp.where(lane == k, a * inv0, old - a * w0)
-            return jnp.where(lane == k + 1, b * inv1, once - b * w1)
-
-        next0 = advance(old2, a2, b2)
-        next1 = advance(old3, a3, b3)
-        col0, col1 = column(row0), column(row1)
-        new = jnp.where(wide == k, col0 * inv0[:1], work[...] - col0 * w0[:1])
-        work[...] = jnp.where(wide == k + 1, col1 * inv1[:1], new - col1 * w1[:1])
-        done0 = jnp.where(lane == k, -inv0, w0)
-        done0 = jnp.where(lane == k + 1, low * inv1, done0 - low * w1)
-        work[pl.ds(k, 1), :] = done0[:1]
-        work[pl.ds(k + 1, 1), :] = jnp.where(lane == k + 1, -inv1, w1)[:1]
-        return next0, next1
-
-    lax.fori_loop(0, size // 2, step, (load(0), load(1)))
-    return -work[...]
-
-
-def inverse_kernel(diag_ref, out_ref, work):
+def sweep(start):
+    size, group = 128, 4
+    lane = iota((size, size), 1)
+    sub = iota((size, size), 0)
+    row_lane = iota((1, size), 1)
+
+    def eight(n, a):
+        for k0 in range(0, 8, group):
+            cols = [jnp.broadcast_to(a[:, k : k + 1], (size, size)) for k in range(k0, k0 + group)]
+            rows = [a[k : k + 1, :] for k in range(k0, k0 + group)]
+            for j in range(group):
+                k = k0 + j
+                inv = 1.0 / cols[j][k : k + 1, :]
+                scaled = rows[j] * inv
+                for m in range(j + 1, group):
+                    low = cols[m][k : k + 1, :] * inv
+                    factor = cols[j][k0 + m : k0 + m + 1, :]
+                    cols[m] = jnp.where(sub == k, low, cols[m] - cols[j] * low)
+                    rows[m] = jnp.where(row_lane == k, factor * inv, rows[m] - factor * scaled)
+                a = jnp.where(lane == k, cols[j] * inv, a - cols[j] * scaled)
+                a = jnp.where(sub == k, jnp.where(row_lane == k, -inv, scaled), a)
+        a = pltpu.roll(a, size - 8, 1)
+        return jnp.concatenate([a[8:], a[:8]], axis=0)
+
+    return -lax.fori_loop(0, size // 8, eight, start)
+
+
+def inverse_kernel(diag_ref, out_ref):
     half = BLOCK // 2
     eye = jnp.where(iota((half, half), 0) == iota((half, half), 1), 1.0, 0.0)
-    upper = WEIGHT * diag_ref[:half, half:]
-    work[...] = WEIGHT * diag_ref[:half, :half] + eye
-    lead = sweep(work)
-    lead_split = split(lead)
-    upper_split = split(upper)
-    mixed = dot_split(lead_split, upper_split)
-    mixed_split = split(mixed)
-    work[...] = WEIGHT * diag_ref[half:, half:] + eye - dot_split(upper_split, mixed_split, 0, 0)
-    rest = sweep(work)
-    cross = dot_split(mixed_split, split(rest))
-    out_ref[:half, :half] = lead + dot_split(split(cross), mixed_split, 1, 1)
+    upper = split(WEIGHT * diag_ref[:half, half:])
+    lead = sweep(WEIGHT * diag_ref[:half, :half] + eye)
+    mixed = split(dot_split(split(lead), upper))
+    rest = WEIGHT * diag_ref[half:, half:] + eye - dot_split(upper, mixed, 0, 0)
+    rest = sweep(rest)
+    cross = dot_split(mixed, split(rest))
+    out_ref[:half, :half] = lead + dot_split(split(cross), mixed, 1, 1)
     out_ref[:half, half:] = -cross
     out_ref[half:, :half] = -jnp.transpose(cross)
     out_ref[half:, half:] = rest
@@ -249,7 +221,7 @@
         folded[part, :] = both + pltpu.roll(both, 32, 1)
         return carry
 
-    lax.fori_loop(0, CHUNKS, chunk, 0, unroll=2)
+    lax.fori_loop(0, CHUNKS, chunk, 0, unroll=4)
     slot = iota((LIST, USERS_DEV), 0)
     live = jnp.where(slot < counts_ref[...], 1.0, 0.0)
     for a in range(LIST):
@@ -330,7 +302,8 @@
 
 
 def gather_dims(table):
-    tables = [table] + [shift(table, "y", 4 - i) for i in (1, 3, 2)]
+    tables = [table] + [shift(table, "y", 4 - i) for i in (1, 3)]
+    tables = tables + [shift(table, "y", 2)]
     tables = tables + [shift(t, "core", 1) for t in tables]
     y = lax.axis_index("y")
     core = lax.axis_index("core")
@@ -351,7 +324,7 @@
     tables, blocks = gather_dims(item_table)
     diag = dot(item_table, item_table, 0, 0).reshape(N_ROWS, slice_rows, BLOCK)
     pos, sent = call(
-        index_kernel, (shape((CHUNK, 128), I32), shape((N_ROWS, 16, BLOCK), F32)), 3, 1 << 30, 4 << 20
+        index_kernel, (shape((CHUNK, 128), I32), shape((N_ROWS, 8, BLOCK + 128), F32)), 3, 1 << 30, 4 << 20
     )(observed_items.T, item_row.reshape(256, 128), diag)
     came = exchange(sent, ROWS)
     users = users.reshape(8, N_DIM, group, BLOCK)
@@ -377,14 +350,10 @@
         ],
         in_specs=[SMEM] + [VMEM] * 4 + [pl.BlockSpec(memory_space=pl.ANY)] * N_DIM,
     )(blocks, *users, *tables)
-    times = [times[0]] + [shift(times[i], "x", i) for i in range(1, 4)]
+    far = shift(times[2], "x", 2)
+    times = [times[0], far] + [shift(times[i], "x", i) for i in (1, 3)]
     inverse = call(
-        inverse_kernel,
-        shape((BLOCK, BLOCK), F32),
-        1,
-        4 << 30,
-        8 << 20,
-        scratch=[pltpu.VMEM((BLOCK // 2, BLOCK // 2), F32)],
+        inverse_kernel, shape((BLOCK, BLOCK), F32), 1, 4 << 30, 8 << 20
     )(diag.reshape(BLOCK, BLOCK))
     counts = counts.reshape(1, USERS_DEV)
     fetched, pred = call(

time: 206 us -> 191 us (0.927)
  Pallas kernels: 56.8 us -> 45.1 us
  blocking collectives: 27 us -> 24.8 us
    pallas_call x2, Pallas kernels: 29.8 us -> 19.2 us  [the longest x1 14.1 us: body(): call(inverse_kernel, shape((BLOCK, BLOCK), F32), 1, 4 << 30, 8 << 20)]
    all_to_all x1, blocking collectives: 27 us -> 24.8 us  [exchange(): return lax.all_to_all(x, axes, 0, 0, tiled=True)]
  transfers between devices with their start and end apart: 21 -> 21, of which waited for: 9 -> 8; matrix products, arithmetic and copies ran while one was open for 1% -> 1% of each run, Pallas kernels for 23% -> 19%
where the time goes in v3:
time: 191 us; the launch traced here: 187 us
  waiting for transfers between devices  64.5 us (34%)
  starting transfers between devices  47.1 us (25%)
  Pallas kernels  45.1 us (24%)
  blocking collectives  24.8 us (13%)
  local copies, waits for them, and re-layouts  3.31 us (2%)
    ppermute x17, waiting for transfers between devices, shift(): return lax.ppermute(x, axis, [(i, (i + by) % size) for i in range(size)])  46.3 us
    all_to_all x4, starting transfers between devices, exchange(): return lax.all_to_all(x, axes, 0, 0, tiled=True)  27.9 us
    all_to_all x1, blocking collectives, exchange(): return lax.all_to_all(x, axes, 0, 0, tiled=True)  24.8 us
    ppermute x17, starting transfers between devices, shift(): return lax.ppermute(x, axis, [(i, (i + by) % size) for i in range(size)])  19.2 us
    all_to_all x4, waiting for transfers between devices, exchange(): return lax.all_to_all(x, axes, 0, 0, tiled=True)  18.2 us
    pallas_call x1, Pallas kernels, body(): call(inverse_kernel, shape((BLOCK, BLOCK), F32), 1, 4 << 30, 8 << 20)  14.1 us
    pallas_call x1, Pallas kernels, body(): call(product_kernel, [shape((8, N_DIM, group, BLOCK), F32)] * 4, 5 + len(...  6.79 us
    pallas_call x1, Pallas kernels, body(): call(inner_kernel, shape((LIST, LIST, USERS_DEV), F32), 3, 3 << 30, 16 <<...  5.96 us
  transfers between devices with their start and end apart: 21, of which 8 were waited for; matrix products, arithmetic and copies ran while one was open for 1% of the time, Pallas kernels for 19%

profile of v3, /device:TPU:2, one launch (start us, length us, event | category | flops | bytes accessed | tf_op | source)
XLA Modules:
  0.0 187.5 jit_solution(4413669556715565325)
XLA Ops:
  0.0 1.6 convolution_bitcast_fusion.diag_ref
  1.6 5.1 %shard_map.55 = (s32[256,128]{1,0:T(8,128)S(1)}, f32[32,8,384]{2,1,0:T(8,128)S(1)}) custom-call(s32[32,64]{1,0:T(8,128)S(1)} %bitcast.32, s32[256,128]{1,0:T(8,128)S(1)} %bitcast.31, f32[32,8,256]{2,1,0:T(8,128)S(1)} %convolution_bitcast_fusion.diag_ref), custom_call_target="tpu_custom_call" | custom-call | flops 1073741824 | bytes 4194304 | tf_op jit(solution)/shard_map/pallas_call | solution.py:326
  6.7 0.0 copy-start.1
  6.7 24.8 %all_to_all.25.came_ref = f32[32,8,384]{2,1,0:T(8,128)S(1)} all-to-all(f32[32,8,384]{2,1,0:T(8,128)S(1)} %get-tuple-element.16), channel_id=1, replica_groups=mesh['y'=4,'core'=2,'x'=4,'z'=8] {'x','z'}, dimensions={0} | all-to-all | bytes 786432 | tf_op jit(solution)/shard_map/all_to_all | solution.py:315
  31.5 0.7 broadcast_in_dim.8
  32.3 7.7 %all-to-all-start.3 = ((bf16[64,8,256]{2,1,0:T(8,128)(2,1)}), bf16[64,8,256]{2,1,0:T(8,128)(2,1)S(1)}, u32[]{:S(2)}, u32[]{:S(2)}) async-start(bf16[64,8,256]{2,1,0:T(8,128)(2,1)} %bitcast.16), calls=%async_computation.3 | async-start | bytes 524288 | tf_op jit(solution)/shard_map/all_to_all | solution.py:315
  39.9 2.5 %shard_map.56 = (bf16[2048,256]{1,0:T(8,128)(2,1)}, f32[32,8,256]{2,1,0:T(8,128)}) custom-call(f32[32,8,384]{2,1,0:T(8,128)S(1)} %all_to_all.25.came_ref, bf16[1024,256]{1,0:T(8,128)(2,1)S(1)} %copy-done), custom_call_target="tpu_custom_call" | custom-call | flops 1073741824 | bytes 4194304 | tf_op jit(solution)/shard_map/pallas_call | solution.py:332
  42.4 10.4 %all-to-all-done.3 = bf16[64,8,256]{2,1,0:T(8,128)(2,1)S(1)} async-done(((bf16[64,8,256]{2,1,0:T(8,128)(2,1)}), bf16[64,8,256]{2,1,0:T(8,128)(2,1)S(1)}, u32[]{:S(2)}, u32[]{:S(2)}) %all-to-all-start.3) | async-done | bytes 262176 | tf_op jit(solution)/shard_map/all_to_all | solution.py:315
  52.8 5.7 %all-to-all-start.2 = ((f32[32,8,256]{2,1,0:T(8,128)}), f32[32,8,256]{2,1,0:T(8,128)S(1)}, u32[]{:S(2)}, u32[]{:S(2)}) async-start(f32[32,8,256]{2,1,0:T(8,128)} %get-tuple-element.19), calls=%async_computation.2 | async-start | bytes 524288 | tf_op jit(solution)/shard_map/all_to_all | solution.py:315
  58.6 1.2 collective-permute-start.3
  59.8 0.9 collective-permute-start.4
  60.7 1.3 collective-permute-start.5
  62.0 7.8 %all-to-all-done.2 = f32[32,8,256]{2,1,0:T(8,128)S(1)} async-done(((f32[32,8,256]{2,1,0:T(8,128)}), f32[32,8,256]{2,1,0:T(8,128)S(1)}, u32[]{:S(2)}, u32[]{:S(2)}) %all-to-all-start.2) | async-done | bytes 262176 | tf_op jit(solution)/shard_map/all_to_all | solution.py:315
  69.8 5.6 %all-to-all-start.1 = ((bf16[32,64,256]{2,1,0:T(8,128)(2,1)}), bf16[32,64,256]{2,1,0:T(8,128)(2,1)S(1)}, u32[]{:S(2)}, u32[]{:S(2)}) async-start(bf16[32,64,256]{2,1,0:T(8,128)(2,1)} %bitcast.3), calls=%async_computation.1 | async-start | bytes 2097152 | tf_op jit(solution)/shard_map/all_to_all | solution.py:315
  75.4 0.1 collective-permute-start.6
  75.5 0.3 collective-permute-start
  75.8 0.0 collective-permute-done.3.refs_5_
  75.8 0.2 collective-permute-start.7
  76.0 8.7 %collective-permute-done.4.refs_6_ = bf16[1024,256]{1,0:T(8,128)(2,1)S(1)} collective-permute-done((bf16[1024,256]{1,0:T(8,128)(2,1)S(1)}, bf16[1024,256]{1,0:T(8,128)(2,1)S(1)}, u32[]{:S(2)}, u32[]{:S(2)}) %collective-permute-start.4) | collective-permute-done | bytes 524320 | tf_op jit(solution)/shard_map/ppermute | solution.py:301
  84.8 0.0 collective-permute-start.8
  84.8 0.5 collective-permute-start.9
  85.3 0.8 copy-done.2
  86.1 2.1 %collective-permute-start.1 = (bf16[8,8,8,256]{3,2,1,0:T(8,128)(2,1)S(1)}, bf16[8,8,8,256]{3,2,1,0:T(8,128)(2,1)}, u32[]{:S(2)}, u32[]{:S(2)}) collective-permute-start(bf16[8,8,8,256]{3,2,1,0:T(8,128)(2,1)S(1)} %bitcast.27), channel_id=1, source_target_pairs={{0,16},{8,24},{16,0},{24,8},{1,17},{9,25},{17,1},{25,9},{2,18},{10... | collective-permute-start | bytes 786440 | tf_op jit(solution)/shard_map/ppermute | solution.py:301
  88.2 0.2 collective-permute-done.refs_1_
  88.4 2.8 %collective-permute-start.2 = (bf16[8,8,8,256]{3,2,1,0:T(8,128)(2,1)S(1)}, bf16[8,8,8,256]{3,2,1,0:T(8,128)(2,1)}, u32[]{:S(2)}, u32[]{:S(2)}) collective-permute-start(bf16[8,8,8,256]{3,2,1,0:T(8,128)(2,1)S(1)} %bitcast.28), channel_id=1, source_target_pairs={{0,8},{8,16},{16,24},{24,0},{1,9},{9,17},{17,25},{25,1},{2,10},{10... | collective-permute-start | bytes 786440 | tf_op jit(solution)/shard_map/ppermute | solution.py:301
  91.2 0.1 stack.35.block_ref
  91.3 9.8 %collective-permute-done.1.refs_2_ = bf16[8,8,8,256]{3,2,1,0:T(8,128)(2,1)} collective-permute-done((bf16[8,8,8,256]{3,2,1,0:T(8,128)(2,1)S(1)}, bf16[8,8,8,256]{3,2,1,0:T(8,128)(2,1)}, u32[]{:S(2)}, u32[]{:S(2)}) %collective-permute-start.1) | collective-permute-done | bytes 262176 | tf_op jit(solution)/shard_map/ppermute | solution.py:301
  101.0 4.4 %collective-permute-done.2.refs_3_ = bf16[8,8,8,256]{3,2,1,0:T(8,128)(2,1)} collective-permute-done((bf16[8,8,8,256]{3,2,1,0:T(8,128)(2,1)S(1)}, bf16[8,8,8,256]{3,2,1,0:T(8,128)(2,1)}, u32[]{:S(2)}, u32[]{:S(2)}) %collective-permute-start.2) | collective-permute-done | bytes 262176 | tf_op jit(solution)/shard_map/ppermute | solution.py:301
  105.5 0.0 collective-permute-done.7.refs_9_
  105.5 0.0 collective-permute-done.8.refs_10_
  105.5 0.0 collective-permute-done.9.refs_11_
  105.5 1.0 copy-done.3
  106.5 6.8 %shard_map.60 = (f32[8,8,8,256]{3,2,1,0:T(8,128)S(1)}, f32[8,8,8,256]{3,2,1,0:T(8,128)S(1)}, f32[8,8,8,256]{3,2,1,0:T(8,128)S(1)}, f32[8,8,8,256]{3,2,1,0:T(8,128)S(1)}) custom-call(s32[8]{0:T(128)S(1)} %stack.35.block_ref, bf16[8,8,8,256]{3,2,1,0:T(8,128)(2,1)S(1)} %bitcast.29, bf16[8,8,8,256]{3,2,1,0:T(8,128)(2,1)S(1)} %collective-permute-done.refs_1_, ...), custom_call_target="tpu_custom_call" | custom-call | flops 4294967296 | bytes 8388608 | tf_op jit(solution)/shard_map/pallas_call | solution.py:341
  113.3 1.5 collective-permute-start.10
  114.8 2.1 %collective-permute-start.11 = (f32[8,8,8,256]{3,2,1,0:T(8,128)S(1)}, f32[8,8,8,256]{3,2,1,0:T(8,128)S(1)}, u32[]{:S(2)}, u32[]{:S(2)}) collective-permute-start(f32[8,8,8,256]{3,2,1,0:T(8,128)S(1)} %get-tuple-element.22), channel_id=1, source_target_pairs={{0,8},{8,16},{16,24},{24,0},{1,9},{9,17},{17,25},{25,1},{2,10},{10... | collective-permute-start | bytes 1572872 | tf_op jit(solution)/shard_map/ppermute | solution.py:301
  116.9 12.8 %collective-permute-done.10 = f32[8,8,8,256]{3,2,1,0:T(8,128)S(1)} collective-permute-done((f32[8,8,8,256]{3,2,1,0:T(8,128)S(1)}, f32[8,8,8,256]{3,2,1,0:T(8,128)S(1)}, u32[]{:S(2)}, u32[]{:S(2)}) %collective-permute-start.10) | collective-permute-done | bytes 524320 | tf_op jit(solution)/shard_map/ppermute | solution.py:301
  129.7 10.2 %collective-permute-done.11 = f32[8,8,8,256]{3,2,1,0:T(8,128)S(1)} collective-permute-done((f32[8,8,8,256]{3,2,1,0:T(8,128)S(1)}, f32[8,8,8,256]{3,2,1,0:T(8,128)S(1)}, u32[]{:S(2)}, u32[]{:S(2)}) %collective-permute-start.11) | collective-permute-done | bytes 524320 | tf_op jit(solution)/shard_map/ppermute | solution.py:301
  140.0 0.9 add_add_fusion
  140.9 8.9 %all-to-all-start.4 = ((f32[64,8,256]{2,1,0:T(8,128)}), f32[64,8,256]{2,1,0:T(8,128)S(1)}, u32[]{:S(2)}, u32[]{:S(2)}) async-start(f32[64,8,256]{2,1,0:T(8,128)} %bitcast.18), calls=%async_computation.4 | async-start | bytes 1048576 | tf_op jit(solution)/shard_map/all_to_all | solution.py:315
  149.8 5.4 %shard_map.57 = (bf16[2048,256]{1,0:T(8,128)(2,1)S(1)}, f32[32,64]{1,0:T(8,128)S(1)}) custom-call(s32[256,128]{1,0:T(8,128)S(1)} %copy-done.8, bf16[2048,256]{1,0:T(8,128)(2,1)S(1)} %bitcast.23, bf16[64,256]{1,0:T(8,128)(2,1)S(1)} %copy-done.1), custom_call_target="tpu_custom_call" | custom-call | flops 3221225472 | bytes 8388608 | tf_op jit(solution)/shard_map/pallas_call | solution.py:359
  155.2 0.4 collective-permute-start.13
  155.5 14.1 %shard_map.58.inverse_ref = f32[256,256]{1,0:T(8,128)S(1)} custom-call(f32[256,256]{1,0:T(8,128)S(1)} %bitcast.25), custom_call_target="tpu_custom_call" | custom-call | flops 4294967296 | bytes 8388608 | tf_op jit(solution)/shard_map/pallas_call | solution.py:355
  169.6 1.7 collective-permute-start.14
  171.4 2.7 %collective-permute-start.15 = (f32[32,64]{1,0:T(8,128)S(1)}, f32[32,64]{1,0:T(8,128)S(1)}, u32[]{:S(2)}, u32[]{:S(2)}) collective-permute-start(f32[32,64]{1,0:T(8,128)S(1)} %add.104.refs_0_), channel_id=1, source_target_pairs={{0,128},{64,192},{128,0},{192,64},{1,129},{65,193},{129,1},{193,65... | collective-permute-start | bytes 24584 | tf_op jit(solution)/shard_map/ppermute | solution.py:301
  174.0 1.5 collective-permute-start.16
  175.5 0.7 copy-done.6
  176.2 6.0 %shard_map.59.inner_ref = f32[32,32,64]{2,1,0:T(8,128)S(1)} custom-call(bf16[2048,256]{1,0:T(8,128)(2,1)S(1)} %get-tuple-element.18.fetched_ref, f32[256,256]{1,0:T(8,128)S(1)} %shard_map.58.inverse_ref, s32[1,64]{1,0:T(1,128)S(1)} %bitcast.33), custom_call_target="tpu_custom_call" | custom-call | flops 3221225472 | bytes 16777216 | tf_op jit(solution)/shard_map/pallas_call | solution.py:370
  182.2 5.3 %shard_map.61 = f32[64,256]{1,0:T(8,128)} custom-call(bf16[2048,256]{1,0:T(8,128)(2,1)S(1)} %get-tuple-element.18.fetched_ref, f32[256,256]{1,0:T(8,128)S(1)} %shard_map.58.inverse_ref, f32[32,32,64]{2,1,0:T(8,128)S(1)} %shard_map.59.inner_ref, s32[1,64]{1,0:T(1,128)S(1)} %bitcast.34, bf16[64,256]{1,0:T(8,128)(2,1)S(1)} %copy-done.1, ...), custom_call_target="tpu_custom_call" | custom-call | flops 1073741824 | bytes 4194304 | tf_op jit(solution)/shard_map/pallas_call | solution.py:382
  (25 shorter events, 0.1 us)
Async XLA Ops:
  0.0 1.6 copy-start.5
  0.0 1.6 copy-start.4
  6.7 24.8 %copy-start.7 = (s32[256,128]{1,0:T(8,128)}, s32[256,128]{1,0:T(8,128)S(1)}, u32[]{:S(2)}) copy-start(s32[256,128]{1,0:T(8,128)S(1)} %get-tuple-element.15.pos_ref) | copy-start | bytes 393220
  6.7 24.8 %copy-start.1 = (bf16[64,256]{1,0:T(8,128)(2,1)S(1)}, bf16[64,256]{1,0:T(8,128)(2,1)}, u32[]{:S(2)}) copy-start(bf16[64,256]{1,0:T(8,128)(2,1)} %users_ref.3) | copy-start | bytes 98308
  31.5 8.4 %copy-start = (bf16[1024,256]{1,0:T(8,128)(2,1)S(1)}, bf16[1024,256]{1,0:T(8,128)(2,1)}, u32[]{:S(2)}) copy-start(bf16[1024,256]{1,0:T(8,128)(2,1)} %refs_4_.1) | copy-start | bytes 1572868
  32.3 20.6 %all-to-all-start.3 = ((bf16[64,8,256]{2,1,0:T(8,128)(2,1)}), bf16[64,8,256]{2,1,0:T(8,128)(2,1)S(1)}, u32[]{:S(2)}, u32[]{:S(2)}) async-start(bf16[64,8,256]{2,1,0:T(8,128)(2,1)} %bitcast.16), calls=%async_computation.3 | async-start | bytes 524288 | tf_op jit(solution)/shard_map/all_to_all | solution.py:315
  52.8 17.0 %all-to-all-start.2 = ((f32[32,8,256]{2,1,0:T(8,128)}), f32[32,8,256]{2,1,0:T(8,128)S(1)}, u32[]{:S(2)}, u32[]{:S(2)}) async-start(f32[32,8,256]{2,1,0:T(8,128)} %get-tuple-element.19), calls=%async_computation.2 | async-start | bytes 524288 | tf_op jit(solution)/shard_map/all_to_all | solution.py:315
  58.6 17.3 %collective-permute-start.3 = (bf16[1024,256]{1,0:T(8,128)(2,1)S(1)}, bf16[1024,256]{1,0:T(8,128)(2,1)S(1)}, u32[]{:S(2)}, u32[]{:S(2)}) collective-permute-start(bf16[1024,256]{1,0:T(8,128)(2,1)S(1)} %copy-done), channel_id=1, source_target_pairs={{0,192},{64,0},{128,64},{192,128},{1,193},{65,1},{129,65},{193,129... | collective-permute-start | bytes 1572872 | tf_op jit(solution)/shard_map/ppermute | solution.py:301
  59.8 25.0 %collective-permute-start.4 = (bf16[1024,256]{1,0:T(8,128)(2,1)S(1)}, bf16[1024,256]{1,0:T(8,128)(2,1)S(1)}, u32[]{:S(2)}, u32[]{:S(2)}) collective-permute-start(bf16[1024,256]{1,0:T(8,128)(2,1)S(1)} %copy-done), channel_id=1, source_target_pairs={{0,64},{64,128},{128,192},{192,0},{1,65},{65,129},{129,193},{193,1... | collective-permute-start | bytes 1572872 | tf_op jit(solution)/shard_map/ppermute | solution.py:301
  60.7 24.1 %collective-permute-start.5 = (bf16[1024,256]{1,0:T(8,128)(2,1)S(1)}, bf16[1024,256]{1,0:T(8,128)(2,1)}, u32[]{:S(2)}, u32[]{:S(2)}) collective-permute-start(bf16[1024,256]{1,0:T(8,128)(2,1)S(1)} %copy-done), channel_id=1, source_target_pairs={{0,128},{64,192},{128,0},{192,64},{1,129},{65,193},{129,1},{193,65... | collective-permute-start | bytes 1572872 | tf_op jit(solution)/shard_map/ppermute | solution.py:301
  69.8 71.1 %all-to-all-start.1 = ((bf16[32,64,256]{2,1,0:T(8,128)(2,1)}), bf16[32,64,256]{2,1,0:T(8,128)(2,1)S(1)}, u32[]{:S(2)}, u32[]{:S(2)}) async-start(bf16[32,64,256]{2,1,0:T(8,128)(2,1)} %bitcast.3), calls=%async_computation.1 | async-start | bytes 2097152 | tf_op jit(solution)/shard_map/all_to_all | solution.py:315
  75.4 9.9 %collective-permute-start.6 = (bf16[1024,256]{1,0:T(8,128)(2,1)S(1)}, bf16[1024,256]{1,0:T(8,128)(2,1)S(1)}, u32[]{:S(2)}, u32[]{:S(2)}) collective-permute-start(bf16[1024,256]{1,0:T(8,128)(2,1)S(1)} %copy-done), channel_id=1, source_target_pairs={{0,32},{32,0},{1,33},{33,1},{2,34},{34,2},{3,35},{35,3},{4,36},{36... | collective-permute-start | bytes 1572872 | tf_op jit(solution)/shard_map/ppermute | solution.py:301
  75.5 12.9 %collective-permute-start = (bf16[8,8,8,256]{3,2,1,0:T(8,128)(2,1)S(1)}, bf16[8,8,8,256]{3,2,1,0:T(8,128)(2,1)S(1)}, u32[]{:S(2)}, u32[]{:S(2)}) collective-permute-start(bf16[8,8,8,256]{3,2,1,0:T(8,128)(2,1)S(1)} %bitcast.26), channel_id=1, source_target_pairs={{0,24},{8,0},{16,8},{24,16},{1,25},{9,1},{17,9},{25,17},{2,26},{10... | collective-permute-start | bytes 786440 | tf_op jit(solution)/shard_map/ppermute | solution.py:301
  75.8 29.6 %collective-permute-start.7 = (bf16[1024,256]{1,0:T(8,128)(2,1)S(1)}, bf16[1024,256]{1,0:T(8,128)(2,1)}, u32[]{:S(2)}, u32[]{:S(2)}) collective-permute-start(bf16[1024,256]{1,0:T(8,128)(2,1)S(1)} %collective-permute-done.3.refs_5_), channel_id=1, source_target_pairs={{0,32},{32,0},{1,33},{33,1},{2,34},{34,2},{3,35},{35,3},{4,36},{36... | collective-permute-start | bytes 1572872 | tf_op jit(solution)/shard_map/ppermute | solution.py:301
  84.8 20.7 %collective-permute-start.8 = (bf16[1024,256]{1,0:T(8,128)(2,1)S(1)}, bf16[1024,256]{1,0:T(8,128)(2,1)}, u32[]{:S(2)}, u32[]{:S(2)}) collective-permute-start(bf16[1024,256]{1,0:T(8,128)(2,1)S(1)} %collective-permute-done.4.refs_6_), channel_id=1, source_target_pairs={{0,32},{32,0},{1,33},{33,1},{2,34},{34,2},{3,35},{35,3},{4,36},{36... | collective-permute-start | bytes 1572872 | tf_op jit(solution)/shard_map/ppermute | solution.py:301
  84.8 20.7 %collective-permute-start.9 = (bf16[1024,256]{1,0:T(8,128)(2,1)}, bf16[1024,256]{1,0:T(8,128)(2,1)}, u32[]{:S(2)}, u32[]{:S(2)}) collective-permute-start(bf16[1024,256]{1,0:T(8,128)(2,1)} %collective-permute-done.5.refs_7_), channel_id=1, source_target_pairs={{0,32},{32,0},{1,33},{33,1},{2,34},{34,2},{3,35},{35,3},{4,36},{36... | collective-permute-start | bytes 1572872 | tf_op jit(solution)/shard_map/ppermute | solution.py:301
  85.3 0.8 copy-start.2
  86.1 15.0 %collective-permute-start.1 = (bf16[8,8,8,256]{3,2,1,0:T(8,128)(2,1)S(1)}, bf16[8,8,8,256]{3,2,1,0:T(8,128)(2,1)}, u32[]{:S(2)}, u32[]{:S(2)}) collective-permute-start(bf16[8,8,8,256]{3,2,1,0:T(8,128)(2,1)S(1)} %bitcast.27), channel_id=1, source_target_pairs={{0,16},{8,24},{16,0},{24,8},{1,17},{9,25},{17,1},{25,9},{2,18},{10... | collective-permute-start | bytes 786440 | tf_op jit(solution)/shard_map/ppermute | solution.py:301
  88.4 17.0 %collective-permute-start.2 = (bf16[8,8,8,256]{3,2,1,0:T(8,128)(2,1)S(1)}, bf16[8,8,8,256]{3,2,1,0:T(8,128)(2,1)}, u32[]{:S(2)}, u32[]{:S(2)}) collective-permute-start(bf16[8,8,8,256]{3,2,1,0:T(8,128)(2,1)S(1)} %bitcast.28), channel_id=1, source_target_pairs={{0,8},{8,16},{16,24},{24,0},{1,9},{9,17},{17,25},{25,1},{2,10},{10... | collective-permute-start | bytes 786440 | tf_op jit(solution)/shard_map/ppermute | solution.py:301
  105.5 1.0 copy-start.3
  113.3 16.4 %collective-permute-start.10 = (f32[8,8,8,256]{3,2,1,0:T(8,128)S(1)}, f32[8,8,8,256]{3,2,1,0:T(8,128)S(1)}, u32[]{:S(2)}, u32[]{:S(2)}) collective-permute-start(f32[8,8,8,256]{3,2,1,0:T(8,128)S(1)} %get-tuple-element.21), channel_id=1, source_target_pairs={{0,16},{8,24},{16,0},{24,8},{1,17},{9,25},{17,1},{25,9},{2,18},{10... | collective-permute-start | bytes 1572872 | tf_op jit(solution)/shard_map/ppermute | solution.py:301
  114.8 25.1 %collective-permute-start.11 = (f32[8,8,8,256]{3,2,1,0:T(8,128)S(1)}, f32[8,8,8,256]{3,2,1,0:T(8,128)S(1)}, u32[]{:S(2)}, u32[]{:S(2)}) collective-permute-start(f32[8,8,8,256]{3,2,1,0:T(8,128)S(1)} %get-tuple-element.22), channel_id=1, source_target_pairs={{0,8},{8,16},{16,24},{24,0},{1,9},{9,17},{17,25},{25,1},{2,10},{10... | collective-permute-start | bytes 1572872 | tf_op jit(solution)/shard_map/ppermute | solution.py:301
  116.9 23.1 %collective-permute-start.12 = (f32[8,8,8,256]{3,2,1,0:T(8,128)S(1)}, f32[8,8,8,256]{3,2,1,0:T(8,128)S(1)}, u32[]{:S(2)}, u32[]{:S(2)}) collective-permute-start(f32[8,8,8,256]{3,2,1,0:T(8,128)S(1)} %get-tuple-element.23), channel_id=1, source_target_pairs={{0,24},{8,0},{16,8},{24,16},{1,25},{9,1},{17,9},{25,17},{2,26},{10... | collective-permute-start | bytes 1572872 | tf_op jit(solution)/shard_map/ppermute | solution.py:301
  140.9 8.9 %copy-start.8 = (s32[256,128]{1,0:T(8,128)S(1)}, s32[256,128]{1,0:T(8,128)}, u32[]{:S(2)}) copy-start(s32[256,128]{1,0:T(8,128)} %copy-done.7) | copy-start | bytes 393220
  140.9 41.2 %all-to-all-start.4 = ((f32[64,8,256]{2,1,0:T(8,128)}), f32[64,8,256]{2,1,0:T(8,128)S(1)}, u32[]{:S(2)}, u32[]{:S(2)}) async-start(f32[64,8,256]{2,1,0:T(8,128)} %bitcast.18), calls=%async_computation.4 | async-start | bytes 1048576 | tf_op jit(solution)/shard_map/all_to_all | solution.py:315
  155.2 14.5 %collective-permute-start.13 = (f32[32,64]{1,0:T(8,128)S(1)}, f32[32,64]{1,0:T(8,128)S(1)}, u32[]{:S(2)}, u32[]{:S(2)}) collective-permute-start(f32[32,64]{1,0:T(8,128)S(1)} %get-tuple-element.24), channel_id=1, source_target_pairs={{0,32},{32,0},{1,33},{33,1},{2,34},{34,2},{3,35},{35,3},{4,36},{36... | collective-permute-start | bytes 24584 | tf_op jit(solution)/shard_map/ppermute | solution.py:301
  169.6 12.5 %collective-permute-start.14 = (f32[32,64]{1,0:T(8,128)S(1)}, f32[32,64]{1,0:T(8,128)S(1)}, u32[]{:S(2)}, u32[]{:S(2)}) collective-permute-start(f32[32,64]{1,0:T(8,128)S(1)} %add.104.refs_0_), channel_id=1, source_target_pairs={{0,64},{64,128},{128,192},{192,0},{1,65},{65,129},{129,193},{193,1... | collective-permute-start | bytes 24584 | tf_op jit(solution)/shard_map/ppermute | solution.py:301
  171.4 10.8 %collective-permute-start.15 = (f32[32,64]{1,0:T(8,128)S(1)}, f32[32,64]{1,0:T(8,128)S(1)}, u32[]{:S(2)}, u32[]{:S(2)}) collective-permute-start(f32[32,64]{1,0:T(8,128)S(1)} %add.104.refs_0_), channel_id=1, source_target_pairs={{0,128},{64,192},{128,0},{192,64},{1,129},{65,193},{129,1},{193,65... | collective-permute-start | bytes 24584 | tf_op jit(solution)/shard_map/ppermute | solution.py:301
  174.0 8.1 %collective-permute-start.16 = (f32[32,64]{1,0:T(8,128)S(1)}, f32[32,64]{1,0:T(8,128)S(1)}, u32[]{:S(2)}, u32[]{:S(2)}) collective-permute-start(f32[32,64]{1,0:T(8,128)S(1)} %add.104.refs_0_), channel_id=1, source_target_pairs={{0,192},{64,0},{128,64},{192,128},{1,193},{65,1},{129,65},{193,129... | collective-permute-start | bytes 24584 | tf_op jit(solution)/shard_map/ppermute | solution.py:301
  175.5 0.7 copy-start.6

commit v4 on v3

--- a/solution.py
+++ b/solution.py
@@ -42,10 +42,18 @@
 
 
 def dot_split(a, b, ca=1, cb=0):
-    a0, a1, a2 = a
-    b0, b1, b2 = b
-    small = dot(a2, b0, ca, cb) + dot(a0, b2, ca, cb) + dot(a1, b1, ca, cb)
-    return (small + (dot(a1, b0, ca, cb) + dot(a0, b1, ca, cb))) + dot(a0, b0, ca, cb)
+    n = a[0].shape[1 - ca]
+    top = dot(jnp.concatenate(a, axis=1 - ca), b[0], ca, cb)
+    mid = dot(jnp.concatenate(a[:2], axis=1 - ca), b[1], ca, cb)
+    low = dot(a[0], b[2], ca, cb)
+    small = top[2 * n :] + low + mid[n:]
+    return (small + (top[n : 2 * n] + mid[:n])) + top[:n]
+
+
+def dot_pieces(a, b, ca=1, cb=0):
+    n = a[0].shape[1 - ca]
+    all_rows = dot(jnp.concatenate(a, axis=1 - ca), b, ca, cb)
+    return (all_rows[2 * n :] + all_rows[n : 2 * n]) + all_rows[:n]
 
 
 def one_hot(column, width):
@@ -129,14 +137,15 @@
     users = users_ref[...]
     lane = iota((LIST, USERS_DEV), 1)
     pred = jnp.zeros((LIST, USERS_DEV), F32)
-    for c in range(CHUNKS):
-        part = slice(c * CHUNK, (c + 1) * CHUNK)
-        rows = dot(one_hot(pos_ref[:, c : c + 1], SLOTS), came).astype(BF16)
-        fetched_ref[part, :] = rows
+    size = 4 * CHUNK
+    for n in range(SLOTS // size):
+        chosen = [one_hot(pos_ref[:, c : c + 1], SLOTS) for c in range(4 * n, 4 * n + 4)]
+        rows = dot(jnp.concatenate(chosen, axis=0), came).astype(BF16)
+        fetched_ref[n * size : (n + 1) * size, :] = rows
         cross = dot(rows, users, 1, 1)
-        for i in range(CHUNK // LIST):
-            user = c * (CHUNK // LIST) + i
-            pred = pred + jnp.where(lane == user, cross[i * LIST : (i + 1) * LIST, :], 0.0)
+        for i in range(size // LIST):
+            user = n * (size // LIST) + i
+            pred = jnp.where(lane == user, cross[i * LIST : (i + 1) * LIST, :], pred)
     pred_ref[...] = pred
 
 
@@ -154,10 +163,9 @@
         users = jnp.concatenate(users, axis=0).astype(BF16)
         copies[i].wait()
         scores = scores + dot(users, held[i], 1, 1)
-    s0, s1, s2 = split(scores)
+    pieces = split(scores)
     for i in range(N_DIM):
-        table = held[i]
-        times = (dot(s2, table) + dot(s1, table)) + dot(s0, table)
+        times = dot_pieces(pieces, held[i])
         for n, out_ref in enumerate(out_refs):
             part = times[n * quarter : (n + 1) * quarter]
             out_ref[:, block_ref[i]] = part.reshape(8, quarter // 8, BLOCK)
@@ -209,19 +217,18 @@
     i0, i1, i2 = split(inverse_ref[...])
     same = iota((CHUNK, CHUNK), 0) // LIST == iota((CHUNK, CHUNK), 1) // LIST
 
-    def chunk(c, carry):
-        part = pl.ds(pl.multiple_of(c * CHUNK, CHUNK), CHUNK)
+    def chunk(c):
+        part = slice(c * CHUNK, (c + 1) * CHUNK)
         rows = fetched_ref[part, :]
         scaled = (dot(rows, i2) + dot(rows, i1)) + dot(rows, i0)
-        s0, s1, s2 = split(scaled)
-        cross = (dot(s2, rows, 1, 1) + dot(s1, rows, 1, 1)) + dot(s0, rows, 1, 1)
+        cross = dot_pieces(split(scaled), rows, 1, 1)
         cross = jnp.where(same, cross, 0.0)
         both = cross[:, :128] + cross[:, 128:]
         both = both + pltpu.roll(both, 64, 1)
         folded[part, :] = both + pltpu.roll(both, 32, 1)
-        return carry
-
-    lax.fori_loop(0, CHUNKS, chunk, 0, unroll=4)
+
+    for c in range(CHUNKS):
+        chunk(c)
     slot = iota((LIST, USERS_DEV), 0)
     live = jnp.where(slot < counts_ref[...], 1.0, 0.0)
     for a in range(LIST):
@@ -253,8 +260,7 @@
 
 
 def weigh(values, fetched):
-    s0, s1, s2 = split(spread(values))
-    return (dot(s2, fetched) + dot(s1, fetched)) + dot(s0, fetched)
+    return dot_pieces(split(spread(values)), fetched)
 
 
 def final_kernel(
@@ -265,7 +271,6 @@
     inverse = split(inverse_ref[...])
     own = users_ref[...].astype(F32)
     slot = iota((LIST, USERS_DEV), 0)
-    lane = iota((LIST, USERS_DEV), 1)
     live = jnp.where(slot < counts_ref[...], 1.0, 0.0)
     pred = pred_refs[0][...]
     for ref in pred_refs[1:]:
@@ -276,14 +281,13 @@
         times = times + times_ref[i]
     gradient = weigh(residual, fetched) + WEIGHT * times + own
     scaled = dot_split(split(gradient), inverse)
-    y0, y1, y2 = split(scaled)
-    cross = (dot(fetched, y2, 1, 1) + dot(fetched, y1, 1, 1)) + dot(fetched, y0, 1, 1)
-    projected = jnp.zeros((LIST, USERS_DEV), F32)
+    cross = dot(fetched, jnp.concatenate(split(scaled), axis=0), 1, 1)
+    lane = lax.rem(iota((LIST, 3 * USERS_DEV), 1), USERS_DEV)
+    found = jnp.zeros((LIST, 3 * USERS_DEV), F32)
     for user in range(USERS_DEV):
-        projected = projected + jnp.where(
-            lane == user, cross[user * LIST : (user + 1) * LIST, :], 0.0
-        )
-    projected = projected * live
+        found = jnp.where(lane == user, cross[user * LIST : (user + 1) * LIST, :], found)
+    projected = found[:, 2 * USERS_DEV :] + found[:, USERS_DEV : 2 * USERS_DEV]
+    projected = (projected + found[:, :USERS_DEV]) * live
     weights = jnp.zeros((LIST, USERS_DEV), F32)
     for a in range(LIST):
         weights = weights + inner_ref[a] * projected[a : a + 1, :]
@@ -303,8 +307,9 @@
 
 def gather_dims(table):
     tables = [table] + [shift(table, "y", 4 - i) for i in (1, 3)]
-    tables = tables + [shift(table, "y", 2)]
-    tables = tables + [shift(t, "core", 1) for t in tables]
+    far = shift(table, "y", 2)
+    swapped = [shift(t, "core", 1) for t in tables]
+    tables = tables + [far] + swapped + [shift(far, "core", 1)]
     y = lax.axis_index("y")
     core = lax.axis_index("core")
     blocks = [((y + i) % 4) * 2 + (core + j) % 2 for j in (0, 1) for i in (0, 1, 3, 2)]

time: 191 us -> 187 us (0.979)
  Pallas kernels: 45.1 us -> 41.6 us
    pallas_call x1, Pallas kernels: 5.3 us -> 3.23 us  [body(): call(final_kernel, shape((USERS_DEV, BLOCK), F32), 10, 1 << 30, 4 << 20)]
  transfers between devices with their start and end apart: 21 -> 21, of which waited for: 8 -> 8; matrix products, arithmetic and copies ran while one was open for 1% -> 1% of each run, Pallas kernels for 19% -> 18%
where the time goes in v4:
time: 187 us; the launch traced here: 184 us
  waiting for transfers between devices  64.5 us (34%)
  starting transfers between devices  47.1 us (25%)
  Pallas kernels  41.6 us (22%)
  blocking collectives  24.8 us (13%)
  local copies, waits for them, and re-layouts  3.31 us (2%)
    ppermute x17, waiting for transfers between devices, shift(): return lax.ppermute(x, axis, [(i, (i + by) % size) for i in range(size)])  46.3 us
    all_to_all x4, starting transfers between devices, exchange(): return lax.all_to_all(x, axes, 0, 0, tiled=True)  27.9 us
    all_to_all x1, blocking collectives, exchange(): return lax.all_to_all(x, axes, 0, 0, tiled=True)  24.8 us
    ppermute x17, starting transfers between devices, shift(): return lax.ppermute(x, axis, [(i, (i + by) % size) for i in range(size)])  19.2 us
    all_to_all x4, waiting for transfers between devices, exchange(): return lax.all_to_all(x, axes, 0, 0, tiled=True)  18.2 us
    pallas_call x1, Pallas kernels, body(): call(inverse_kernel, shape((BLOCK, BLOCK), F32), 1, 4 << 30, 8 << 20)  14 us
    pallas_call x1, Pallas kernels, body(): call(product_kernel, [shape((8, N_DIM, group, BLOCK), F32)] * 4, 5 + len(...  6.79 us
    pallas_call x1, Pallas kernels, body(): call(inner_kernel, shape((LIST, LIST, USERS_DEV), F32), 3, 3 << 30, 16 <<...  5.26 us
  transfers between devices with their start and end apart: 21, of which 8 were waited for; matrix products, arithmetic and copies ran while one was open for 1% of the time, Pallas kernels for 18%

profile of v4, /device:TPU:2, one launch (start us, length us, event | category | flops | bytes accessed | tf_op | source)
XLA Modules:
  0.0 184.0 jit_solution(15935529086243822823)
XLA Ops:
  0.0 1.6 convolution_bitcast_fusion.diag_ref
  1.6 5.1 %shard_map.55 = (s32[256,128]{1,0:T(8,128)S(1)}, f32[32,8,384]{2,1,0:T(8,128)S(1)}) custom-call(s32[32,64]{1,0:T(8,128)S(1)} %bitcast.32, s32[256,128]{1,0:T(8,128)S(1)} %bitcast.31, f32[32,8,256]{2,1,0:T(8,128)S(1)} %convolution_bitcast_fusion.diag_ref), custom_call_target="tpu_custom_call" | custom-call | flops 1073741824 | bytes 4194304 | tf_op jit(solution)/shard_map/pallas_call | solution.py:331
  6.7 0.0 copy-start.1
  6.7 24.8 %all_to_all.25.came_ref = f32[32,8,384]{2,1,0:T(8,128)S(1)} all-to-all(f32[32,8,384]{2,1,0:T(8,128)S(1)} %get-tuple-element.16), channel_id=1, replica_groups=mesh['y'=4,'core'=2,'x'=4,'z'=8] {'x','z'}, dimensions={0} | all-to-all | bytes 786432 | tf_op jit(solution)/shard_map/all_to_all | solution.py:320
  31.5 0.7 broadcast_in_dim.8
  32.3 7.7 %all-to-all-start.3 = ((bf16[64,8,256]{2,1,0:T(8,128)(2,1)}), bf16[64,8,256]{2,1,0:T(8,128)(2,1)S(1)}, u32[]{:S(2)}, u32[]{:S(2)}) async-start(bf16[64,8,256]{2,1,0:T(8,128)(2,1)} %bitcast.16), calls=%async_computation.3 | async-start | bytes 524288 | tf_op jit(solution)/shard_map/all_to_all | solution.py:320
  39.9 2.5 %shard_map.56 = (bf16[2048,256]{1,0:T(8,128)(2,1)}, f32[32,8,256]{2,1,0:T(8,128)}) custom-call(f32[32,8,384]{2,1,0:T(8,128)S(1)} %all_to_all.25.came_ref, bf16[1024,256]{1,0:T(8,128)(2,1)S(1)} %copy-done), custom_call_target="tpu_custom_call" | custom-call | flops 1073741824 | bytes 4194304 | tf_op jit(solution)/shard_map/pallas_call | solution.py:337
  42.4 10.4 %all-to-all-done.3 = bf16[64,8,256]{2,1,0:T(8,128)(2,1)S(1)} async-done(((bf16[64,8,256]{2,1,0:T(8,128)(2,1)}), bf16[64,8,256]{2,1,0:T(8,128)(2,1)S(1)}, u32[]{:S(2)}, u32[]{:S(2)}) %all-to-all-start.3) | async-done | bytes 262176 | tf_op jit(solution)/shard_map/all_to_all | solution.py:320
  52.8 5.7 %all-to-all-start.2 = ((f32[32,8,256]{2,1,0:T(8,128)}), f32[32,8,256]{2,1,0:T(8,128)S(1)}, u32[]{:S(2)}, u32[]{:S(2)}) async-start(f32[32,8,256]{2,1,0:T(8,128)} %get-tuple-element.19), calls=%async_computation.2 | async-start | bytes 524288 | tf_op jit(solution)/shard_map/all_to_all | solution.py:320
  58.6 1.2 collective-permute-start.3
  59.8 0.9 collective-permute-start.4
  60.7 1.3 collective-permute-start.5
  62.0 7.8 %all-to-all-done.2 = f32[32,8,256]{2,1,0:T(8,128)S(1)} async-done(((f32[32,8,256]{2,1,0:T(8,128)}), f32[32,8,256]{2,1,0:T(8,128)S(1)}, u32[]{:S(2)}, u32[]{:S(2)}) %all-to-all-start.2) | async-done | bytes 262176 | tf_op jit(solution)/shard_map/all_to_all | solution.py:320
  69.8 5.6 %all-to-all-start.1 = ((bf16[32,64,256]{2,1,0:T(8,128)(2,1)}), bf16[32,64,256]{2,1,0:T(8,128)(2,1)S(1)}, u32[]{:S(2)}, u32[]{:S(2)}) async-start(bf16[32,64,256]{2,1,0:T(8,128)(2,1)} %bitcast.3), calls=%async_computation.1 | async-start | bytes 2097152 | tf_op jit(solution)/shard_map/all_to_all | solution.py:320
  75.4 0.1 collective-permute-start.6
  75.5 0.3 collective-permute-start
  75.8 0.0 collective-permute-done.3.refs_5_
  75.8 0.2 collective-permute-start.7
  76.0 8.7 %collective-permute-done.4.refs_6_ = bf16[1024,256]{1,0:T(8,128)(2,1)S(1)} collective-permute-done((bf16[1024,256]{1,0:T(8,128)(2,1)S(1)}, bf16[1024,256]{1,0:T(8,128)(2,1)S(1)}, u32[]{:S(2)}, u32[]{:S(2)}) %collective-permute-start.4) | collective-permute-done | bytes 524320 | tf_op jit(solution)/shard_map/ppermute | solution.py:305
  84.8 0.0 collective-permute-start.8
  84.8 0.5 collective-permute-start.9
  85.3 0.8 copy-done.2
  86.1 2.1 %collective-permute-start.1 = (bf16[8,8,8,256]{3,2,1,0:T(8,128)(2,1)S(1)}, bf16[8,8,8,256]{3,2,1,0:T(8,128)(2,1)}, u32[]{:S(2)}, u32[]{:S(2)}) collective-permute-start(bf16[8,8,8,256]{3,2,1,0:T(8,128)(2,1)S(1)} %bitcast.27), channel_id=1, source_target_pairs={{0,16},{8,24},{16,0},{24,8},{1,17},{9,25},{17,1},{25,9},{2,18},{10... | collective-permute-start | bytes 786440 | tf_op jit(solution)/shard_map/ppermute | solution.py:305
  88.2 0.2 collective-permute-done.refs_1_
  88.4 2.8 %collective-permute-start.2 = (bf16[8,8,8,256]{3,2,1,0:T(8,128)(2,1)S(1)}, bf16[8,8,8,256]{3,2,1,0:T(8,128)(2,1)}, u32[]{:S(2)}, u32[]{:S(2)}) collective-permute-start(bf16[8,8,8,256]{3,2,1,0:T(8,128)(2,1)S(1)} %bitcast.28), channel_id=1, source_target_pairs={{0,8},{8,16},{16,24},{24,0},{1,9},{9,17},{17,25},{25,1},{2,10},{10... | collective-permute-start | bytes 786440 | tf_op jit(solution)/shard_map/ppermute | solution.py:305
  91.2 0.1 stack.35.block_ref
  91.3 9.8 %collective-permute-done.1.refs_2_ = bf16[8,8,8,256]{3,2,1,0:T(8,128)(2,1)} collective-permute-done((bf16[8,8,8,256]{3,2,1,0:T(8,128)(2,1)S(1)}, bf16[8,8,8,256]{3,2,1,0:T(8,128)(2,1)}, u32[]{:S(2)}, u32[]{:S(2)}) %collective-permute-start.1) | collective-permute-done | bytes 262176 | tf_op jit(solution)/shard_map/ppermute | solution.py:305
  101.0 4.4 %collective-permute-done.2.refs_3_ = bf16[8,8,8,256]{3,2,1,0:T(8,128)(2,1)} collective-permute-done((bf16[8,8,8,256]{3,2,1,0:T(8,128)(2,1)S(1)}, bf16[8,8,8,256]{3,2,1,0:T(8,128)(2,1)}, u32[]{:S(2)}, u32[]{:S(2)}) %collective-permute-start.2) | collective-permute-done | bytes 262176 | tf_op jit(solution)/shard_map/ppermute | solution.py:305
  105.5 0.0 collective-permute-done.7.refs_9_
  105.5 0.0 collective-permute-done.8.refs_10_
  105.5 0.0 collective-permute-done.9.refs_11_
  105.5 1.0 copy-done.3
  106.5 6.8 %shard_map.60 = (f32[8,8,8,256]{3,2,1,0:T(8,128)S(1)}, f32[8,8,8,256]{3,2,1,0:T(8,128)S(1)}, f32[8,8,8,256]{3,2,1,0:T(8,128)S(1)}, f32[8,8,8,256]{3,2,1,0:T(8,128)S(1)}) custom-call(s32[8]{0:T(128)S(1)} %stack.35.block_ref, bf16[8,8,8,256]{3,2,1,0:T(8,128)(2,1)S(1)} %bitcast.29, bf16[8,8,8,256]{3,2,1,0:T(8,128)(2,1)S(1)} %collective-permute-done.refs_1_, ...), custom_call_target="tpu_custom_call" | custom-call | flops 4294967296 | bytes 8388608 | tf_op jit(solution)/shard_map/pallas_call | solution.py:346
  113.3 1.5 collective-permute-start.10
  114.9 2.1 %collective-permute-start.11 = (f32[8,8,8,256]{3,2,1,0:T(8,128)S(1)}, f32[8,8,8,256]{3,2,1,0:T(8,128)S(1)}, u32[]{:S(2)}, u32[]{:S(2)}) collective-permute-start(f32[8,8,8,256]{3,2,1,0:T(8,128)S(1)} %get-tuple-element.22), channel_id=1, source_target_pairs={{0,8},{8,16},{16,24},{24,0},{1,9},{9,17},{17,25},{25,1},{2,10},{10... | collective-permute-start | bytes 1572872 | tf_op jit(solution)/shard_map/ppermute | solution.py:305
  116.9 12.8 %collective-permute-done.10 = f32[8,8,8,256]{3,2,1,0:T(8,128)S(1)} collective-permute-done((f32[8,8,8,256]{3,2,1,0:T(8,128)S(1)}, f32[8,8,8,256]{3,2,1,0:T(8,128)S(1)}, u32[]{:S(2)}, u32[]{:S(2)}) %collective-permute-start.10) | collective-permute-done | bytes 524320 | tf_op jit(solution)/shard_map/ppermute | solution.py:305
  129.7 10.2 %collective-permute-done.11 = f32[8,8,8,256]{3,2,1,0:T(8,128)S(1)} collective-permute-done((f32[8,8,8,256]{3,2,1,0:T(8,128)S(1)}, f32[8,8,8,256]{3,2,1,0:T(8,128)S(1)}, u32[]{:S(2)}, u32[]{:S(2)}) %collective-permute-start.11) | collective-permute-done | bytes 524320 | tf_op jit(solution)/shard_map/ppermute | solution.py:305
  140.0 0.9 add_add_fusion
  140.9 8.9 %all-to-all-start.4 = ((f32[64,8,256]{2,1,0:T(8,128)}), f32[64,8,256]{2,1,0:T(8,128)S(1)}, u32[]{:S(2)}, u32[]{:S(2)}) async-start(f32[64,8,256]{2,1,0:T(8,128)} %bitcast.18), calls=%async_computation.4 | async-start | bytes 1048576 | tf_op jit(solution)/shard_map/all_to_all | solution.py:320
  149.8 4.7 %shard_map.57 = (bf16[2048,256]{1,0:T(8,128)(2,1)S(1)}, f32[32,64]{1,0:T(8,128)S(1)}) custom-call(s32[256,128]{1,0:T(8,128)S(1)} %copy-done.8, bf16[2048,256]{1,0:T(8,128)(2,1)S(1)} %bitcast.23, bf16[64,256]{1,0:T(8,128)(2,1)S(1)} %copy-done.1), custom_call_target="tpu_custom_call" | custom-call | flops 3221225472 | bytes 8388608 | tf_op jit(solution)/shard_map/pallas_call | solution.py:364
  154.6 0.4 collective-permute-start.13
  154.9 14.0 %shard_map.58.inverse_ref = f32[256,256]{1,0:T(8,128)S(1)} custom-call(f32[256,256]{1,0:T(8,128)S(1)} %bitcast.25), custom_call_target="tpu_custom_call" | custom-call | flops 4294967296 | bytes 8388608 | tf_op jit(solution)/shard_map/pallas_call | solution.py:360
  168.9 1.7 collective-permute-start.14
  170.7 2.7 %collective-permute-start.15 = (f32[32,64]{1,0:T(8,128)S(1)}, f32[32,64]{1,0:T(8,128)S(1)}, u32[]{:S(2)}, u32[]{:S(2)}) collective-permute-start(f32[32,64]{1,0:T(8,128)S(1)} %add.104.refs_0_), channel_id=1, source_target_pairs={{0,128},{64,192},{128,0},{192,64},{1,129},{65,193},{129,1},{193,65... | collective-permute-start | bytes 24584 | tf_op jit(solution)/shard_map/ppermute | solution.py:305
  173.3 1.5 collective-permute-start.16
  174.8 0.7 copy-done.6
  175.4 5.3 %shard_map.59.inner_ref = f32[32,32,64]{2,1,0:T(8,128)S(1)} custom-call(bf16[2048,256]{1,0:T(8,128)(2,1)S(1)} %get-tuple-element.18.fetched_ref, f32[256,256]{1,0:T(8,128)S(1)} %shard_map.58.inverse_ref, s32[1,64]{1,0:T(1,128)S(1)} %bitcast.33), custom_call_target="tpu_custom_call" | custom-call | flops 3221225472 | bytes 16777216 | tf_op jit(solution)/shard_map/pallas_call | solution.py:375
  180.8 3.2 %shard_map.61 = f32[64,256]{1,0:T(8,128)} custom-call(bf16[2048,256]{1,0:T(8,128)(2,1)S(1)} %get-tuple-element.18.fetched_ref, f32[256,256]{1,0:T(8,128)S(1)} %shard_map.58.inverse_ref, f32[32,32,64]{2,1,0:T(8,128)S(1)} %shard_map.59.inner_ref, s32[1,64]{1,0:T(1,128)S(1)} %bitcast.34, bf16[64,256]{1,0:T(8,128)(2,1)S(1)} %copy-done.1, ...), custom_call_target="tpu_custom_call" | custom-call | flops 1073741824 | bytes 4194304 | tf_op jit(solution)/shard_map/pallas_call | solution.py:387
  (25 shorter events, 0.1 us)
Async XLA Ops:
  0.0 1.6 copy-start.5
  0.0 1.6 copy-start.4
  6.7 24.8 %copy-start.7 = (s32[256,128]{1,0:T(8,128)}, s32[256,128]{1,0:T(8,128)S(1)}, u32[]{:S(2)}) copy-start(s32[256,128]{1,0:T(8,128)S(1)} %get-tuple-element.15.pos_ref) | copy-start | bytes 393220
  6.7 24.8 %copy-start.1 = (bf16[64,256]{1,0:T(8,128)(2,1)S(1)}, bf16[64,256]{1,0:T(8,128)(2,1)}, u32[]{:S(2)}) copy-start(bf16[64,256]{1,0:T(8,128)(2,1)} %users_ref.3) | copy-start | bytes 98308
  31.5 8.4 %copy-start = (bf16[1024,256]{1,0:T(8,128)(2,1)S(1)}, bf16[1024,256]{1,0:T(8,128)(2,1)}, u32[]{:S(2)}) copy-start(bf16[1024,256]{1,0:T(8,128)(2,1)} %refs_4_.1) | copy-start | bytes 1572868
  32.3 20.6 %all-to-all-start.3 = ((bf16[64,8,256]{2,1,0:T(8,128)(2,1)}), bf16[64,8,256]{2,1,0:T(8,128)(2,1)S(1)}, u32[]{:S(2)}, u32[]{:S(2)}) async-start(bf16[64,8,256]{2,1,0:T(8,128)(2,1)} %bitcast.16), calls=%async_computation.3 | async-start | bytes 524288 | tf_op jit(solution)/shard_map/all_to_all | solution.py:320
  52.8 17.0 %all-to-all-start.2 = ((f32[32,8,256]{2,1,0:T(8,128)}), f32[32,8,256]{2,1,0:T(8,128)S(1)}, u32[]{:S(2)}, u32[]{:S(2)}) async-start(f32[32,8,256]{2,1,0:T(8,128)} %get-tuple-element.19), calls=%async_computation.2 | async-start | bytes 524288 | tf_op jit(solution)/shard_map/all_to_all | solution.py:320
  58.6 17.3 %collective-permute-start.3 = (bf16[1024,256]{1,0:T(8,128)(2,1)S(1)}, bf16[1024,256]{1,0:T(8,128)(2,1)S(1)}, u32[]{:S(2)}, u32[]{:S(2)}) collective-permute-start(bf16[1024,256]{1,0:T(8,128)(2,1)S(1)} %copy-done), channel_id=1, source_target_pairs={{0,192},{64,0},{128,64},{192,128},{1,193},{65,1},{129,65},{193,129... | collective-permute-start | bytes 1572872 | tf_op jit(solution)/shard_map/ppermute | solution.py:305
  59.8 25.0 %collective-permute-start.4 = (bf16[1024,256]{1,0:T(8,128)(2,1)S(1)}, bf16[1024,256]{1,0:T(8,128)(2,1)S(1)}, u32[]{:S(2)}, u32[]{:S(2)}) collective-permute-start(bf16[1024,256]{1,0:T(8,128)(2,1)S(1)} %copy-done), channel_id=1, source_target_pairs={{0,64},{64,128},{128,192},{192,0},{1,65},{65,129},{129,193},{193,1... | collective-permute-start | bytes 1572872 | tf_op jit(solution)/shard_map/ppermute | solution.py:305
  60.7 24.1 %collective-permute-start.5 = (bf16[1024,256]{1,0:T(8,128)(2,1)S(1)}, bf16[1024,256]{1,0:T(8,128)(2,1)}, u32[]{:S(2)}, u32[]{:S(2)}) collective-permute-start(bf16[1024,256]{1,0:T(8,128)(2,1)S(1)} %copy-done), channel_id=1, source_target_pairs={{0,128},{64,192},{128,0},{192,64},{1,129},{65,193},{129,1},{193,65... | collective-permute-start | bytes 1572872 | tf_op jit(solution)/shard_map/ppermute | solution.py:305
  69.8 71.1 %all-to-all-start.1 = ((bf16[32,64,256]{2,1,0:T(8,128)(2,1)}), bf16[32,64,256]{2,1,0:T(8,128)(2,1)S(1)}, u32[]{:S(2)}, u32[]{:S(2)}) async-start(bf16[32,64,256]{2,1,0:T(8,128)(2,1)} %bitcast.3), calls=%async_computation.1 | async-start | bytes 2097152 | tf_op jit(solution)/shard_map/all_to_all | solution.py:320
  75.4 9.9 %collective-permute-start.6 = (bf16[1024,256]{1,0:T(8,128)(2,1)S(1)}, bf16[1024,256]{1,0:T(8,128)(2,1)S(1)}, u32[]{:S(2)}, u32[]{:S(2)}) collective-permute-start(bf16[1024,256]{1,0:T(8,128)(2,1)S(1)} %copy-done), channel_id=1, source_target_pairs={{0,32},{32,0},{1,33},{33,1},{2,34},{34,2},{3,35},{35,3},{4,36},{36... | collective-permute-start | bytes 1572872 | tf_op jit(solution)/shard_map/ppermute | solution.py:305
  75.5 12.9 %collective-permute-start = (bf16[8,8,8,256]{3,2,1,0:T(8,128)(2,1)S(1)}, bf16[8,8,8,256]{3,2,1,0:T(8,128)(2,1)S(1)}, u32[]{:S(2)}, u32[]{:S(2)}) collective-permute-start(bf16[8,8,8,256]{3,2,1,0:T(8,128)(2,1)S(1)} %bitcast.26), channel_id=1, source_target_pairs={{0,24},{8,0},{16,8},{24,16},{1,25},{9,1},{17,9},{25,17},{2,26},{10... | collective-permute-start | bytes 786440 | tf_op jit(solution)/shard_map/ppermute | solution.py:305
  75.8 29.6 %collective-permute-start.7 = (bf16[1024,256]{1,0:T(8,128)(2,1)S(1)}, bf16[1024,256]{1,0:T(8,128)(2,1)}, u32[]{:S(2)}, u32[]{:S(2)}) collective-permute-start(bf16[1024,256]{1,0:T(8,128)(2,1)S(1)} %collective-permute-done.3.refs_5_), channel_id=1, source_target_pairs={{0,32},{32,0},{1,33},{33,1},{2,34},{34,2},{3,35},{35,3},{4,36},{36... | collective-permute-start | bytes 1572872 | tf_op jit(solution)/shard_map/ppermute | solution.py:305
  84.8 20.7 %collective-permute-start.8 = (bf16[1024,256]{1,0:T(8,128)(2,1)S(1)}, bf16[1024,256]{1,0:T(8,128)(2,1)}, u32[]{:S(2)}, u32[]{:S(2)}) collective-permute-start(bf16[1024,256]{1,0:T(8,128)(2,1)S(1)} %collective-permute-done.4.refs_6_), channel_id=1, source_target_pairs={{0,32},{32,0},{1,33},{33,1},{2,34},{34,2},{3,35},{35,3},{4,36},{36... | collective-permute-start | bytes 1572872 | tf_op jit(solution)/shard_map/ppermute | solution.py:305
  84.8 20.7 %collective-permute-start.9 = (bf16[1024,256]{1,0:T(8,128)(2,1)}, bf16[1024,256]{1,0:T(8,128)(2,1)}, u32[]{:S(2)}, u32[]{:S(2)}) collective-permute-start(bf16[1024,256]{1,0:T(8,128)(2,1)} %collective-permute-done.5.refs_7_), channel_id=1, source_target_pairs={{0,32},{32,0},{1,33},{33,1},{2,34},{34,2},{3,35},{35,3},{4,36},{36... | collective-permute-start | bytes 1572872 | tf_op jit(solution)/shard_map/ppermute | solution.py:305
  85.3 0.8 copy-start.2
  86.1 15.0 %collective-permute-start.1 = (bf16[8,8,8,256]{3,2,1,0:T(8,128)(2,1)S(1)}, bf16[8,8,8,256]{3,2,1,0:T(8,128)(2,1)}, u32[]{:S(2)}, u32[]{:S(2)}) collective-permute-start(bf16[8,8,8,256]{3,2,1,0:T(8,128)(2,1)S(1)} %bitcast.27), channel_id=1, source_target_pairs={{0,16},{8,24},{16,0},{24,8},{1,17},{9,25},{17,1},{25,9},{2,18},{10... | collective-permute-start | bytes 786440 | tf_op jit(solution)/shard_map/ppermute | solution.py:305
  88.4 17.0 %collective-permute-start.2 = (bf16[8,8,8,256]{3,2,1,0:T(8,128)(2,1)S(1)}, bf16[8,8,8,256]{3,2,1,0:T(8,128)(2,1)}, u32[]{:S(2)}, u32[]{:S(2)}) collective-permute-start(bf16[8,8,8,256]{3,2,1,0:T(8,128)(2,1)S(1)} %bitcast.28), channel_id=1, source_target_pairs={{0,8},{8,16},{16,24},{24,0},{1,9},{9,17},{17,25},{25,1},{2,10},{10... | collective-permute-start | bytes 786440 | tf_op jit(solution)/shard_map/ppermute | solution.py:305
  105.5 1.0 copy-start.3
  113.3 16.4 %collective-permute-start.10 = (f32[8,8,8,256]{3,2,1,0:T(8,128)S(1)}, f32[8,8,8,256]{3,2,1,0:T(8,128)S(1)}, u32[]{:S(2)}, u32[]{:S(2)}) collective-permute-start(f32[8,8,8,256]{3,2,1,0:T(8,128)S(1)} %get-tuple-element.21), channel_id=1, source_target_pairs={{0,16},{8,24},{16,0},{24,8},{1,17},{9,25},{17,1},{25,9},{2,18},{10... | collective-permute-start | bytes 1572872 | tf_op jit(solution)/shard_map/ppermute | solution.py:305
  114.9 25.1 %collective-permute-start.11 = (f32[8,8,8,256]{3,2,1,0:T(8,128)S(1)}, f32[8,8,8,256]{3,2,1,0:T(8,128)S(1)}, u32[]{:S(2)}, u32[]{:S(2)}) collective-permute-start(f32[8,8,8,256]{3,2,1,0:T(8,128)S(1)} %get-tuple-element.22), channel_id=1, source_target_pairs={{0,8},{8,16},{16,24},{24,0},{1,9},{9,17},{17,25},{25,1},{2,10},{10... | collective-permute-start | bytes 1572872 | tf_op jit(solution)/shard_map/ppermute | solution.py:305
  116.9 23.1 %collective-permute-start.12 = (f32[8,8,8,256]{3,2,1,0:T(8,128)S(1)}, f32[8,8,8,256]{3,2,1,0:T(8,128)S(1)}, u32[]{:S(2)}, u32[]{:S(2)}) collective-permute-start(f32[8,8,8,256]{3,2,1,0:T(8,128)S(1)} %get-tuple-element.23), channel_id=1, source_target_pairs={{0,24},{8,0},{16,8},{24,16},{1,25},{9,1},{17,9},{25,17},{2,26},{10... | collective-permute-start | bytes 1572872 | tf_op jit(solution)/shard_map/ppermute | solution.py:305
  140.9 8.9 %copy-start.8 = (s32[256,128]{1,0:T(8,128)S(1)}, s32[256,128]{1,0:T(8,128)}, u32[]{:S(2)}) copy-start(s32[256,128]{1,0:T(8,128)} %copy-done.7) | copy-start | bytes 393220
  140.9 39.8 %all-to-all-start.4 = ((f32[64,8,256]{2,1,0:T(8,128)}), f32[64,8,256]{2,1,0:T(8,128)S(1)}, u32[]{:S(2)}, u32[]{:S(2)}) async-start(f32[64,8,256]{2,1,0:T(8,128)} %bitcast.18), calls=%async_computation.4 | async-start | bytes 1048576 | tf_op jit(solution)/shard_map/all_to_all | solution.py:320
  154.6 14.4 %collective-permute-start.13 = (f32[32,64]{1,0:T(8,128)S(1)}, f32[32,64]{1,0:T(8,128)S(1)}, u32[]{:S(2)}, u32[]{:S(2)}) collective-permute-start(f32[32,64]{1,0:T(8,128)S(1)} %get-tuple-element.24), channel_id=1, source_target_pairs={{0,32},{32,0},{1,33},{33,1},{2,34},{34,2},{3,35},{35,3},{4,36},{36... | collective-permute-start | bytes 24584 | tf_op jit(solution)/shard_map/ppermute | solution.py:305
  168.9 11.8 %collective-permute-start.14 = (f32[32,64]{1,0:T(8,128)S(1)}, f32[32,64]{1,0:T(8,128)S(1)}, u32[]{:S(2)}, u32[]{:S(2)}) collective-permute-start(f32[32,64]{1,0:T(8,128)S(1)} %add.104.refs_0_), channel_id=1, source_target_pairs={{0,64},{64,128},{128,192},{192,0},{1,65},{65,129},{129,193},{193,1... | collective-permute-start | bytes 24584 | tf_op jit(solution)/shard_map/ppermute | solution.py:305
  170.7 10.1 %collective-permute-start.15 = (f32[32,64]{1,0:T(8,128)S(1)}, f32[32,64]{1,0:T(8,128)S(1)}, u32[]{:S(2)}, u32[]{:S(2)}) collective-permute-start(f32[32,64]{1,0:T(8,128)S(1)} %add.104.refs_0_), channel_id=1, source_target_pairs={{0,128},{64,192},{128,0},{192,64},{1,129},{65,193},{129,1},{193,65... | collective-permute-start | bytes 24584 | tf_op jit(solution)/shard_map/ppermute | solution.py:305
  173.3 7.4 %collective-permute-start.16 = (f32[32,64]{1,0:T(8,128)S(1)}, f32[32,64]{1,0:T(8,128)S(1)}, u32[]{:S(2)}, u32[]{:S(2)}) collective-permute-start(f32[32,64]{1,0:T(8,128)S(1)} %add.104.refs_0_), channel_id=1, source_target_pairs={{0,192},{64,0},{128,64},{192,128},{1,193},{65,1},{129,65},{193,129... | collective-permute-start | bytes 24584 | tf_op jit(solution)/shard_map/ppermute | solution.py:305
  174.8 0.7 copy-start.6

commit v5 on v4

--- a/solution.py
+++ b/solution.py
@@ -356,7 +356,8 @@
         in_specs=[SMEM] + [VMEM] * 4 + [pl.BlockSpec(memory_space=pl.ANY)] * N_DIM,
     )(blocks, *users, *tables)
     far = shift(times[2], "x", 2)
-    times = [times[0], far] + [shift(times[i], "x", i) for i in (1, 3)]
+    one = shift(times[1], "x", 1)
+    times = [times[0], far, shift(times[3], "x", 3)]
     inverse = call(
         inverse_kernel, shape((BLOCK, BLOCK), F32), 1, 4 << 30, 8 << 20
     )(diag.reshape(BLOCK, BLOCK))
@@ -370,7 +371,8 @@
     )(pos, came, user_rows)
     pred = pred + shift(pred, "core", 1)
     pred = [pred] + [shift(pred, "y", i) for i in range(1, 4)]
-    times = (times[0] + times[1]) + (times[2] + times[3])
+    early = (times[0] + times[1]) + times[2]
+    times = lax.optimization_barrier(early) + one
     times = exchange(times.reshape(8 * N_DIM, group, BLOCK), ("z",) + DIM)
     inner = call(
         inner_kernel,

time: 187 us -> 188 us (level)
  transfers between devices with their start and end apart: 21 -> 21, of which waited for: 8 -> 9; matrix products, arithmetic and copies ran while one was open for 1% -> 1% of each run, Pallas kernels for 18% -> 18%
where the time goes in v5:
time: 188 us; the launch traced here: 184 us
  waiting for transfers between devices  64.3 us (34%)
  starting transfers between devices  47.2 us (25%)
  Pallas kernels  41.6 us (22%)
  blocking collectives  24.8 us (13%)
  local copies, waits for them, and re-layouts  3.31 us (2%)
    ppermute x17, waiting for transfers between devices, shift(): return lax.ppermute(x, axis, [(i, (i + by) % size) for i in range(size)])  46.1 us
    all_to_all x4, starting transfers between devices, exchange(): return lax.all_to_all(x, axes, 0, 0, tiled=True)  28 us
    all_to_all x1, blocking collectives, exchange(): return lax.all_to_all(x, axes, 0, 0, tiled=True)  24.8 us
    ppermute x17, starting transfers between devices, shift(): return lax.ppermute(x, axis, [(i, (i + by) % size) for i in range(size)])  19.2 us
    all_to_all x4, waiting for transfers between devices, exchange(): return lax.all_to_all(x, axes, 0, 0, tiled=True)  18.2 us
    pallas_call x1, Pallas kernels, body(): call(inverse_kernel, shape((BLOCK, BLOCK), F32), 1, 4 << 30, 8 << 20)  14 us
    pallas_call x1, Pallas kernels, body(): call(product_kernel, [shape((8, N_DIM, group, BLOCK), F32)] * 4, 5 + len(...  6.79 us
    pallas_call x1, Pallas kernels, body(): call(inner_kernel, shape((LIST, LIST, USERS_DEV), F32), 3, 3 << 30, 16 <<...  5.26 us
  transfers between devices with their start and end apart: 21, of which 9 were waited for; matrix products, arithmetic and copies ran while one was open for 1% of the time, Pallas kernels for 18%

profile of v5, /device:TPU:2, one launch (start us, length us, event | category | flops | bytes accessed | tf_op | source)
XLA Modules:
  0.0 184.0 jit_solution(13115647647248387287)
XLA Ops:
  0.0 1.6 convolution_bitcast_fusion.diag_ref
  1.6 5.1 %shard_map.55 = (s32[256,128]{1,0:T(8,128)S(1)}, f32[32,8,384]{2,1,0:T(8,128)S(1)}) custom-call(s32[32,64]{1,0:T(8,128)S(1)} %bitcast.32, s32[256,128]{1,0:T(8,128)S(1)} %bitcast.31, f32[32,8,256]{2,1,0:T(8,128)S(1)} %convolution_bitcast_fusion.diag_ref), custom_call_target="tpu_custom_call" | custom-call | flops 1073741824 | bytes 4194304 | tf_op jit(solution)/shard_map/pallas_call | solution.py:331
  6.7 0.0 copy-start.1
  6.7 24.8 %all_to_all.25.came_ref = f32[32,8,384]{2,1,0:T(8,128)S(1)} all-to-all(f32[32,8,384]{2,1,0:T(8,128)S(1)} %get-tuple-element.16), channel_id=1, replica_groups=mesh['y'=4,'core'=2,'x'=4,'z'=8] {'x','z'}, dimensions={0} | all-to-all | bytes 786432 | tf_op jit(solution)/shard_map/all_to_all | solution.py:320
  31.5 0.7 broadcast_in_dim.8
  32.3 7.7 %all-to-all-start.3 = ((bf16[64,8,256]{2,1,0:T(8,128)(2,1)}), bf16[64,8,256]{2,1,0:T(8,128)(2,1)S(1)}, u32[]{:S(2)}, u32[]{:S(2)}) async-start(bf16[64,8,256]{2,1,0:T(8,128)(2,1)} %bitcast.16), calls=%async_computation.3 | async-start | bytes 524288 | tf_op jit(solution)/shard_map/all_to_all | solution.py:320
  39.9 2.5 %shard_map.56 = (bf16[2048,256]{1,0:T(8,128)(2,1)}, f32[32,8,256]{2,1,0:T(8,128)}) custom-call(f32[32,8,384]{2,1,0:T(8,128)S(1)} %all_to_all.25.came_ref, bf16[1024,256]{1,0:T(8,128)(2,1)S(1)} %copy-done), custom_call_target="tpu_custom_call" | custom-call | flops 1073741824 | bytes 4194304 | tf_op jit(solution)/shard_map/pallas_call | solution.py:337
  42.4 10.4 %all-to-all-done.3 = bf16[64,8,256]{2,1,0:T(8,128)(2,1)S(1)} async-done(((bf16[64,8,256]{2,1,0:T(8,128)(2,1)}), bf16[64,8,256]{2,1,0:T(8,128)(2,1)S(1)}, u32[]{:S(2)}, u32[]{:S(2)}) %all-to-all-start.3) | async-done | bytes 262176 | tf_op jit(solution)/shard_map/all_to_all | solution.py:320
  52.8 5.7 %all-to-all-start.2 = ((f32[32,8,256]{2,1,0:T(8,128)}), f32[32,8,256]{2,1,0:T(8,128)S(1)}, u32[]{:S(2)}, u32[]{:S(2)}) async-start(f32[32,8,256]{2,1,0:T(8,128)} %get-tuple-element.19), calls=%async_computation.2 | async-start | bytes 524288 | tf_op jit(solution)/shard_map/all_to_all | solution.py:320
  58.6 1.2 collective-permute-start.3
  59.8 0.9 collective-permute-start.4
  60.7 1.3 collective-permute-start.5
  62.0 7.8 %all-to-all-done.2 = f32[32,8,256]{2,1,0:T(8,128)S(1)} async-done(((f32[32,8,256]{2,1,0:T(8,128)}), f32[32,8,256]{2,1,0:T(8,128)S(1)}, u32[]{:S(2)}, u32[]{:S(2)}) %all-to-all-start.2) | async-done | bytes 262176 | tf_op jit(solution)/shard_map/all_to_all | solution.py:320
  69.8 5.6 %all-to-all-start.1 = ((bf16[32,64,256]{2,1,0:T(8,128)(2,1)}), bf16[32,64,256]{2,1,0:T(8,128)(2,1)S(1)}, u32[]{:S(2)}, u32[]{:S(2)}) async-start(bf16[32,64,256]{2,1,0:T(8,128)(2,1)} %bitcast.3), calls=%async_computation.1 | async-start | bytes 2097152 | tf_op jit(solution)/shard_map/all_to_all | solution.py:320
  75.4 0.1 collective-permute-start.6
  75.5 0.3 collective-permute-start
  75.8 0.0 collective-permute-done.3.refs_5_
  75.8 0.2 collective-permute-start.7
  76.0 8.7 %collective-permute-done.4.refs_6_ = bf16[1024,256]{1,0:T(8,128)(2,1)S(1)} collective-permute-done((bf16[1024,256]{1,0:T(8,128)(2,1)S(1)}, bf16[1024,256]{1,0:T(8,128)(2,1)S(1)}, u32[]{:S(2)}, u32[]{:S(2)}) %collective-permute-start.4) | collective-permute-done | bytes 524320 | tf_op jit(solution)/shard_map/ppermute | solution.py:305
  84.8 0.0 collective-permute-start.8
  84.8 0.5 collective-permute-start.9
  85.3 0.8 copy-done.2
  86.1 2.1 %collective-permute-start.1 = (bf16[8,8,8,256]{3,2,1,0:T(8,128)(2,1)S(1)}, bf16[8,8,8,256]{3,2,1,0:T(8,128)(2,1)}, u32[]{:S(2)}, u32[]{:S(2)}) collective-permute-start(bf16[8,8,8,256]{3,2,1,0:T(8,128)(2,1)S(1)} %bitcast.27), channel_id=1, source_target_pairs={{0,16},{8,24},{16,0},{24,8},{1,17},{9,25},{17,1},{25,9},{2,18},{10... | collective-permute-start | bytes 786440 | tf_op jit(solution)/shard_map/ppermute | solution.py:305
  88.2 0.2 collective-permute-done.refs_1_
  88.4 2.8 %collective-permute-start.2 = (bf16[8,8,8,256]{3,2,1,0:T(8,128)(2,1)S(1)}, bf16[8,8,8,256]{3,2,1,0:T(8,128)(2,1)}, u32[]{:S(2)}, u32[]{:S(2)}) collective-permute-start(bf16[8,8,8,256]{3,2,1,0:T(8,128)(2,1)S(1)} %bitcast.28), channel_id=1, source_target_pairs={{0,8},{8,16},{16,24},{24,0},{1,9},{9,17},{17,25},{25,1},{2,10},{10... | collective-permute-start | bytes 786440 | tf_op jit(solution)/shard_map/ppermute | solution.py:305
  91.2 0.1 stack.35.block_ref
  91.3 9.8 %collective-permute-done.1.refs_2_ = bf16[8,8,8,256]{3,2,1,0:T(8,128)(2,1)} collective-permute-done((bf16[8,8,8,256]{3,2,1,0:T(8,128)(2,1)S(1)}, bf16[8,8,8,256]{3,2,1,0:T(8,128)(2,1)}, u32[]{:S(2)}, u32[]{:S(2)}) %collective-permute-start.1) | collective-permute-done | bytes 262176 | tf_op jit(solution)/shard_map/ppermute | solution.py:305
  101.0 4.4 %collective-permute-done.2.refs_3_ = bf16[8,8,8,256]{3,2,1,0:T(8,128)(2,1)} collective-permute-done((bf16[8,8,8,256]{3,2,1,0:T(8,128)(2,1)S(1)}, bf16[8,8,8,256]{3,2,1,0:T(8,128)(2,1)}, u32[]{:S(2)}, u32[]{:S(2)}) %collective-permute-start.2) | collective-permute-done | bytes 262176 | tf_op jit(solution)/shard_map/ppermute | solution.py:305
  105.5 1.0 copy-done.3
  106.5 6.8 %shard_map.60 = (f32[8,8,8,256]{3,2,1,0:T(8,128)S(1)}, f32[8,8,8,256]{3,2,1,0:T(8,128)S(1)}, f32[8,8,8,256]{3,2,1,0:T(8,128)S(1)}, f32[8,8,8,256]{3,2,1,0:T(8,128)S(1)}) custom-call(s32[8]{0:T(128)S(1)} %stack.35.block_ref, bf16[8,8,8,256]{3,2,1,0:T(8,128)(2,1)S(1)} %bitcast.29, bf16[8,8,8,256]{3,2,1,0:T(8,128)(2,1)S(1)} %collective-permute-done.refs_1_, ...), custom_call_target="tpu_custom_call" | custom-call | flops 4294967296 | bytes 8388608 | tf_op jit(solution)/shard_map/pallas_call | solution.py:346
  113.3 1.5 collective-permute-start.10
  114.9 2.0 %collective-permute-start.11 = (f32[8,8,8,256]{3,2,1,0:T(8,128)S(1)}, f32[8,8,8,256]{3,2,1,0:T(8,128)S(1)}, u32[]{:S(2)}, u32[]{:S(2)}) collective-permute-start(f32[8,8,8,256]{3,2,1,0:T(8,128)S(1)} %get-tuple-element.22), channel_id=1, source_target_pairs={{0,24},{8,0},{16,8},{24,16},{1,25},{9,1},{17,9},{25,17},{2,26},{10... | collective-permute-start | bytes 1572872 | tf_op jit(solution)/shard_map/ppermute | solution.py:305
  116.9 0.0 collective-permute-start.12
  116.9 12.8 %collective-permute-done.10 = f32[8,8,8,256]{3,2,1,0:T(8,128)S(1)} collective-permute-done((f32[8,8,8,256]{3,2,1,0:T(8,128)S(1)}, f32[8,8,8,256]{3,2,1,0:T(8,128)S(1)}, u32[]{:S(2)}, u32[]{:S(2)}) %collective-permute-start.10) | collective-permute-done | bytes 524320 | tf_op jit(solution)/shard_map/ppermute | solution.py:305
  129.7 9.9 %collective-permute-done.11 = f32[8,8,8,256]{3,2,1,0:T(8,128)S(1)} collective-permute-done((f32[8,8,8,256]{3,2,1,0:T(8,128)S(1)}, f32[8,8,8,256]{3,2,1,0:T(8,128)S(1)}, u32[]{:S(2)}, u32[]{:S(2)}) %collective-permute-start.11) | collective-permute-done | bytes 524320 | tf_op jit(solution)/shard_map/ppermute | solution.py:305
  139.7 0.1 add_add_fusion
  139.8 0.2 collective-permute-done.12
  140.0 0.9 add.103
  140.9 9.0 %all-to-all-start.4 = ((f32[64,8,256]{2,1,0:T(8,128)}), f32[64,8,256]{2,1,0:T(8,128)S(1)}, u32[]{:S(2)}, u32[]{:S(2)}) async-start(f32[64,8,256]{2,1,0:T(8,128)} %bitcast.18), calls=%async_computation.4 | async-start | bytes 1048576 | tf_op jit(solution)/shard_map/all_to_all | solution.py:320
  149.9 4.7 %shard_map.57 = (bf16[2048,256]{1,0:T(8,128)(2,1)S(1)}, f32[32,64]{1,0:T(8,128)S(1)}) custom-call(s32[256,128]{1,0:T(8,128)S(1)} %copy-done.8, bf16[2048,256]{1,0:T(8,128)(2,1)S(1)} %bitcast.23, bf16[64,256]{1,0:T(8,128)(2,1)S(1)} %copy-done.1), custom_call_target="tpu_custom_call" | custom-call | flops 3221225472 | bytes 8388608 | tf_op jit(solution)/shard_map/pallas_call | solution.py:365
  154.6 0.4 collective-permute-start.13
  155.0 14.0 %shard_map.58.inverse_ref = f32[256,256]{1,0:T(8,128)S(1)} custom-call(f32[256,256]{1,0:T(8,128)S(1)} %bitcast.25), custom_call_target="tpu_custom_call" | custom-call | flops 4294967296 | bytes 8388608 | tf_op jit(solution)/shard_map/pallas_call | solution.py:361
  169.0 1.7 collective-permute-start.14
  170.7 2.7 %collective-permute-start.15 = (f32[32,64]{1,0:T(8,128)S(1)}, f32[32,64]{1,0:T(8,128)S(1)}, u32[]{:S(2)}, u32[]{:S(2)}) collective-permute-start(f32[32,64]{1,0:T(8,128)S(1)} %add.104.refs_0_), channel_id=1, source_target_pairs={{0,128},{64,192},{128,0},{192,64},{1,129},{65,193},{129,1},{193,65... | collective-permute-start | bytes 24584 | tf_op jit(solution)/shard_map/ppermute | solution.py:305
  173.4 1.5 collective-permute-start.16
  174.8 0.7 copy-done.6
  175.5 5.3 %shard_map.59.inner_ref = f32[32,32,64]{2,1,0:T(8,128)S(1)} custom-call(bf16[2048,256]{1,0:T(8,128)(2,1)S(1)} %get-tuple-element.18.fetched_ref, f32[256,256]{1,0:T(8,128)S(1)} %shard_map.58.inverse_ref, s32[1,64]{1,0:T(1,128)S(1)} %bitcast.33), custom_call_target="tpu_custom_call" | custom-call | flops 3221225472 | bytes 16777216 | tf_op jit(solution)/shard_map/pallas_call | solution.py:377
  180.8 3.2 %shard_map.61 = f32[64,256]{1,0:T(8,128)} custom-call(bf16[2048,256]{1,0:T(8,128)(2,1)S(1)} %get-tuple-element.18.fetched_ref, f32[256,256]{1,0:T(8,128)S(1)} %shard_map.58.inverse_ref, f32[32,32,64]{2,1,0:T(8,128)S(1)} %shard_map.59.inner_ref, s32[1,64]{1,0:T(1,128)S(1)} %bitcast.34, bf16[64,256]{1,0:T(8,128)(2,1)S(1)} %copy-done.1, ...), custom_call_target="tpu_custom_call" | custom-call | flops 1073741824 | bytes 4194304 | tf_op jit(solution)/shard_map/pallas_call | solution.py:389
  (26 shorter events, 0.1 us)
Async XLA Ops:
  0.0 1.6 copy-start.5
  0.0 1.6 copy-start.4
  6.7 24.8 %copy-start.7 = (s32[256,128]{1,0:T(8,128)}, s32[256,128]{1,0:T(8,128)S(1)}, u32[]{:S(2)}) copy-start(s32[256,128]{1,0:T(8,128)S(1)} %get-tuple-element.15.pos_ref) | copy-start | bytes 393220
  6.7 24.8 %copy-start.1 = (bf16[64,256]{1,0:T(8,128)(2,1)S(1)}, bf16[64,256]{1,0:T(8,128)(2,1)}, u32[]{:S(2)}) copy-start(bf16[64,256]{1,0:T(8,128)(2,1)} %users_ref.3) | copy-start | bytes 98308
  31.5 8.4 %copy-start = (bf16[1024,256]{1,0:T(8,128)(2,1)S(1)}, bf16[1024,256]{1,0:T(8,128)(2,1)}, u32[]{:S(2)}) copy-start(bf16[1024,256]{1,0:T(8,128)(2,1)} %refs_4_.1) | copy-start | bytes 1572868
  32.3 20.6 %all-to-all-start.3 = ((bf16[64,8,256]{2,1,0:T(8,128)(2,1)}), bf16[64,8,256]{2,1,0:T(8,128)(2,1)S(1)}, u32[]{:S(2)}, u32[]{:S(2)}) async-start(bf16[64,8,256]{2,1,0:T(8,128)(2,1)} %bitcast.16), calls=%async_computation.3 | async-start | bytes 524288 | tf_op jit(solution)/shard_map/all_to_all | solution.py:320
  52.8 17.0 %all-to-all-start.2 = ((f32[32,8,256]{2,1,0:T(8,128)}), f32[32,8,256]{2,1,0:T(8,128)S(1)}, u32[]{:S(2)}, u32[]{:S(2)}) async-start(f32[32,8,256]{2,1,0:T(8,128)} %get-tuple-element.19), calls=%async_computation.2 | async-start | bytes 524288 | tf_op jit(solution)/shard_map/all_to_all | solution.py:320
  58.6 17.3 %collective-permute-start.3 = (bf16[1024,256]{1,0:T(8,128)(2,1)S(1)}, bf16[1024,256]{1,0:T(8,128)(2,1)S(1)}, u32[]{:S(2)}, u32[]{:S(2)}) collective-permute-start(bf16[1024,256]{1,0:T(8,128)(2,1)S(1)} %copy-done), channel_id=1, source_target_pairs={{0,192},{64,0},{128,64},{192,128},{1,193},{65,1},{129,65},{193,129... | collective-permute-start | bytes 1572872 | tf_op jit(solution)/shard_map/ppermute | solution.py:305
  59.8 25.0 %collective-permute-start.4 = (bf16[1024,256]{1,0:T(8,128)(2,1)S(1)}, bf16[1024,256]{1,0:T(8,128)(2,1)S(1)}, u32[]{:S(2)}, u32[]{:S(2)}) collective-permute-start(bf16[1024,256]{1,0:T(8,128)(2,1)S(1)} %copy-done), channel_id=1, source_target_pairs={{0,64},{64,128},{128,192},{192,0},{1,65},{65,129},{129,193},{193,1... | collective-permute-start | bytes 1572872 | tf_op jit(solution)/shard_map/ppermute | solution.py:305
  60.7 24.1 %collective-permute-start.5 = (bf16[1024,256]{1,0:T(8,128)(2,1)S(1)}, bf16[1024,256]{1,0:T(8,128)(2,1)}, u32[]{:S(2)}, u32[]{:S(2)}) collective-permute-start(bf16[1024,256]{1,0:T(8,128)(2,1)S(1)} %copy-done), channel_id=1, source_target_pairs={{0,128},{64,192},{128,0},{192,64},{1,129},{65,193},{129,1},{193,65... | collective-permute-start | bytes 1572872 | tf_op jit(solution)/shard_map/ppermute | solution.py:305
  69.8 71.0 %all-to-all-start.1 = ((bf16[32,64,256]{2,1,0:T(8,128)(2,1)}), bf16[32,64,256]{2,1,0:T(8,128)(2,1)S(1)}, u32[]{:S(2)}, u32[]{:S(2)}) async-start(bf16[32,64,256]{2,1,0:T(8,128)(2,1)} %bitcast.3), calls=%async_computation.1 | async-start | bytes 2097152 | tf_op jit(solution)/shard_map/all_to_all | solution.py:320
  75.4 9.9 %collective-permute-start.6 = (bf16[1024,256]{1,0:T(8,128)(2,1)S(1)}, bf16[1024,256]{1,0:T(8,128)(2,1)S(1)}, u32[]{:S(2)}, u32[]{:S(2)}) collective-permute-start(bf16[1024,256]{1,0:T(8,128)(2,1)S(1)} %copy-done), channel_id=1, source_target_pairs={{0,32},{32,0},{1,33},{33,1},{2,34},{34,2},{3,35},{35,3},{4,36},{36... | collective-permute-start | bytes 1572872 | tf_op jit(solution)/shard_map/ppermute | solution.py:305
  75.5 12.9 %collective-permute-start = (bf16[8,8,8,256]{3,2,1,0:T(8,128)(2,1)S(1)}, bf16[8,8,8,256]{3,2,1,0:T(8,128)(2,1)S(1)}, u32[]{:S(2)}, u32[]{:S(2)}) collective-permute-start(bf16[8,8,8,256]{3,2,1,0:T(8,128)(2,1)S(1)} %bitcast.26), channel_id=1, source_target_pairs={{0,24},{8,0},{16,8},{24,16},{1,25},{9,1},{17,9},{25,17},{2,26},{10... | collective-permute-start | bytes 786440 | tf_op jit(solution)/shard_map/ppermute | solution.py:305
  75.8 29.6 %collective-permute-start.7 = (bf16[1024,256]{1,0:T(8,128)(2,1)S(1)}, bf16[1024,256]{1,0:T(8,128)(2,1)}, u32[]{:S(2)}, u32[]{:S(2)}) collective-permute-start(bf16[1024,256]{1,0:T(8,128)(2,1)S(1)} %collective-permute-done.3.refs_5_), channel_id=1, source_target_pairs={{0,32},{32,0},{1,33},{33,1},{2,34},{34,2},{3,35},{35,3},{4,36},{36... | collective-permute-start | bytes 1572872 | tf_op jit(solution)/shard_map/ppermute | solution.py:305
  84.8 20.7 %collective-permute-start.8 = (bf16[1024,256]{1,0:T(8,128)(2,1)S(1)}, bf16[1024,256]{1,0:T(8,128)(2,1)}, u32[]{:S(2)}, u32[]{:S(2)}) collective-permute-start(bf16[1024,256]{1,0:T(8,128)(2,1)S(1)} %collective-permute-done.4.refs_6_), channel_id=1, source_target_pairs={{0,32},{32,0},{1,33},{33,1},{2,34},{34,2},{3,35},{35,3},{4,36},{36... | collective-permute-start | bytes 1572872 | tf_op jit(solution)/shard_map/ppermute | solution.py:305
  84.8 20.7 %collective-permute-start.9 = (bf16[1024,256]{1,0:T(8,128)(2,1)}, bf16[1024,256]{1,0:T(8,128)(2,1)}, u32[]{:S(2)}, u32[]{:S(2)}) collective-permute-start(bf16[1024,256]{1,0:T(8,128)(2,1)} %collective-permute-done.5.refs_7_), channel_id=1, source_target_pairs={{0,32},{32,0},{1,33},{33,1},{2,34},{34,2},{3,35},{35,3},{4,36},{36... | collective-permute-start | bytes 1572872 | tf_op jit(solution)/shard_map/ppermute | solution.py:305
  85.3 0.8 copy-start.2
  86.1 15.0 %collective-permute-start.1 = (bf16[8,8,8,256]{3,2,1,0:T(8,128)(2,1)S(1)}, bf16[8,8,8,256]{3,2,1,0:T(8,128)(2,1)}, u32[]{:S(2)}, u32[]{:S(2)}) collective-permute-start(bf16[8,8,8,256]{3,2,1,0:T(8,128)(2,1)S(1)} %bitcast.27), channel_id=1, source_target_pairs={{0,16},{8,24},{16,0},{24,8},{1,17},{9,25},{17,1},{25,9},{2,18},{10... | collective-permute-start | bytes 786440 | tf_op jit(solution)/shard_map/ppermute | solution.py:305
  88.4 17.0 %collective-permute-start.2 = (bf16[8,8,8,256]{3,2,1,0:T(8,128)(2,1)S(1)}, bf16[8,8,8,256]{3,2,1,0:T(8,128)(2,1)}, u32[]{:S(2)}, u32[]{:S(2)}) collective-permute-start(bf16[8,8,8,256]{3,2,1,0:T(8,128)(2,1)S(1)} %bitcast.28), channel_id=1, source_target_pairs={{0,8},{8,16},{16,24},{24,0},{1,9},{9,17},{17,25},{25,1},{2,10},{10... | collective-permute-start | bytes 786440 | tf_op jit(solution)/shard_map/ppermute | solution.py:305
  105.5 1.0 copy-start.3
  113.3 16.4 %collective-permute-start.10 = (f32[8,8,8,256]{3,2,1,0:T(8,128)S(1)}, f32[8,8,8,256]{3,2,1,0:T(8,128)S(1)}, u32[]{:S(2)}, u32[]{:S(2)}) collective-permute-start(f32[8,8,8,256]{3,2,1,0:T(8,128)S(1)} %get-tuple-element.21), channel_id=1, source_target_pairs={{0,16},{8,24},{16,0},{24,8},{1,17},{9,25},{17,1},{25,9},{2,18},{10... | collective-permute-start | bytes 1572872 | tf_op jit(solution)/shard_map/ppermute | solution.py:305
  114.9 24.8 %collective-permute-start.11 = (f32[8,8,8,256]{3,2,1,0:T(8,128)S(1)}, f32[8,8,8,256]{3,2,1,0:T(8,128)S(1)}, u32[]{:S(2)}, u32[]{:S(2)}) collective-permute-start(f32[8,8,8,256]{3,2,1,0:T(8,128)S(1)} %get-tuple-element.22), channel_id=1, source_target_pairs={{0,24},{8,0},{16,8},{24,16},{1,25},{9,1},{17,9},{25,17},{2,26},{10... | collective-permute-start | bytes 1572872 | tf_op jit(solution)/shard_map/ppermute | solution.py:305
  116.9 23.1 %collective-permute-start.12 = (f32[8,8,8,256]{3,2,1,0:T(8,128)S(1)}, f32[8,8,8,256]{3,2,1,0:T(8,128)S(1)}, u32[]{:S(2)}, u32[]{:S(2)}) collective-permute-start(f32[8,8,8,256]{3,2,1,0:T(8,128)S(1)} %get-tuple-element.23), channel_id=1, source_target_pairs={{0,8},{8,16},{16,24},{24,0},{1,9},{9,17},{17,25},{25,1},{2,10},{10... | collective-permute-start | bytes 1572872 | tf_op jit(solution)/shard_map/ppermute | solution.py:305
  140.9 9.0 %copy-start.8 = (s32[256,128]{1,0:T(8,128)S(1)}, s32[256,128]{1,0:T(8,128)}, u32[]{:S(2)}) copy-start(s32[256,128]{1,0:T(8,128)} %copy-done.7) | copy-start | bytes 393220
  140.9 39.9 %all-to-all-start.4 = ((f32[64,8,256]{2,1,0:T(8,128)}), f32[64,8,256]{2,1,0:T(8,128)S(1)}, u32[]{:S(2)}, u32[]{:S(2)}) async-start(f32[64,8,256]{2,1,0:T(8,128)} %bitcast.18), calls=%async_computation.4 | async-start | bytes 1048576 | tf_op jit(solution)/shard_map/all_to_all | solution.py:320
  154.6 14.4 %collective-permute-start.13 = (f32[32,64]{1,0:T(8,128)S(1)}, f32[32,64]{1,0:T(8,128)S(1)}, u32[]{:S(2)}, u32[]{:S(2)}) collective-permute-start(f32[32,64]{1,0:T(8,128)S(1)} %get-tuple-element.24), channel_id=1, source_target_pairs={{0,32},{32,0},{1,33},{33,1},{2,34},{34,2},{3,35},{35,3},{4,36},{36... | collective-permute-start | bytes 24584 | tf_op jit(solution)/shard_map/ppermute | solution.py:305
  169.0 11.8 %collective-permute-start.14 = (f32[32,64]{1,0:T(8,128)S(1)}, f32[32,64]{1,0:T(8,128)S(1)}, u32[]{:S(2)}, u32[]{:S(2)}) collective-permute-start(f32[32,64]{1,0:T(8,128)S(1)} %add.104.refs_0_), channel_id=1, source_target_pairs={{0,64},{64,128},{128,192},{192,0},{1,65},{65,129},{129,193},{193,1... | collective-permute-start | bytes 24584 | tf_op jit(solution)/shard_map/ppermute | solution.py:305
  170.7 10.1 %collective-permute-start.15 = (f32[32,64]{1,0:T(8,128)S(1)}, f32[32,64]{1,0:T(8,128)S(1)}, u32[]{:S(2)}, u32[]{:S(2)}) collective-permute-start(f32[32,64]{1,0:T(8,128)S(1)} %add.104.refs_0_), channel_id=1, source_target_pairs={{0,128},{64,192},{128,0},{192,64},{1,129},{65,193},{129,1},{193,65... | collective-permute-start | bytes 24584 | tf_op jit(solution)/shard_map/ppermute | solution.py:305
  173.4 7.4 %collective-permute-start.16 = (f32[32,64]{1,0:T(8,128)S(1)}, f32[32,64]{1,0:T(8,128)S(1)}, u32[]{:S(2)}, u32[]{:S(2)}) collective-permute-start(f32[32,64]{1,0:T(8,128)S(1)} %add.104.refs_0_), channel_id=1, source_target_pairs={{0,192},{64,0},{128,64},{192,128},{1,193},{65,1},{129,65},{193,129... | collective-permute-start | bytes 24584 | tf_op jit(solution)/shard_map/ppermute | solution.py:305
  174.8 0.7 copy-start.6
